TPU v7x, 32 devices: a whole 2x2x4 slice. The times are simulated.
32 devices in a mesh: frames: 8 (over y, x, core), chan: 4 (over z).
Axes of the slice: x: 2, y: 2, z: 4, core: 2. Of those that a mesh axis runs over, the one named last changes fastest.
Arguments:
- inputs: bfloat16 [16, 256, 16, 128], P('frames', 'chan'), may hold values from -6 to 6
- saved: bfloat16 [16, 256, 16, 128], P('frames', 'chan'), may hold values from -6 to 6
- cotangent: bfloat16 [8, 256, 512], P('frames', 'chan'), may hold values from -24 to 24
- spatial_w: bfloat16 [3, 3, 256, 256], P(None, None, 'chan'), may hold values from -0.125 to 0.125
- temporal_w: bfloat16 [3, 256, 256], replicated, may hold values from -0.21875 to 0.21875
Outputs:
- input_grad: bfloat16 [16, 256, 16, 128], P('frames', 'chan')
- spatial_grad: float32 [3, 3, 256, 256], P(None, None, 'chan')
- temporal_grad: float32 [3, 256, 256], P(None, 'chan')
All inputs are finite; a program needn't handle non-finite values.
Results may differ from a plain program's by a relative error of at most 0.0049.
Values may be sent and summed in bfloat16 or wider, within the bound.
No kernel may reach another device: no remote copies, remote signals or barrier semaphores. Data moves between devices by JAX's collectives and lax.ppermute only.
A program may use at most 64 MiB of HBM per device.

v0:
```python
import math

import jax
import jax.numpy as jnp
from jax import lax
from jax.sharding import PartitionSpec as P


def temporal_terms(saved_ext, grad_ext, temporal_w, row_total, frame_count):
    result = jnp.zeros((frame_count, row_total, grad_ext.shape[2]), jnp.float32)
    for tap in range(3):
        result = result + jnp.einsum(
            "fol,io->fil",
            grad_ext[2 - tap : 2 - tap + frame_count],
            temporal_w[tap],
            preferred_element_type=jnp.float32,
        )
    partial_value = jnp.stack(
        [
            jnp.einsum(
                "fil,fol->io",
                saved_ext[tap : tap + frame_count],
                grad_ext[1 : frame_count + 1],
                preferred_element_type=jnp.float32,
            )
            for tap in range(3)
        ]
    )
    return (result.astype(jnp.bfloat16), partial_value)


def shards(inputs, saved, cotangent, spatial_w, temporal_w):
    frame_count, quarter, row_count, col_count = inputs.shape
    channels = temporal_w.shape[1]
    row_half, col_half = (row_count // 2, col_count // 2)
    scale = 1.0 / math.sqrt(frame_count * lax.axis_size("frames") * row_count * col_count)
    full_cot = lax.all_gather(cotangent, "chan", axis=1, tiled=True)
    row_first, row_total = (0, channels)
    frame_pad = ((1, 1), (0, 0), (0, 0))
    pooled_saved = saved.reshape(frame_count, quarter, row_half, 2, col_half, 2).transpose(
        0, 1, 3, 5, 2, 4
    )
    pooled_saved = pooled_saved.reshape(frame_count, quarter, 4, row_half * col_half)
    pooled_cot = full_cot.reshape(1, channels, 1, row_half * col_half)
    moved_saved, moved_cot = (
        lax.all_to_all(pooled_saved, "frames", split_axis=3, concat_axis=0, tiled=True),
        lax.all_to_all(pooled_cot, "frames", split_axis=3, concat_axis=0, tiled=True),
    )
    frame_total, local_cells = (moved_saved.shape[0], moved_saved.shape[3])
    spread = jnp.broadcast_to(moved_cot[:, None], (frame_total // 2, 2, channels, 4, local_cells))
    upsampled = (
        spread.reshape(frame_total, channels, 4 * local_cells).astype(jnp.float32) * 0.125
    ).astype(jnp.bfloat16)
    grad_ext = jnp.pad(upsampled, frame_pad)
    saved_ext = jnp.pad(moved_saved.reshape(frame_total, quarter, 4 * local_cells), frame_pad)
    cell_grad, temporal_part = temporal_terms(
        saved_ext, grad_ext, temporal_w, row_total, frame_total
    )
    cell_grad = cell_grad.reshape(frame_total, row_total, 4, local_cells)
    back_grad = lax.all_to_all(cell_grad, "frames", split_axis=0, concat_axis=3, tiled=True)
    back_grad = back_grad.reshape(frame_count, row_total, 2, 2, row_half, col_half).transpose(
        0, 1, 4, 2, 5, 3
    )
    saved_grad = back_grad.reshape(frame_count, row_total, row_count, col_count)
    temporal_total = lax.psum(temporal_part, "frames")
    space_pad = ((0, 0), (0, 0), (1, 1), (1, 1))
    grad_pad = jnp.pad(saved_grad, space_pad)
    input_pad = jnp.pad(inputs, space_pad)
    input_sum = jnp.zeros((frame_count, quarter, row_count, col_count), jnp.float32)
    kernel_rows = []
    for tap_row in range(3):
        kernel_cols = []
        for tap_col in range(3):
            window = grad_pad[
                :, :, 2 - tap_row : 2 - tap_row + row_count, 2 - tap_col : 2 - tap_col + col_count
            ]
            input_sum = input_sum + jnp.einsum(
                "fohw,io->fihw",
                window,
                spatial_w[tap_row, tap_col],
                preferred_element_type=jnp.float32,
            )
            shifted = input_pad[:, :, tap_row : tap_row + row_count, tap_col : tap_col + col_count]
            kernel_cols.append(
                jnp.einsum("fihw,fohw->io", shifted, saved_grad, preferred_element_type=jnp.float32)
            )
        kernel_rows.append(jnp.stack(kernel_cols))
    spatial_part = jnp.stack(kernel_rows)
    spatial_total = lax.psum(spatial_part, "frames")
    return (input_sum.astype(jnp.bfloat16), spatial_total * scale, temporal_total * scale)


def solution(mesh):
    return jax.shard_map(
        shards,
        mesh=mesh,
        in_specs=(
            P("frames", "chan", None, None),
            P("frames", "chan", None, None),
            P("frames", "chan", None),
            P(None, None, "chan", None),
            P(),
        ),
        out_specs=(
            P("frames", "chan", None, None),
            P(None, None, "chan", None),
            P(None, "chan", None),
        ),
        check_vma=False,
    )
```

profile of v0, /device:TPU:0, one launch (start us, length us, event | category | flops | bytes accessed | tf_op | source)
XLA Modules:
  0.0 170.7 jit_solution(4398962847321769897)
XLA Ops:
  7.2 16.0 %all_gather.3 = bf16[1,256,512]{2,1,0:T(8,128)(2,1)S(1)} all-gather(bf16[1,64,512]{2,1,0:T(8,128)(2,1)} %param.7), channel_id=1, replica_groups=mesh['frames'=8,'chan'=4] {'chan'}, dimensions={1}, use_global_device_ids=true | all-gather | bytes 327680 | tf_op jit(solution)/shard_map/all_gather | solution.py:37
  23.6 0.5 broadcast.35
  24.1 2.2 %reduce = bf16[512,256]{1,0:T(8,128)(2,1)S(1)} reduce(bf16[512,1,1,256]{3,2,1,0:T(2,128)(2,1)S(1)} %bitcast.212, bf16[]{:T(256)} %broadcast.35), dimensions={1,2}, to_apply=%bitcast.179.reduce_sub_computation | reduce | bytes 524290
  26.3 0.8 reshape.84
  27.1 3.7 %all-to-all-start = ((bf16[8,2,8192]{2,1,0:T(2,128)(2,1)}), bf16[8,2,8192]{2,1,0:T(2,128)(2,1)S(1)}, u32[]{:S(2)}, u32[]{:S(2)}) async-start(bf16[8,2,8192]{2,1,0:T(2,128)(2,1)} %reshape.84), calls=%async_computation | async-start | bytes 524288 | tf_op jit(solution)/shard_map/all_to_all | solution.py:47
  30.8 0.6 copy.77
  31.4 0.7 copy.108
  32.1 1.5 reshape.86
  33.6 4.1 %all-to-all-done = bf16[8,2,8192]{2,1,0:T(2,128)(2,1)S(1)} async-done(((bf16[8,2,8192]{2,1,0:T(2,128)(2,1)}), bf16[8,2,8192]{2,1,0:T(2,128)(2,1)S(1)}, u32[]{:S(2)}, u32[]{:S(2)}) %all-to-all-start) | async-done | bytes 262176 | tf_op jit(solution)/shard_map/all_to_all | solution.py:47
  37.7 3.5 %all-to-all-start.2 = ((bf16[8,2,16384]{2,1,0:T(2,128)(2,1)}), bf16[8,2,16384]{2,1,0:T(2,128)(2,1)S(1)}, u32[]{:S(2)}, u32[]{:S(2)}) async-start(bf16[8,2,16384]{2,1,0:T(2,128)(2,1)} %reshape.86), calls=%async_computation.2 | async-start | bytes 1048576 | tf_op jit(solution)/shard_map/all_to_all | solution.py:46
  41.8 0.7 copy-done.2
  42.5 0.7 fusion.20
  43.3 0.7 fusion.22
  44.0 2.1 %add_convert_fusion = bf16[16,256,256]{2,1,0:T(8,128)(2,1)} fusion(f32[16,256,256]{2,1,0:T(8,128)S(1)} %fusion.22, f32[16,256,256]{2,1,0:T(8,128)S(1)} %fusion.20, bf16[16,256,256]{1,2,0:T(8,128)(2,1)S(1)} %bitcast.202, bf16[3,256,256]{2,1,0:T(8,128)(2,1)S(1)} %copy-done.2), kind=kOutput, calls=%fused_computation.8 | convolution fusion | flops 506462208 | bytes 12713984 | tf_op jit(solution)/shard_map/fol,io->fil/dot_general | solution.py:12
  46.1 4.8 %all-to-all-done.2 = bf16[8,2,16384]{2,1,0:T(2,128)(2,1)S(1)} async-done(((bf16[8,2,16384]{2,1,0:T(2,128)(2,1)}), bf16[8,2,16384]{2,1,0:T(2,128)(2,1)S(1)}, u32[]{:S(2)}, u32[]{:S(2)}) %all-to-all-start.2) | async-done | bytes 524320 | tf_op jit(solution)/shard_map/all_to_all | solution.py:46
  50.9 4.4 %all-to-all-start.1 = ((bf16[16,256,4,64]{1,3,2,0:T(8,128)(2,1)}), bf16[16,256,4,64]{1,3,2,0:T(8,128)(2,1)}, u32[]{:S(2)}, u32[]{:S(2)}) async-start(bf16[16,256,4,64]{1,3,2,0:T(8,128)(2,1)} %bitcast.205), calls=%async_computation.1 | async-start | bytes 4194304 | tf_op jit(solution)/shard_map/all_to_all | solution.py:60
  55.5 1.2 copy.66
  56.7 1.7 reshape.87
  58.3 2.4 %copy.81 = bf16[2,64,4,8,64]{4,1,2,0,3:T(8,128)(2,1)} copy(bf16[2,64,4,8,64]{1,2,0,4,3:T(4,128)(2,1)} %bitcast.209) | data formatting | bytes 1048576 | tf_op jit(solution)/shard_map/all_to_all | solution.py:46
  60.7 3.1 %copy.82 = bf16[8,2,64,4,64]{4,3,2,1,0:T(4,128)(2,1)} copy(bf16[8,2,64,4,64]{4,2,3,1,0:T(8,128)(2,1)} %bitcast.207) | data formatting | bytes 1048576 | tf_op jit(solution)/shard_map/all_to_all | solution.py:46
  63.9 2.1 %reshape.55 = bf16[16,64,256]{2,1,0:T(8,128)(2,1)S(1)} reshape(bf16[8,2,64,4,64]{4,3,2,1,0:T(4,128)(2,1)} %copy.82) | data formatting | bytes 1048576 | tf_op jit(solution)/shard_map/reshape | solution.py:55
  65.9 1.7 %convolution_bitcast_fusion = f32[1,64,256]{2,1,0:T(8,128)S(1)} fusion(bf16[8,256,64]{1,2,0:T(8,128)(2,1)S(1)} %bitcast.214, bf16[2,64,4,8,64]{4,1,2,0,3:T(8,128)(2,1)} %copy.81), kind=kOutput, calls=%fused_computation.35 | convolution fusion | flops 134217728 | bytes 851968 | tf_op jit(solution)/shard_map/fil,fol->io/dot_general | solution.py:20
  68.7 0.7 pad_maximum_fusion.1
  69.4 12.5 %all-to-all-done.1 = bf16[16,256,4,64]{1,3,2,0:T(8,128)(2,1)} async-done(((bf16[16,256,4,64]{1,3,2,0:T(8,128)(2,1)}), bf16[16,256,4,64]{1,3,2,0:T(8,128)(2,1)}, u32[]{:S(2)}, u32[]{:S(2)}) %all-to-all-start.1) | async-done | bytes 2097184 | tf_op jit(solution)/shard_map/all_to_all | solution.py:60
  81.9 5.1 %copy.63 = bf16[2,256,8,2,64,2]{1,0,5,4,3,2:T(2,128)(2,1)} copy(bf16[2,256,8,2,64,2]{1,4,5,3,0,2:T(8,128)(2,1)} %bitcast.17) | data formatting | bytes 4194304 | tf_op jit(solution)/shard_map/transpose | solution.py:61
  87.0 5.1 %copy.64 = bf16[2,256,16,128]{3,1,2,0:T(8,128)(2,1)S(1)} copy(bf16[2,256,16,128]{1,0,3,2:T(2,128)(2,1)} %bitcast.206) | data formatting | bytes 4194304 | tf_op jit(solution)/shard_map/reshape | solution.py:64
  92.0 0.8 convolution_bitcast_fusion.10
  92.8 0.8 convolution_bitcast_fusion.11
  93.6 0.8 convolution_bitcast_fusion.6
  94.3 0.8 convolution_bitcast_fusion.8
  95.1 0.8 convolution_bitcast_fusion.9
  95.9 0.8 convolution_bitcast_fusion.7
  96.6 0.8 convolution_bitcast_fusion.3
  97.4 0.8 convolution_bitcast_fusion.4
  98.2 0.8 convolution_bitcast_fusion.5
  98.9 0.7 fusion
  99.7 0.5 fusion.31
  100.6 0.8 fusion.14
  101.4 0.9 fusion.13
  102.2 0.8 fusion.11
  103.0 0.8 fusion.10
  103.9 0.9 pad_maximum_fusion
  104.8 0.5 fusion.9
  105.3 0.8 fusion.17
  106.1 1.1 copy.85
  107.2 53.1 %all-reduce.7.cloned.1.call-done = (f32[3,3,64,256]{3,2,1,0:T(8,128)}, f32[3,64,256]{2,1,0:T(8,128)}) async-done(((f32[3,3,64,256]{3,2,1,0:T(8,128)}, f32[3,64,256]{2,1,0:T(8,128)}), (f32[3,3,64,256]{3,2,1,0:T(8,128)}, f32[3,64,256]{2,1,0:T(8,128)})) %all-reduce.7.cloned.1.call-update) | async-done | bytes 786448 | tf_op jit(solution)/shard_map/psum | solution.py:89
  160.3 1.9 %broadcast_multiply_fusion = f32[3,3,64,256]{3,2,1,0:T(8,128)} fusion(f32[3,3,64,256]{3,2,1,0:T(8,128)} %get-tuple-element.15), kind=kLoop, calls=%fused_computation.50 | loop fusion | flops 147456 | bytes 1179648 | tf_op jit(solution)/shard_map/mul | solution.py:90
  162.3 1.6 broadcast_multiply_fusion.1
  (18 shorter events, 2.7 us)
Async XLA Ops:
  7.2 23.7 %copy-start.1 = (bf16[2,64,16,128]{3,2,1,0:T(8,128)(2,1)S(1)}, bf16[2,64,16,128]{3,2,1,0:T(8,128)(2,1)}, u32[]{:S(2)}) copy-start(bf16[2,64,16,128]{3,2,1,0:T(8,128)(2,1)} %param.6) | copy-start | bytes 1572868
  27.1 10.6 %all-to-all-start = ((bf16[8,2,8192]{2,1,0:T(2,128)(2,1)}), bf16[8,2,8192]{2,1,0:T(2,128)(2,1)S(1)}, u32[]{:S(2)}, u32[]{:S(2)}) async-start(bf16[8,2,8192]{2,1,0:T(2,128)(2,1)} %reshape.84), calls=%async_computation | async-start | bytes 524288 | tf_op jit(solution)/shard_map/all_to_all | solution.py:47
  37.7 13.2 %all-to-all-start.2 = ((bf16[8,2,16384]{2,1,0:T(2,128)(2,1)}), bf16[8,2,16384]{2,1,0:T(2,128)(2,1)S(1)}, u32[]{:S(2)}, u32[]{:S(2)}) async-start(bf16[8,2,16384]{2,1,0:T(2,128)(2,1)} %reshape.86), calls=%async_computation.2 | async-start | bytes 1048576 | tf_op jit(solution)/shard_map/all_to_all | solution.py:46
  41.5 1.0 copy-start.2
  50.9 31.0 %all-to-all-start.1 = ((bf16[16,256,4,64]{1,3,2,0:T(8,128)(2,1)}), bf16[16,256,4,64]{1,3,2,0:T(8,128)(2,1)}, u32[]{:S(2)}, u32[]{:S(2)}) async-start(bf16[16,256,4,64]{1,3,2,0:T(8,128)(2,1)} %bitcast.205), calls=%async_computation.1 | async-start | bytes 4194304 | tf_op jit(solution)/shard_map/all_to_all | solution.py:60
  55.2 105.1 %all-reduce.7.cloned.1.call-start = ((), (), s32[]{:S(2)}) async-start(), calls=%async_computation.3 | async-start | bytes 1572864 | tf_op jit(solution)/shard_map/psum | solution.py:89
  94.3 1.5 copy-start
  97.4 1.5 copy-start.3
Sparse Core Ops, SparseCore 0:
  104.9 55.3 all-reduce.6
where the time goes:
time: 172 us; the launch traced here: 171 us
  waiting for transfers between devices  74.6 us (43%)
  local copies, waits for them, and re-layouts  27.5 us (16%)
  matrix products  19.2 us (11%)
  blocking collectives  16 us (9%)
  between operations  14.3 us (8%)
  starting transfers between devices  11.8 us (7%)
  other arithmetic  7.4 us (4%)
    psum x1, waiting for transfers between devices, shards(): spatial_total = lax.psum(spatial_part, 'frames')  53.1 us
    all_gather x1, blocking collectives, shards(): full_cot = lax.all_gather(cotangent, 'chan', axis=1, tiled=True)  16 us
    all_to_all x1, waiting for transfers between devices, shards(): lax.all_to_all(cell_grad, 'frames', split_axis=0, concat_axis=3, tiled=True)  12.5 us
    unnamed x16, local copies, waits for them, and re-layouts  8.32 us
    dot_general x9, matrix products, shards(): jnp.einsum('fihw,fohw->io', shifted, saved_grad, preferred_element_type=j...  6.84 us
    dot_general x9, matrix products, shards(): jnp.einsum('fohw,io->fihw', window, spatial_w[tap_row, tap_col], preferre...  6.16 us
    all_to_all x2, local copies, waits for them, and re-layouts, shards(): lax.all_to_all(pooled_saved, 'frames', split_axis=3, concat_axis=0, tiled...  5.53 us
    transpose x1, local copies, waits for them, and re-layouts, shards(): back_grad.reshape(frame_count, row_total, 2, 2, row_half, col_half)  5.08 us
  transfers between devices with their start and end apart: 4, of which 4 were waited for; matrix products, arithmetic and copies ran while one was open for 14% of the time, Pallas kernels for 0%

commit v1 on v0

v1 whole, which is shorter than its diff:
```python
import functools
import math

import jax
import jax.numpy as jnp
from jax import lax
from jax.experimental import pallas as pl
from jax.experimental.pallas import tpu as pltpu
from jax.sharding import PartitionSpec as P

F32, BF16 = jnp.float32, jnp.bfloat16
LANES = 128


def one_hot_pool(slots, shifts, cols):
    half = LANES // 2
    shape = (slots * cols, len(shifts) * LANES)
    row = lax.broadcasted_iota(jnp.int32, shape, 0)
    col = lax.broadcasted_iota(jnp.int32, shape, 1)
    slot, w = row // cols, row % cols
    which, lane = col // LANES, col % LANES
    first = 2 * (lane % half) + which + (shifts[0] - 1)
    hit = (slot // 2 == lane // half) & ((w == first) | (w == first + 1))
    return jnp.where(hit, 1.0, 0.0).astype(BF16)


def one_hot_spread(cols):
    half = LANES // 2
    shape = (LANES, 3 * 2 * cols)
    row = lax.broadcasted_iota(jnp.int32, shape, 0)
    col = lax.broadcasted_iota(jnp.int32, shape, 1)
    tap, pair, w = col // (2 * cols), (col // cols) % 2, col % cols
    at = w - tap + 1
    hit = (at >= 0) & (at < cols) & (row == pair * half + at // 2)
    return jnp.where(hit, 1.0, 0.0).astype(BF16)


def prep_kernel(x_ref, y_ref, sw_ref, s_ref, p_ref, wc_ref, rows, left):
    frames, chans, height, cols = x_ref.shape
    steps = height // 4
    zero = jnp.zeros((chans, cols), BF16)
    pool = one_hot_pool(4, (0, 1, 2), cols)

    def place(a, f, h, value):
        t, slot = (h - a + 1) // 4, (h - a + 1) % 4
        if 0 <= t < steps:
            at = (f * steps + t) * chans
            left[a, at : at + chans, slot * cols : (slot + 1) * cols] = value

    rows[...] = y_ref[...].reshape(frames * chans * height, cols).astype(F32)
    for f in range(frames):
        for h in range(height):
            at = f * chans * height + h
            place(1, f, h, rows[pl.ds(at, chans, stride=height), :].astype(BF16))
    done = jnp.dot(left[1], pool[:, LANES : 2 * LANES], preferred_element_type=F32).astype(BF16)
    for f in range(frames):
        for t in range(steps):
            at = (f * steps + t) * chans
            p_ref[f, :, t * LANES : (t + 1) * LANES] = done[at : at + chans]

    rows[...] = x_ref[...].reshape(frames * chans * height, cols).astype(F32)
    for f in range(frames):
        for h in range(-1, height + 1):
            if 0 <= h < height:
                at = f * chans * height + h
                value = rows[pl.ds(at, chans, stride=height), :].astype(BF16)
            else:
                value = zero
            for a in range(3):
                place(a, f, h, value)
    for a in range(3):
        done = jnp.dot(left[a], pool, preferred_element_type=F32).astype(BF16)
        for f in range(frames):
            for t in range(steps):
                at = (f * steps + t) * chans
                for b in range(3):
                    to = (a * 3 + b) * chans
                    s_ref[f, to : to + chans, t * LANES : (t + 1) * LANES] = done[
                        at : at + chans, b * LANES : (b + 1) * LANES
                    ]
    for b in range(3):
        w0, w1, w2 = (sw_ref[a, b].astype(F32) for a in range(3))
        for j, value in enumerate((w0, w0 + w1, w1 + w2, w2)):
            wc_ref[b, j * chans : (j + 1) * chans, :] = value.astype(BF16)


def dot_nt(a, b):
    return lax.dot_general(a, b, (((1,), (1,)), ((), ())), preferred_element_type=F32)


def main_kernel(scale, count, *refs):
    pieces, rest = refs[:count], refs[count:]
    before_ref, after_ref, s_ref, p_ref, tw_ref, g_ref, keep_ref, send_ref, cells, part = rest
    me = lax.axis_index("chan")
    at_frame = lax.axis_index("frames")
    last = lax.axis_size("frames") - 1
    quarter, spots = pieces[0].shape
    channels = count * quarter
    has_before = jnp.where(at_frame > 0, 1.0, 0.0).astype(BF16)
    has_after = jnp.where(at_frame < last, 1.0, 0.0).astype(BF16)
    for k in range(count):
        at = partner(me, k, count)
        cells[0, at] = pieces[k][...]
        cells[1, at] = before_ref[k] * has_before
        cells[2, at] = after_ref[k] * has_after
    now = cells[0].reshape(channels, spots)
    before = cells[1].reshape(channels, spots)
    after = cells[2].reshape(channels, spots)
    w0, w1, w2 = tw_ref[0], tw_ref[1], tw_ref[2]
    dot = functools.partial(jnp.dot, preferred_element_type=F32)
    middle = dot(w1, now)
    g0 = ((dot(w0, now) + middle + dot(w2, before)) * 0.125).astype(BF16)
    g1 = ((dot(w2, now) + middle + dot(w0, after)) * 0.125).astype(BF16)
    g_ref[0] = g0
    g_ref[1] = g1
    both_p = p_ref[...].reshape(2 * quarter, spots)
    e_now, e_before, e_after = (dot_nt(both_p, c) for c in (now, before, after))
    e0, e1 = e_now[:quarter], e_now[quarter:]
    small = scale * 0.125
    taps = s_ref.shape[1] // quarter
    spatial = (dot_nt(s_ref[0], g0) + dot_nt(s_ref[1], g1)) * scale
    part[:taps] = spatial.reshape(taps, quarter, channels)
    part[taps] = (e0 + e_after[quarter:]) * small
    part[taps + 1] = (e0 + e1) * small
    part[taps + 2] = (e_before[:quarter] + e1) * small
    half = part.shape[0] // 2
    side = lax.rem(at_frame, 2)
    keep_ref[...] = part[pl.ds(side * half, half)]
    send_ref[...] = part[pl.ds((1 - side) * half, half)]


def back_kernel(g_ref, wc_ref, out_ref, sums, rows):
    frames, chans, height, cols = out_ref.shape
    spread = one_hot_spread(cols)
    pooled = height // 2
    for f in range(frames):
        for t in range(height // 4):
            wide = jnp.dot(
                g_ref[f, :, t * LANES : (t + 1) * LANES], spread, preferred_element_type=F32
            ).astype(BF16)
            total = jnp.dot(wc_ref[0], wide[:, : 2 * cols], preferred_element_type=F32)
            for b in (1, 2):
                total = total + jnp.dot(
                    wc_ref[b],
                    wide[:, b * 2 * cols : (b + 1) * 2 * cols],
                    preferred_element_type=F32,
                )
            sums[2 * t] = total[:, :cols]
            sums[2 * t + 1] = total[:, cols:]
        for p in range(pooled):
            even = sums[p, chans : 2 * chans, :]
            if p > 0:
                even = even + sums[p - 1, 3 * chans :, :]
            odd = sums[p, 2 * chans : 3 * chans, :]
            if p < pooled - 1:
                odd = odd + sums[p + 1, :chans, :]
            rows[pl.ds(2 * p, chans, stride=height), :] = even
            rows[pl.ds(2 * p + 1, chans, stride=height), :] = odd
        out_ref[f] = rows[...].reshape(chans, height, cols).astype(BF16)


def partner(me, k, count):
    if count & (count - 1) == 0:
        return jnp.bitwise_xor(me, k)
    return lax.rem(me + k, count)


def swap(value, axis, k):
    count = lax.axis_size(axis)
    if count & (count - 1) == 0:
        pairs = [(i, i ^ k) for i in range(count)]
    else:
        pairs = [((i + k) % count, i) for i in range(count)]
    return lax.ppermute(value, axis, pairs)


def vmem(count):
    return [pl.BlockSpec(memory_space=pltpu.VMEM)] * count


def shape(dims, dtype):
    return jax.ShapeDtypeStruct(dims, dtype)


def cost(flops, size):
    return pl.CostEstimate(flops=flops, bytes_accessed=size, transcendentals=0)


def both(a, b):
    return a.astype(F32) + b.astype(F32)


def reduce_frames(keep, send):
    count = lax.axis_size("frames")
    side = lax.rem(lax.axis_index("frames"), 2)
    total = keep + swap(send, "frames", 1)
    bits = [1 << i for i in range(1, count.bit_length() - 1)]
    cut = total.shape[0] // 2
    a, b = total[:cut], total[cut:]
    for first, second in zip(bits, bits[::-1]):
        a, b = a.astype(BF16), b.astype(BF16)
        a, b = both(a, swap(a, "frames", first)), both(b, swap(b, "frames", second))
    mine = jnp.concatenate([a, b])
    other = swap(mine, "frames", 1)
    return jnp.where(side == 0, mine, other), jnp.where(side == 0, other, mine)


def shards(inputs, saved, cotangent, spatial_w, temporal_w):
    frames, quarter, height, cols = inputs.shape
    channels = temporal_w.shape[1]
    spots = cotangent.shape[2]
    count = lax.axis_size("chan")
    ring = lax.axis_size("frames")
    scale = 1.0 / math.sqrt(frames * ring * height * cols)
    steps = height // 4
    taps = spatial_w.shape[0] * spatial_w.shape[1]

    mine = cotangent[0]
    pieces = [mine] + [swap(mine, "chan", k) for k in range(1, count)]
    gathered = jnp.stack(pieces)
    up = [(i, (i + 1) % ring) for i in range(ring)]
    before = lax.ppermute(gathered, "frames", up)
    after = lax.ppermute(gathered, "frames", [(j, i) for i, j in up])

    sums, pooled, combined = pl.pallas_call(
        prep_kernel,
        out_shape=(
            shape((frames, taps * quarter, spots), BF16),
            shape((frames, quarter, spots), BF16),
            shape((3, 4 * quarter, channels), BF16),
        ),
        in_specs=vmem(3),
        out_specs=tuple(vmem(3)),
        scratch_shapes=[
            pltpu.VMEM((frames * quarter * height, cols), F32),
            pltpu.VMEM((3, frames * steps * quarter, 4 * cols), BF16),
        ],
        compiler_params=pltpu.CompilerParams(vmem_limit_bytes=20 << 20),
        cost_estimate=cost(1 << 30, 4 << 20),
        name="prep",
    )(inputs, saved, spatial_w)

    slices = taps + 3
    grad, keep, send = pl.pallas_call(
        functools.partial(main_kernel, scale, count),
        out_shape=(
            shape((frames, channels, spots), BF16),
            shape((slices // 2, quarter, channels), F32),
            shape((slices // 2, quarter, channels), F32),
        ),
        in_specs=vmem(count + 5),
        out_specs=tuple(vmem(3)),
        scratch_shapes=[
            pltpu.VMEM((3, count, quarter, spots), BF16),
            pltpu.VMEM((slices, quarter, channels), F32),
        ],
        compiler_params=pltpu.CompilerParams(vmem_limit_bytes=20 << 20),
        cost_estimate=cost(1 << 30, 4 << 20),
        name="main",
    )(*pieces, before, after, sums, pooled, temporal_w)

    input_grad = pl.pallas_call(
        back_kernel,
        out_shape=shape(inputs.shape, BF16),
        in_specs=vmem(2),
        out_specs=vmem(1)[0],
        scratch_shapes=[
            pltpu.VMEM((height // 2, 4 * quarter, cols), F32),
            pltpu.VMEM((quarter * height, cols), F32),
        ],
        compiler_params=pltpu.CompilerParams(vmem_limit_bytes=20 << 20),
        cost_estimate=cost(3 << 30, 4 << 20),
        name="back",
    )(grad, combined)

    low, high = reduce_frames(keep, send)
    rest = taps - slices // 2
    spatial = jnp.concatenate([low, high[:rest]])
    return (input_grad, spatial.reshape(spatial_w.shape), high[rest:])


def solution(mesh):
    return jax.shard_map(
        shards,
        mesh=mesh,
        in_specs=(
            P("frames", "chan", None, None),
            P("frames", "chan", None, None),
            P("frames", "chan", None),
            P(None, None, "chan", None),
            P(),
        ),
        out_specs=(
            P("frames", "chan", None, None),
            P(None, None, "chan", None),
            P(None, "chan", None),
        ),
        check_vma=False,
    )
```

time: 172 us -> 42.5 us (0.25)
  waiting for transfers between devices: 74.6 us -> 15.5 us
  local copies, waits for them, and re-layouts: 27.5 us -> 3.77 us
  matrix products: 19.2 us -> 0 us
  blocking collectives: 16 us -> 0 us
  between operations: 14.3 us -> 0.76 us
  Pallas kernels: 0 us -> 6.4 us
  other arithmetic: 7.4 us -> 2.04 us
  starting transfers between devices: 11.8 us -> 13.8 us
    psum x1 -> x0, waiting for transfers between devices: 53.1 us -> none  [shards(): spatial_total = lax.psum(spatial_part, 'frames')]
    all_to_all x3 -> x0, waiting for transfers between devices: 21.4 us -> none  [the longest x1 12.5 us: shards(): lax.all_to_all(cell_grad, 'frames', split_axis=0, concat_axis=3, tiled=True)]
    dot_general x24 -> x0, matrix products: 19.2 us -> none  [the longest x9 6.84 us: shards(): jnp.einsum('fihw,fohw->io', shifted, saved_grad, preferred_element_type=j...]
    all_gather x1 -> x0, blocking collectives: 16 us -> none  [shards(): full_cot = lax.all_gather(cotangent, 'chan', axis=1, tiled=True)]
    ppermute x0 -> x11, waiting for transfers between devices: none -> 15.5 us  [the longest x9 15.5 us: swap(): return lax.ppermute(value, axis, pairs)]
    ppermute x0 -> x11, starting transfers between devices: none -> 13.8 us  [the longest x9 11.1 us: swap(): return lax.ppermute(value, axis, pairs)]
    all_to_all x3 -> x0, starting transfers between devices: 11.6 us -> none  [the longest x1 4.36 us: shards(): lax.all_to_all(cell_grad, 'frames', split_axis=0, concat_axis=3, tiled=True)]
    reshape x4 -> x0, local copies, waits for them, and re-layouts: 8.3 us -> none  [the longest x1 5.07 us: shards(): saved_grad = back_grad.reshape(frame_count, row_total, row_count, col_count)]
  transfers between devices with their start and end apart: 4 -> 11, of which waited for: 4 -> 7; matrix products, arithmetic and copies ran while one was open for 14% -> 0% of each run, Pallas kernels for 0% -> 12%
where the time goes in v1:
time: 42.5 us; the launch traced here: 42.3 us
  waiting for transfers between devices  15.5 us (36%)
  starting transfers between devices  13.8 us (32%)
  Pallas kernels  6.4 us (15%)
  local copies, waits for them, and re-layouts  3.77 us (9%)
  other arithmetic  2.04 us (5%)
  between operations  0.76 us (2%)
    ppermute x9, waiting for transfers between devices, swap(): return lax.ppermute(value, axis, pairs)  15.5 us
    ppermute x9, starting transfers between devices, swap(): return lax.ppermute(value, axis, pairs)  11.1 us
    pallas_call x1, Pallas kernels, shards(): pl.pallas_call(back_kernel, out_shape=shape(inputs.shape, BF16), in_specs...  3.12 us
    unnamed x10, local copies, waits for them, and re-layouts  3.05 us
    ppermute x1, starting transfers between devices, shards(): after = lax.ppermute(gathered, 'frames', [(j, i) for i, j in up])  2.63 us
    pallas_call x1, Pallas kernels, shards(): pl.pallas_call(prep_kernel, out_shape=(shape((frames, taps * quarter, spo...  2.03 us
    pallas_call x1, Pallas kernels, shards(): pl.pallas_call(functools.partial(main_kernel, scale, count), out_shape=(s...  1.25 us
    another operation x1, other arithmetic, shards(): gathered = jnp.stack(pieces)  0.92 us
  transfers between devices with their start and end apart: 11, of which 7 were waited for; matrix products, arithmetic and copies ran while one was open for 0% of the time, Pallas kernels for 12%

profile of v1, /device:TPU:0, one launch (start us, length us, event | category | flops | bytes accessed | tf_op | source)
XLA Modules:
  0.0 42.3 jit_solution(10032139157646473520)
XLA Ops:
  0.6 3.1 %collective-permute-start = (bf16[64,512]{1,0:T(8,128)(2,1)}, bf16[64,512]{1,0:T(8,128)(2,1)S(1)}, u32[]{:S(2)}, u32[]{:S(2)}) collective-permute-start(bf16[64,512]{1,0:T(8,128)(2,1)} %bitcast.5), channel_id=1, source_target_pairs={{0,1},{1,0},{2,3},{3,2},{4,5},{5,4},{6,7},{7,6},{8,9},{9,8},{10,11... | collective-permute-start | bytes 196616 | tf_op jit(solution)/shard_map/ppermute | solution.py:174
  3.7 2.6 %collective-permute-start.1 = (bf16[64,512]{1,0:T(8,128)(2,1)}, bf16[64,512]{1,0:T(8,128)(2,1)S(1)}, u32[]{:S(2)}, u32[]{:S(2)}) collective-permute-start(bf16[64,512]{1,0:T(8,128)(2,1)} %bitcast.6), channel_id=1, source_target_pairs={{0,2},{1,3},{2,0},{3,1},{4,6},{5,7},{6,4},{7,5},{8,10},{9,11},{10,... | collective-permute-start | bytes 196616 | tf_op jit(solution)/shard_map/ppermute | solution.py:174
  6.3 0.0 collective-permute-start.2
  6.3 0.0 collective-permute-done.refs_1_
  6.3 4.9 %collective-permute-done.1.refs_2_ = bf16[64,512]{1,0:T(8,128)(2,1)S(1)} collective-permute-done((bf16[64,512]{1,0:T(8,128)(2,1)}, bf16[64,512]{1,0:T(8,128)(2,1)S(1)}, u32[]{:S(2)}, u32[]{:S(2)}) %collective-permute-start.1) | collective-permute-done | bytes 65568 | tf_op jit(solution)/shard_map/ppermute | solution.py:174
  11.2 1.4 %collective-permute-done.2.refs_3_ = bf16[64,512]{1,0:T(8,128)(2,1)S(1)} collective-permute-done((bf16[64,512]{1,0:T(8,128)(2,1)}, bf16[64,512]{1,0:T(8,128)(2,1)S(1)}, u32[]{:S(2)}, u32[]{:S(2)}) %collective-permute-start.2) | collective-permute-done | bytes 65568 | tf_op jit(solution)/shard_map/ppermute | solution.py:174
  12.6 0.0 copy-start.3
  12.6 0.9 %pad_maximum_fusion.2 = bf16[4,64,512]{2,1,0:T(8,128)(2,1)S(1)} fusion(bf16[1,64,512]{2,1,0:T(8,128)(2,1)S(1)} %bitcast.11, bf16[1,64,512]{2,1,0:T(8,128)(2,1)S(1)} %bitcast.10, bf16[1,64,512]{2,1,0:T(8,128)(2,1)S(1)} %bitcast.9, bf16[1,64,512]{2,1,0:T(8,128)(2,1)} %param.7), kind=kLoop, calls=%fused_computation.3 | loop fusion | flops 393216 | bytes 524288 | tf_op jit(solution)/shard_map/stack | solution.py:220
  13.6 0.0 copy-start
  13.6 0.1 collective-permute-start.3
  13.6 2.6 %collective-permute-start.4 = (bf16[4,64,512]{2,1,0:T(8,128)(2,1)S(1)}, bf16[4,64,512]{2,1,0:T(8,128)(2,1)S(1)}, u32[]{:S(2)}, u32[]{:S(2)}) collective-permute-start(bf16[4,64,512]{2,1,0:T(8,128)(2,1)S(1)} %pad_maximum_fusion.2), channel_id=1, source_target_pairs={{4,0},{8,4},{12,8},{16,12},{20,16},{24,20},{28,24},{0,28},{5,1},{9... | collective-permute-start | bytes 786440 | tf_op jit(solution)/shard_map/ppermute | solution.py:223
  16.3 0.0 copy-start.1
  16.3 1.0 %copy-done.1 = bf16[2,64,16,128]{3,2,1,0:T(8,128)(2,1)S(1)} copy-done((bf16[2,64,16,128]{3,2,1,0:T(8,128)(2,1)S(1)}, bf16[2,64,16,128]{3,2,1,0:T(8,128)(2,1)}, u32[]{:S(2)}) %copy-start.1) | copy-done | bytes 524312
  17.3 0.0 copy-start.2
  17.3 1.0 %copy-done.2 = bf16[2,64,16,128]{3,2,1,0:T(8,128)(2,1)S(1)} copy-done((bf16[2,64,16,128]{3,2,1,0:T(8,128)(2,1)S(1)}, bf16[2,64,16,128]{3,2,1,0:T(8,128)(2,1)}, u32[]{:S(2)}) %copy-start.2) | copy-done | bytes 524312
  18.4 0.0 copy-start.4
  18.4 1.0 %copy-done.4 = bf16[3,3,64,256]{3,2,1,0:T(8,128)(2,1)S(1)} copy-done((bf16[3,3,64,256]{3,2,1,0:T(8,128)(2,1)S(1)}, bf16[3,3,64,256]{3,2,1,0:T(8,128)(2,1)}, u32[]{:S(2)}) %copy-start.4) | copy-done | bytes 294936
  19.3 2.0 %prep.1 = (bf16[2,576,512]{2,1,0:T(8,128)(2,1)S(1)}, bf16[2,64,512]{2,1,0:T(8,128)(2,1)S(1)}, bf16[3,256,256]{2,1,0:T(8,128)(2,1)S(1)}) custom-call(bf16[2,64,16,128]{3,2,1,0:T(8,128)(2,1)S(1)} %copy-done.1, bf16[2,64,16,128]{3,2,1,0:T(8,128)(2,1)S(1)} %copy-done.2, bf16[3,3,64,256]{3,2,1,0:T(8,128)(2,1)S(1)} %copy-done.4), custom_call_target="tpu_custom_call" | custom-call | flops 1073741824 | bytes 4194304 | tf_op jit(solution)/shard_map/prep/pallas_call | solution.py:225
  21.4 0.0 collective-permute-done.3.refs_4_
  21.4 0.0 collective-permute-done.4.refs_5_
  21.4 0.0 copy-done.3
  21.4 0.0 copy-done
  21.4 1.2 %main.1 = (bf16[2,256,512]{2,1,0:T(8,128)(2,1)S(1)}, f32[6,64,256]{2,1,0:T(8,128)S(1)}, f32[6,64,256]{2,1,0:T(8,128)S(1)}) custom-call(bf16[64,512]{1,0:T(8,128)(2,1)S(1)} %bitcast.8, bf16[64,512]{1,0:T(8,128)(2,1)S(1)} %collective-permute-done.refs_1_, bf16[64,512]{1,0:T(8,128)(2,1)S(1)} %collective-permute-done.1.refs_2_, ...), custom_call_target="tpu_custom_call" | custom-call | flops 1073741824 | bytes 4194304 | tf_op jit(solution)/shard_map/main/pallas_call | solution.py:244
  22.7 1.7 %collective-permute-start.5 = (f32[6,64,256]{2,1,0:T(8,128)S(1)}, f32[6,64,256]{2,1,0:T(8,128)S(1)}, u32[]{:S(2)}, u32[]{:S(2)}) collective-permute-start(f32[6,64,256]{2,1,0:T(8,128)S(1)} %get-tuple-element.14), channel_id=1, source_target_pairs={{0,4},{4,0},{8,12},{12,8},{16,20},{20,16},{24,28},{28,24},{1,5},{5... | collective-permute-start | bytes 1179656 | tf_op jit(solution)/shard_map/ppermute | solution.py:174
  24.3 1.3 %collective-permute-done.5 = f32[6,64,256]{2,1,0:T(8,128)S(1)} collective-permute-done((f32[6,64,256]{2,1,0:T(8,128)S(1)}, f32[6,64,256]{2,1,0:T(8,128)S(1)}, u32[]{:S(2)}, u32[]{:S(2)}) %collective-permute-start.5) | collective-permute-done | bytes 393248 | tf_op jit(solution)/shard_map/ppermute | solution.py:174
  25.7 0.1 add_convert_fusion
  25.8 1.6 %collective-permute-start.6 = (bf16[3,64,256]{2,1,0:T(8,128)(2,1)S(1)}, bf16[3,64,256]{2,1,0:T(8,128)(2,1)S(1)}, u32[]{:S(2)}, u32[]{:S(2)}) collective-permute-start(bf16[3,64,256]{2,1,0:T(8,128)(2,1)S(1)} %get-tuple-element.21), channel_id=1, source_target_pairs={{0,8},{4,12},{8,0},{12,4},{16,24},{20,28},{24,16},{28,20},{1,9},{5... | collective-permute-start | bytes 294920 | tf_op jit(solution)/shard_map/ppermute | solution.py:174
  27.3 0.5 %collective-permute-start.8 = (bf16[3,64,256]{2,1,0:T(8,128)(2,1)S(1)}, bf16[3,64,256]{2,1,0:T(8,128)(2,1)S(1)}, u32[]{:S(2)}, u32[]{:S(2)}) collective-permute-start(bf16[3,64,256]{2,1,0:T(8,128)(2,1)S(1)} %get-tuple-element.22), channel_id=1, source_target_pairs={{0,16},{4,20},{8,24},{12,28},{16,0},{20,4},{24,8},{28,12},{1,17},{... | collective-permute-start | bytes 294920 | tf_op jit(solution)/shard_map/ppermute | solution.py:174
  27.8 3.1 %collective-permute-done.6 = bf16[3,64,256]{2,1,0:T(8,128)(2,1)S(1)} collective-permute-done((bf16[3,64,256]{2,1,0:T(8,128)(2,1)S(1)}, bf16[3,64,256]{2,1,0:T(8,128)(2,1)S(1)}, u32[]{:S(2)}, u32[]{:S(2)}) %collective-permute-start.6) | collective-permute-done | bytes 98336 | tf_op jit(solution)/shard_map/ppermute | solution.py:174
  30.9 1.2 %collective-permute-done.8 = bf16[3,64,256]{2,1,0:T(8,128)(2,1)S(1)} collective-permute-done((bf16[3,64,256]{2,1,0:T(8,128)(2,1)S(1)}, bf16[3,64,256]{2,1,0:T(8,128)(2,1)S(1)}, u32[]{:S(2)}, u32[]{:S(2)}) %collective-permute-start.8) | collective-permute-done | bytes 98336 | tf_op jit(solution)/shard_map/ppermute | solution.py:174
  32.1 0.1 add_convert_fusion.2
  32.2 0.6 %collective-permute-start.7 = (bf16[3,64,256]{2,1,0:T(8,128)(2,1)S(1)}, bf16[3,64,256]{2,1,0:T(8,128)(2,1)S(1)}, u32[]{:S(2)}, u32[]{:S(2)}) collective-permute-start(bf16[3,64,256]{2,1,0:T(8,128)(2,1)S(1)} %get-tuple-element.19), channel_id=1, source_target_pairs={{0,16},{4,20},{8,24},{12,28},{16,0},{20,4},{24,8},{28,12},{1,17},{... | collective-permute-start | bytes 294920 | tf_op jit(solution)/shard_map/ppermute | solution.py:174
  32.7 1.0 %collective-permute-start.9 = (bf16[3,64,256]{2,1,0:T(8,128)(2,1)S(1)}, bf16[3,64,256]{2,1,0:T(8,128)(2,1)S(1)}, u32[]{:S(2)}, u32[]{:S(2)}) collective-permute-start(bf16[3,64,256]{2,1,0:T(8,128)(2,1)S(1)} %get-tuple-element.20), channel_id=1, source_target_pairs={{0,8},{4,12},{8,0},{12,4},{16,24},{20,28},{24,16},{28,20},{1,9},{5... | collective-permute-start | bytes 294920 | tf_op jit(solution)/shard_map/ppermute | solution.py:174
  33.8 3.1 %collective-permute-done.7 = bf16[3,64,256]{2,1,0:T(8,128)(2,1)S(1)} collective-permute-done((bf16[3,64,256]{2,1,0:T(8,128)(2,1)S(1)}, bf16[3,64,256]{2,1,0:T(8,128)(2,1)S(1)}, u32[]{:S(2)}, u32[]{:S(2)}) %collective-permute-start.7) | collective-permute-done | bytes 98336 | tf_op jit(solution)/shard_map/ppermute | solution.py:174
  36.9 0.5 %collective-permute-done.9 = bf16[3,64,256]{2,1,0:T(8,128)(2,1)S(1)} collective-permute-done((bf16[3,64,256]{2,1,0:T(8,128)(2,1)S(1)}, bf16[3,64,256]{2,1,0:T(8,128)(2,1)S(1)}, u32[]{:S(2)}, u32[]{:S(2)}) %collective-permute-start.9) | collective-permute-done | bytes 98336 | tf_op jit(solution)/shard_map/ppermute | solution.py:174
  37.4 0.1 collective-permute-start.10
  37.5 3.1 %back.1 = bf16[2,64,16,128]{3,2,1,0:T(8,128)(2,1)} custom-call(bf16[2,256,512]{2,1,0:T(8,128)(2,1)S(1)} %get-tuple-element.11.g_ref, bf16[3,256,256]{2,1,0:T(8,128)(2,1)S(1)} %get-tuple-element.12.wc_ref), custom_call_target="tpu_custom_call" | custom-call | flops 3221225472 | bytes 4194304 | tf_op jit(solution)/shard_map/back/pallas_call | solution.py:262
  40.6 0.0 collective-permute-done.10
  40.6 0.1 broadcast_select_fusion.1
  40.7 0.7 %fusion = (f32[3,64,256]{2,1,0:T(8,128)}, f32[3,64,256]{2,1,0:T(8,128)S(1)}) fusion(f32[6,64,256]{2,1,0:T(8,128)S(1)} %get-tuple-element.16), kind=kLoop, calls=%fused_computation.10 | loop fusion | bytes 786432 | tf_op jit(solution)/shard_map/slice | solution.py:279
  41.4 0.9 %pad_maximum_fusion = f32[9,64,256]{2,1,0:T(8,128)} fusion(f32[3,64,256]{2,1,0:T(8,128)S(1)} %get-tuple-element.18, f32[6,64,256]{2,1,0:T(8,128)S(1)} %get-tuple-element.15), kind=kLoop, calls=%fused_computation | loop fusion | flops 147456 | bytes 1179648 | tf_op jit(solution)/shard_map/concatenate | solution.py:278
  (4 shorter events, 0.1 us)
Async XLA Ops:
  0.6 5.7 %collective-permute-start = (bf16[64,512]{1,0:T(8,128)(2,1)}, bf16[64,512]{1,0:T(8,128)(2,1)S(1)}, u32[]{:S(2)}, u32[]{:S(2)}) collective-permute-start(bf16[64,512]{1,0:T(8,128)(2,1)} %bitcast.5), channel_id=1, source_target_pairs={{0,1},{1,0},{2,3},{3,2},{4,5},{5,4},{6,7},{7,6},{8,9},{9,8},{10,11... | collective-permute-start | bytes 196616 | tf_op jit(solution)/shard_map/ppermute | solution.py:174
  3.7 7.5 %collective-permute-start.1 = (bf16[64,512]{1,0:T(8,128)(2,1)}, bf16[64,512]{1,0:T(8,128)(2,1)S(1)}, u32[]{:S(2)}, u32[]{:S(2)}) collective-permute-start(bf16[64,512]{1,0:T(8,128)(2,1)} %bitcast.6), channel_id=1, source_target_pairs={{0,2},{1,3},{2,0},{3,1},{4,6},{5,7},{6,4},{7,5},{8,10},{9,11},{10,... | collective-permute-start | bytes 196616 | tf_op jit(solution)/shard_map/ppermute | solution.py:174
  6.3 6.3 %collective-permute-start.2 = (bf16[64,512]{1,0:T(8,128)(2,1)}, bf16[64,512]{1,0:T(8,128)(2,1)S(1)}, u32[]{:S(2)}, u32[]{:S(2)}) collective-permute-start(bf16[64,512]{1,0:T(8,128)(2,1)} %bitcast.7), channel_id=1, source_target_pairs={{0,3},{1,2},{2,1},{3,0},{4,7},{5,6},{6,5},{7,4},{8,11},{9,10},{10,... | collective-permute-start | bytes 196616 | tf_op jit(solution)/shard_map/ppermute | solution.py:174
  12.6 8.7 %copy-start.3 = (bf16[3,256,256]{2,1,0:T(8,128)(2,1)S(1)}, bf16[3,256,256]{2,1,0:T(8,128)(2,1)}, u32[]{:S(2)}) copy-start(bf16[3,256,256]{2,1,0:T(8,128)(2,1)} %refs_8_.1) | copy-start | bytes 1179652
  13.6 7.8 %copy-start = (bf16[1,64,512]{2,1,0:T(8,128)(2,1)S(1)}, bf16[1,64,512]{2,1,0:T(8,128)(2,1)}, u32[]{:S(2)}) copy-start(bf16[1,64,512]{2,1,0:T(8,128)(2,1)} %param.7) | copy-start | bytes 196612
  13.6 7.8 %collective-permute-start.3 = (bf16[4,64,512]{2,1,0:T(8,128)(2,1)S(1)}, bf16[4,64,512]{2,1,0:T(8,128)(2,1)S(1)}, u32[]{:S(2)}, u32[]{:S(2)}) collective-permute-start(bf16[4,64,512]{2,1,0:T(8,128)(2,1)S(1)} %pad_maximum_fusion.2), channel_id=1, source_target_pairs={{0,4},{4,8},{8,12},{12,16},{16,20},{20,24},{24,28},{28,0},{1,5},{5... | collective-permute-start | bytes 786440 | tf_op jit(solution)/shard_map/ppermute | solution.py:222
  13.6 7.7 %collective-permute-start.4 = (bf16[4,64,512]{2,1,0:T(8,128)(2,1)S(1)}, bf16[4,64,512]{2,1,0:T(8,128)(2,1)S(1)}, u32[]{:S(2)}, u32[]{:S(2)}) collective-permute-start(bf16[4,64,512]{2,1,0:T(8,128)(2,1)S(1)} %pad_maximum_fusion.2), channel_id=1, source_target_pairs={{4,0},{8,4},{12,8},{16,12},{20,16},{24,20},{28,24},{0,28},{5,1},{9... | collective-permute-start | bytes 786440 | tf_op jit(solution)/shard_map/ppermute | solution.py:223
  16.3 1.0 %copy-start.1 = (bf16[2,64,16,128]{3,2,1,0:T(8,128)(2,1)S(1)}, bf16[2,64,16,128]{3,2,1,0:T(8,128)(2,1)}, u32[]{:S(2)}) copy-start(bf16[2,64,16,128]{3,2,1,0:T(8,128)(2,1)} %x_ref.1) | copy-start | bytes 1572868
  17.3 1.0 %copy-start.2 = (bf16[2,64,16,128]{3,2,1,0:T(8,128)(2,1)S(1)}, bf16[2,64,16,128]{3,2,1,0:T(8,128)(2,1)}, u32[]{:S(2)}) copy-start(bf16[2,64,16,128]{3,2,1,0:T(8,128)(2,1)} %y_ref.1) | copy-start | bytes 1572868
  18.4 1.0 %copy-start.4 = (bf16[3,3,64,256]{3,2,1,0:T(8,128)(2,1)S(1)}, bf16[3,3,64,256]{3,2,1,0:T(8,128)(2,1)}, u32[]{:S(2)}) copy-start(bf16[3,3,64,256]{3,2,1,0:T(8,128)(2,1)} %sw_ref.1) | copy-start | bytes 884740
  22.7 3.0 %collective-permute-start.5 = (f32[6,64,256]{2,1,0:T(8,128)S(1)}, f32[6,64,256]{2,1,0:T(8,128)S(1)}, u32[]{:S(2)}, u32[]{:S(2)}) collective-permute-start(f32[6,64,256]{2,1,0:T(8,128)S(1)} %get-tuple-element.14), channel_id=1, source_target_pairs={{0,4},{4,0},{8,12},{12,8},{16,20},{20,16},{24,28},{28,24},{1,5},{5... | collective-permute-start | bytes 1179656 | tf_op jit(solution)/shard_map/ppermute | solution.py:174
  25.8 5.1 %collective-permute-start.6 = (bf16[3,64,256]{2,1,0:T(8,128)(2,1)S(1)}, bf16[3,64,256]{2,1,0:T(8,128)(2,1)S(1)}, u32[]{:S(2)}, u32[]{:S(2)}) collective-permute-start(bf16[3,64,256]{2,1,0:T(8,128)(2,1)S(1)} %get-tuple-element.21), channel_id=1, source_target_pairs={{0,8},{4,12},{8,0},{12,4},{16,24},{20,28},{24,16},{28,20},{1,9},{5... | collective-permute-start | bytes 294920 | tf_op jit(solution)/shard_map/ppermute | solution.py:174
  27.3 4.8 %collective-permute-start.8 = (bf16[3,64,256]{2,1,0:T(8,128)(2,1)S(1)}, bf16[3,64,256]{2,1,0:T(8,128)(2,1)S(1)}, u32[]{:S(2)}, u32[]{:S(2)}) collective-permute-start(bf16[3,64,256]{2,1,0:T(8,128)(2,1)S(1)} %get-tuple-element.22), channel_id=1, source_target_pairs={{0,16},{4,20},{8,24},{12,28},{16,0},{20,4},{24,8},{28,12},{1,17},{... | collective-permute-start | bytes 294920 | tf_op jit(solution)/shard_map/ppermute | solution.py:174
  32.2 4.7 %collective-permute-start.7 = (bf16[3,64,256]{2,1,0:T(8,128)(2,1)S(1)}, bf16[3,64,256]{2,1,0:T(8,128)(2,1)S(1)}, u32[]{:S(2)}, u32[]{:S(2)}) collective-permute-start(bf16[3,64,256]{2,1,0:T(8,128)(2,1)S(1)} %get-tuple-element.19), channel_id=1, source_target_pairs={{0,16},{4,20},{8,24},{12,28},{16,0},{20,4},{24,8},{28,12},{1,17},{... | collective-permute-start | bytes 294920 | tf_op jit(solution)/shard_map/ppermute | solution.py:174
  32.7 4.6 %collective-permute-start.9 = (bf16[3,64,256]{2,1,0:T(8,128)(2,1)S(1)}, bf16[3,64,256]{2,1,0:T(8,128)(2,1)S(1)}, u32[]{:S(2)}, u32[]{:S(2)}) collective-permute-start(bf16[3,64,256]{2,1,0:T(8,128)(2,1)S(1)} %get-tuple-element.20), channel_id=1, source_target_pairs={{0,8},{4,12},{8,0},{12,4},{16,24},{20,28},{24,16},{28,20},{1,9},{5... | collective-permute-start | bytes 294920 | tf_op jit(solution)/shard_map/ppermute | solution.py:174
  37.4 3.2 %collective-permute-start.10 = (f32[6,64,256]{2,1,0:T(8,128)S(1)}, f32[6,64,256]{2,1,0:T(8,128)S(1)}, u32[]{:S(2)}, u32[]{:S(2)}) collective-permute-start(f32[6,64,256]{2,1,0:T(8,128)S(1)} %pad_maximum_fusion.1), channel_id=1, source_target_pairs={{0,4},{4,0},{8,12},{12,8},{16,20},{20,16},{24,28},{28,24},{1,5},{5... | collective-permute-start | bytes 1179656 | tf_op jit(solution)/shard_map/ppermute | solution.py:174

commit v2 on v1

--- a/solution.py
+++ b/solution.py
@@ -35,7 +35,13 @@
     return jnp.where(hit, 1.0, 0.0).astype(BF16)
 
 
-def prep_kernel(x_ref, y_ref, sw_ref, s_ref, p_ref, wc_ref, rows, left):
+def prep_kernel(x_hbm, y_hbm, sw_hbm, s_ref, p_ref, wc_ref, x_ref, y_ref, sw_ref, sem, rows, left):
+    fetches = [
+        pltpu.make_async_copy(src, dst, sem.at[i])
+        for i, (src, dst) in enumerate(((y_hbm, y_ref), (x_hbm, x_ref), (sw_hbm, sw_ref)))
+    ]
+    for fetch in fetches:
+        fetch.start()
     frames, chans, height, cols = x_ref.shape
     steps = height // 4
     zero = jnp.zeros((chans, cols), BF16)
@@ -47,6 +53,7 @@
             at = (f * steps + t) * chans
             left[a, at : at + chans, slot * cols : (slot + 1) * cols] = value
 
+    fetches[0].wait()
     rows[...] = y_ref[...].reshape(frames * chans * height, cols).astype(F32)
     for f in range(frames):
         for h in range(height):
@@ -58,6 +65,7 @@
             at = (f * steps + t) * chans
             p_ref[f, :, t * LANES : (t + 1) * LANES] = done[at : at + chans]
 
+    fetches[1].wait()
     rows[...] = x_ref[...].reshape(frames * chans * height, cols).astype(F32)
     for f in range(frames):
         for h in range(-1, height + 1):
@@ -78,6 +86,7 @@
                     s_ref[f, to : to + chans, t * LANES : (t + 1) * LANES] = done[
                         at : at + chans, b * LANES : (b + 1) * LANES
                     ]
+    fetches[2].wait()
     for b in range(3):
         w0, w1, w2 = (sw_ref[a, b].astype(F32) for a in range(3))
         for j, value in enumerate((w0, w0 + w1, w1 + w2, w2)):
@@ -90,19 +99,21 @@
 
 def main_kernel(scale, count, *refs):
     pieces, rest = refs[:count], refs[count:]
-    before_ref, after_ref, s_ref, p_ref, tw_ref, g_ref, keep_ref, send_ref, cells, part = rest
+    outer, inner, rest = rest[:2], rest[2:4], rest[4:]
+    s_ref, p_ref, tw_ref, g_ref, keep_ref, send_ref, cells, part = rest
     me = lax.axis_index("chan")
     at_frame = lax.axis_index("frames")
     last = lax.axis_size("frames") - 1
     quarter, spots = pieces[0].shape
     channels = count * quarter
-    has_before = jnp.where(at_frame > 0, 1.0, 0.0).astype(BF16)
-    has_after = jnp.where(at_frame < last, 1.0, 0.0).astype(BF16)
+    side = lax.rem(at_frame, 2)
+    has_outer = jnp.where((at_frame > 0) & (at_frame < last), 1.0, 0.0).astype(BF16)
+    cut = outer[0].shape[0]
     for k in range(count):
         at = partner(me, k, count)
         cells[0, at] = pieces[k][...]
-        cells[1, at] = before_ref[k] * has_before
-        cells[2, at] = after_ref[k] * has_after
+        cells[1 + side, at] = outer[k // cut][k % cut] * has_outer
+        cells[2 - side, at] = inner[k // cut][k % cut]
     now = cells[0].reshape(channels, spots)
     before = cells[1].reshape(channels, spots)
     after = cells[2].reshape(channels, spots)
@@ -124,7 +135,6 @@
     part[taps + 1] = (e0 + e1) * small
     part[taps + 2] = (e_before[:quarter] + e1) * small
     half = part.shape[0] // 2
-    side = lax.rem(at_frame, 2)
     keep_ref[...] = part[pl.ds(side * half, half)]
     send_ref[...] = part[pl.ds((1 - side) * half, half)]
 
@@ -190,7 +200,35 @@
     return a.astype(F32) + b.astype(F32)
 
 
-def reduce_frames(keep, send):
+def prep(inputs, saved, spatial_w):
+    frames, quarter, height, cols = inputs.shape
+    taps = spatial_w.shape[0] * spatial_w.shape[1]
+    channels = spatial_w.shape[3]
+    steps, spots = height // 4, height * cols // 4
+    return pl.pallas_call(
+        prep_kernel,
+        out_shape=(
+            shape((frames, taps * quarter, spots), BF16),
+            shape((frames, quarter, spots), BF16),
+            shape((3, 4 * quarter, channels), BF16),
+        ),
+        in_specs=[pl.BlockSpec(memory_space=pl.ANY)] * 3,
+        out_specs=tuple(vmem(3)),
+        scratch_shapes=[
+            pltpu.VMEM(inputs.shape, BF16),
+            pltpu.VMEM(inputs.shape, BF16),
+            pltpu.VMEM(spatial_w.shape, BF16),
+            pltpu.SemaphoreType.DMA((3,)),
+            pltpu.VMEM((frames * quarter * height, cols), F32),
+            pltpu.VMEM((3, frames * steps * quarter, 4 * cols), BF16),
+        ],
+        compiler_params=pltpu.CompilerParams(vmem_limit_bytes=20 << 20),
+        cost_estimate=cost(1 << 30, 4 << 20),
+        name="prep",
+    )(inputs, saved, spatial_w)
+
+
+def reduce_frames(keep, send, beside):
     count = lax.axis_size("frames")
     side = lax.rem(lax.axis_index("frames"), 2)
     total = keep + swap(send, "frames", 1)
@@ -200,9 +238,10 @@
     for first, second in zip(bits, bits[::-1]):
         a, b = a.astype(BF16), b.astype(BF16)
         a, b = both(a, swap(a, "frames", first)), both(b, swap(b, "frames", second))
+        a, b, beside = lax.optimization_barrier((a, b, beside))
     mine = jnp.concatenate([a, b])
     other = swap(mine, "frames", 1)
-    return jnp.where(side == 0, mine, other), jnp.where(side == 0, other, mine)
+    return jnp.where(side == 0, mine, other), jnp.where(side == 0, other, mine), beside
 
 
 def shards(inputs, saved, cotangent, spatial_w, temporal_w):
@@ -212,33 +251,18 @@
     count = lax.axis_size("chan")
     ring = lax.axis_size("frames")
     scale = 1.0 / math.sqrt(frames * ring * height * cols)
-    steps = height // 4
     taps = spatial_w.shape[0] * spatial_w.shape[1]
 
-    mine = cotangent[0]
-    pieces = [mine] + [swap(mine, "chan", k) for k in range(1, count)]
-    gathered = jnp.stack(pieces)
-    up = [(i, (i + 1) % ring) for i in range(ring)]
-    before = lax.ppermute(gathered, "frames", up)
-    after = lax.ppermute(gathered, "frames", [(j, i) for i, j in up])
-
-    sums, pooled, combined = pl.pallas_call(
-        prep_kernel,
-        out_shape=(
-            shape((frames, taps * quarter, spots), BF16),
-            shape((frames, quarter, spots), BF16),
-            shape((3, 4 * quarter, channels), BF16),
-        ),
-        in_specs=vmem(3),
-        out_specs=tuple(vmem(3)),
-        scratch_shapes=[
-            pltpu.VMEM((frames * quarter * height, cols), F32),
-            pltpu.VMEM((3, frames * steps * quarter, 4 * cols), BF16),
-        ],
-        compiler_params=pltpu.CompilerParams(vmem_limit_bytes=20 << 20),
-        cost_estimate=cost(1 << 30, 4 << 20),
-        name="prep",
-    )(inputs, saved, spatial_w)
+    pieces = [cotangent[0]]
+    pieces += [swap(pieces[0], "chan", k) for k in range(1, count)]
+    cut = count // 2
+    parts = [jnp.stack(pieces[:cut]), jnp.stack(pieces[cut:])]
+    across = [(i, (i + (1 if i % 2 else -1)) % ring) for i in range(ring)]
+    other_chip = lax.ppermute(parts[0], "frames", across)
+    sums, pooled, combined = prep(inputs, saved, spatial_w)
+    parts[1], sums, pooled = lax.optimization_barrier((parts[1], sums, pooled))
+    outer = [other_chip, lax.ppermute(parts[1], "frames", across)]
+    inner = [swap(part, "frames", 1) for part in parts]
 
     slices = taps + 3
     grad, keep, send = pl.pallas_call(
@@ -248,7 +272,7 @@
             shape((slices // 2, quarter, channels), F32),
             shape((slices // 2, quarter, channels), F32),
         ),
-        in_specs=vmem(count + 5),
+        in_specs=vmem(count + 7),
         out_specs=tuple(vmem(3)),
         scratch_shapes=[
             pltpu.VMEM((3, count, quarter, spots), BF16),
@@ -257,7 +281,7 @@
         compiler_params=pltpu.CompilerParams(vmem_limit_bytes=20 << 20),
         cost_estimate=cost(1 << 30, 4 << 20),
         name="main",
-    )(*pieces, before, after, sums, pooled, temporal_w)
+    )(*pieces, *outer, *inner, sums, pooled, temporal_w)
 
     input_grad = pl.pallas_call(
         back_kernel,
@@ -273,7 +297,7 @@
         name="back",
     )(grad, combined)
 
-    low, high = reduce_frames(keep, send)
+    low, high, input_grad = reduce_frames(keep, send, input_grad)
     rest = taps - slices // 2
     spatial = jnp.concatenate([low, high[:rest]])
     return (input_grad, spatial.reshape(spatial_w.shape), high[rest:])

time: 42.5 us -> 39.6 us (0.932)
  waiting for transfers between devices: 15.5 us -> 13.6 us
  other arithmetic: 2.04 us -> 1.09 us
    ppermute x9 -> x11, waiting for transfers between devices: 15.5 us -> 7.47 us  [swap(): return lax.ppermute(value, axis, pairs)]
    ppermute x2, waiting for transfers between devices: 0.01 us -> 6.09 us  [the longest x1 3.29 us: shards(): outer = [other_chip, lax.ppermute(parts[1], 'frames', across)]]
    another operation x2 -> x3, other arithmetic: 0.98 us -> 0.08 us  [the longest x1 0.92 us: shards(): gathered = jnp.stack(pieces)]
    ppermute x9 -> x11, starting transfers between devices: 11.1 us -> 10.9 us  [swap(): return lax.ppermute(value, axis, pairs)]
    unnamed x10 -> x11, local copies, waits for them, and re-layouts: 3.05 us -> 3.07 us
  transfers between devices with their start and end apart: 11 -> 13, of which waited for: 7 -> 8; matrix products, arithmetic and copies ran while one was open for 0% -> 0% of each run, Pallas kernels for 12% -> 14%
where the time goes in v2:
time: 39.6 us; the launch traced here: 39.3 us
  waiting for transfers between devices  13.6 us (34%)
  starting transfers between devices  13.4 us (34%)
  Pallas kernels  6.71 us (17%)
  local copies, waits for them, and re-layouts  3.8 us (10%)
  other arithmetic  1.09 us (3%)
  between operations  0.77 us (2%)
    ppermute x11, starting transfers between devices, swap(): return lax.ppermute(value, axis, pairs)  10.9 us
    ppermute x11, waiting for transfers between devices, swap(): return lax.ppermute(value, axis, pairs)  7.47 us
    ppermute x1, waiting for transfers between devices, shards(): outer = [other_chip, lax.ppermute(parts[1], 'frames', across)]  3.29 us
    pallas_call x1, Pallas kernels, shards(): pl.pallas_call(back_kernel, out_shape=shape(inputs.shape, BF16), in_specs...  3.12 us
    unnamed x11, local copies, waits for them, and re-layouts  3.07 us
    ppermute x1, waiting for transfers between devices, shards(): other_chip = lax.ppermute(parts[0], 'frames', across)  2.81 us
    pallas_call x1, Pallas kernels, prep(): pl.pallas_call(prep_kernel, out_shape=(shape((frames, taps * quarter, spo...  2.34 us
    ppermute x1, starting transfers between devices, shards(): outer = [other_chip, lax.ppermute(parts[1], 'frames', across)]  1.39 us
  transfers between devices with their start and end apart: 13, of which 8 were waited for; matrix products, arithmetic and copies ran while one was open for 0% of the time, Pallas kernels for 14%

profile of v2, /device:TPU:0, one launch (start us, length us, event | category | flops | bytes accessed | tf_op | source)
XLA Modules:
  0.0 39.3 jit_solution(13848988677763272275)
XLA Ops:
  0.6 0.0 copy-start
  0.6 4.1 %collective-permute-start.1 = (bf16[64,512]{1,0:T(8,128)(2,1)}, bf16[64,512]{1,0:T(8,128)(2,1)S(1)}, u32[]{:S(2)}, u32[]{:S(2)}) collective-permute-start(bf16[64,512]{1,0:T(8,128)(2,1)} %bitcast.5), channel_id=1, source_target_pairs={{0,2},{1,3},{2,0},{3,1},{4,6},{5,7},{6,4},{7,5},{8,10},{9,11},{10,... | collective-permute-start | bytes 196616 | tf_op jit(solution)/shard_map/ppermute | solution.py:184
  4.8 1.3 %collective-permute-start.2 = (bf16[64,512]{1,0:T(8,128)(2,1)}, bf16[64,512]{1,0:T(8,128)(2,1)S(1)}, u32[]{:S(2)}, u32[]{:S(2)}) collective-permute-start(bf16[64,512]{1,0:T(8,128)(2,1)} %bitcast.6), channel_id=1, source_target_pairs={{0,3},{1,2},{2,1},{3,0},{4,7},{5,6},{6,5},{7,4},{8,11},{9,10},{10,... | collective-permute-start | bytes 196616 | tf_op jit(solution)/shard_map/ppermute | solution.py:184
  6.1 0.2 collective-permute-start
  6.4 0.0 copy-start.1
  6.4 1.0 %copy-done.1 = bf16[2,64,16,128]{3,2,1,0:T(8,128)(2,1)S(1)} copy-done((bf16[2,64,16,128]{3,2,1,0:T(8,128)(2,1)S(1)}, bf16[2,64,16,128]{3,2,1,0:T(8,128)(2,1)}, u32[]{:S(2)}) %copy-start.1) | copy-done | bytes 524312
  7.4 0.0 copy-start.2
  7.4 1.0 %copy-done.2 = bf16[2,64,16,128]{3,2,1,0:T(8,128)(2,1)S(1)} copy-done((bf16[2,64,16,128]{3,2,1,0:T(8,128)(2,1)S(1)}, bf16[2,64,16,128]{3,2,1,0:T(8,128)(2,1)}, u32[]{:S(2)}) %copy-start.2) | copy-done | bytes 524312
  8.4 0.0 copy-start.4
  8.4 1.0 %copy-done.4 = bf16[3,3,64,256]{3,2,1,0:T(8,128)(2,1)S(1)} copy-done((bf16[3,3,64,256]{3,2,1,0:T(8,128)(2,1)S(1)}, bf16[3,3,64,256]{3,2,1,0:T(8,128)(2,1)}, u32[]{:S(2)}) %copy-start.4) | copy-done | bytes 294936
  9.4 0.0 copy-start.3
  9.4 2.3 %prep.1 = (bf16[2,576,512]{2,1,0:T(8,128)(2,1)S(1)}, bf16[2,64,512]{2,1,0:T(8,128)(2,1)S(1)}, bf16[3,256,256]{2,1,0:T(8,128)(2,1)S(1)}) custom-call(bf16[2,64,16,128]{3,2,1,0:T(8,128)(2,1)S(1)} %copy-done.1, bf16[2,64,16,128]{3,2,1,0:T(8,128)(2,1)S(1)} %copy-done.2, bf16[3,3,64,256]{3,2,1,0:T(8,128)(2,1)S(1)} %copy-done.4), custom_call_target="tpu_custom_call" | custom-call | flops 1073741824 | bytes 4194304 | tf_op jit(solution)/shard_map/prep/pallas_call | solution.py:208
  11.8 0.0 collective-permute-done.1.refs_2_
  11.8 0.0 collective-permute-done.2.refs_3_
  11.8 1.4 %collective-permute-start.4 = (bf16[2,64,512]{2,1,0:T(8,128)(2,1)S(1)}, bf16[2,64,512]{2,1,0:T(8,128)(2,1)S(1)}, u32[]{:S(2)}, u32[]{:S(2)}) collective-permute-start(bf16[2,64,512]{2,1,0:T(8,128)(2,1)S(1)} %pad_maximum_fusion.2), channel_id=1, source_target_pairs={{0,28},{4,8},{8,4},{12,16},{16,12},{20,24},{24,20},{28,0},{1,29},{... | collective-permute-start | bytes 393224 | tf_op jit(solution)/shard_map/ppermute | solution.py:264
  13.2 0.3 collective-permute-start.6
  13.5 0.0 collective-permute-done.refs_1_
  13.5 0.0 copy-done
  13.5 1.1 %collective-permute-start.3 = (bf16[2,64,512]{2,1,0:T(8,128)(2,1)S(1)}, bf16[2,64,512]{2,1,0:T(8,128)(2,1)S(1)}, u32[]{:S(2)}, u32[]{:S(2)}) collective-permute-start(bf16[2,64,512]{2,1,0:T(8,128)(2,1)S(1)} %pad_maximum_fusion.1), channel_id=1, source_target_pairs={{0,28},{4,8},{8,4},{12,16},{16,12},{20,24},{24,20},{28,0},{1,29},{... | collective-permute-start | bytes 393224 | tf_op jit(solution)/shard_map/ppermute | solution.py:261
  14.6 0.6 %collective-permute-start.5 = (bf16[2,64,512]{2,1,0:T(8,128)(2,1)S(1)}, bf16[2,64,512]{2,1,0:T(8,128)(2,1)S(1)}, u32[]{:S(2)}, u32[]{:S(2)}) collective-permute-start(bf16[2,64,512]{2,1,0:T(8,128)(2,1)S(1)} %pad_maximum_fusion.1), channel_id=1, source_target_pairs={{0,4},{4,0},{8,12},{12,8},{16,20},{20,16},{24,28},{28,24},{1,5},{5... | collective-permute-start | bytes 393224 | tf_op jit(solution)/shard_map/ppermute | solution.py:184
  15.2 3.3 %collective-permute-done.4.refs_5_ = bf16[2,64,512]{2,1,0:T(8,128)(2,1)S(1)} collective-permute-done((bf16[2,64,512]{2,1,0:T(8,128)(2,1)S(1)}, bf16[2,64,512]{2,1,0:T(8,128)(2,1)S(1)}, u32[]{:S(2)}, u32[]{:S(2)}) %collective-permute-start.4) | collective-permute-done | bytes 131104 | tf_op jit(solution)/shard_map/ppermute | solution.py:264
  18.5 0.0 collective-permute-done.6.refs_7_
  18.5 2.8 %collective-permute-done.3.refs_4_ = bf16[2,64,512]{2,1,0:T(8,128)(2,1)S(1)} collective-permute-done((bf16[2,64,512]{2,1,0:T(8,128)(2,1)S(1)}, bf16[2,64,512]{2,1,0:T(8,128)(2,1)S(1)}, u32[]{:S(2)}, u32[]{:S(2)}) %collective-permute-start.3) | collective-permute-done | bytes 131104 | tf_op jit(solution)/shard_map/ppermute | solution.py:261
  21.3 0.0 collective-permute-done.5.refs_6_
  21.3 0.0 copy-done.3
  21.3 1.2 %main.1 = (bf16[2,256,512]{2,1,0:T(8,128)(2,1)S(1)}, f32[6,64,256]{2,1,0:T(8,128)S(1)}, f32[6,64,256]{2,1,0:T(8,128)S(1)}) custom-call(bf16[64,512]{1,0:T(8,128)(2,1)S(1)} %bitcast.8, bf16[64,512]{1,0:T(8,128)(2,1)S(1)} %collective-permute-done.refs_1_, bf16[64,512]{1,0:T(8,128)(2,1)S(1)} %collective-permute-done.1.refs_2_, ...), custom_call_target="tpu_custom_call" | custom-call | flops 1073741824 | bytes 4194304 | tf_op jit(solution)/shard_map/main/pallas_call | solution.py:268
  22.5 0.1 collective-permute-start.7
  22.6 1.7 %collective-permute-done.7 = f32[6,64,256]{2,1,0:T(8,128)S(1)} collective-permute-done((f32[6,64,256]{2,1,0:T(8,128)S(1)}, f32[6,64,256]{2,1,0:T(8,128)S(1)}, u32[]{:S(2)}, u32[]{:S(2)}) %collective-permute-start.7) | collective-permute-done | bytes 393248 | tf_op jit(solution)/shard_map/ppermute | solution.py:184
  24.3 0.1 add_convert_fusion
  24.4 0.3 collective-permute-start.8
  24.7 1.3 %collective-permute-start.9 = (bf16[3,64,256]{2,1,0:T(8,128)(2,1)S(1)}, bf16[3,64,256]{2,1,0:T(8,128)(2,1)S(1)}, u32[]{:S(2)}, u32[]{:S(2)}) collective-permute-start(bf16[3,64,256]{2,1,0:T(8,128)(2,1)S(1)} %get-tuple-element.39), channel_id=1, source_target_pairs={{0,16},{4,20},{8,24},{12,28},{16,0},{20,4},{24,8},{28,12},{1,17},{... | collective-permute-start | bytes 294920 | tf_op jit(solution)/shard_map/ppermute | solution.py:184
  26.1 3.1 %back.1 = bf16[2,64,16,128]{3,2,1,0:T(8,128)(2,1)} custom-call(bf16[2,256,512]{2,1,0:T(8,128)(2,1)S(1)} %get-tuple-element.25.g_ref, bf16[3,256,256]{2,1,0:T(8,128)(2,1)S(1)} %get-tuple-element.26.wc_ref), custom_call_target="tpu_custom_call" | custom-call | flops 3221225472 | bytes 4194304 | tf_op jit(solution)/shard_map/back/pallas_call | solution.py:286
  29.2 0.1 collective-permute-done.8
  29.3 0.1 collective-permute-done.9
  29.4 0.1 convert_add_fusion.2
  29.4 1.8 %collective-permute-start.11 = (bf16[3,64,256]{2,1,0:T(8,128)(2,1)S(1)}, bf16[3,64,256]{2,1,0:T(8,128)(2,1)S(1)}, u32[]{:S(2)}, u32[]{:S(2)}) collective-permute-start(bf16[3,64,256]{2,1,0:T(8,128)(2,1)S(1)} %get-tuple-element.28), channel_id=1, source_target_pairs={{0,8},{4,12},{8,0},{12,4},{16,24},{20,28},{24,16},{28,20},{1,9},{5... | collective-permute-start | bytes 294920 | tf_op jit(solution)/shard_map/ppermute | solution.py:184
  31.2 0.7 %collective-permute-start.10 = (bf16[3,64,256]{2,1,0:T(8,128)(2,1)S(1)}, bf16[3,64,256]{2,1,0:T(8,128)(2,1)S(1)}, u32[]{:S(2)}, u32[]{:S(2)}) collective-permute-start(bf16[3,64,256]{2,1,0:T(8,128)(2,1)S(1)} %get-tuple-element.27), channel_id=1, source_target_pairs={{0,16},{4,20},{8,24},{12,28},{16,0},{20,4},{24,8},{28,12},{1,17},{... | collective-permute-start | bytes 294920 | tf_op jit(solution)/shard_map/ppermute | solution.py:184
  31.9 2.2 %collective-permute-done.11 = bf16[3,64,256]{2,1,0:T(8,128)(2,1)S(1)} collective-permute-done((bf16[3,64,256]{2,1,0:T(8,128)(2,1)S(1)}, bf16[3,64,256]{2,1,0:T(8,128)(2,1)S(1)}, u32[]{:S(2)}, u32[]{:S(2)}) %collective-permute-start.11) | collective-permute-done | bytes 98336 | tf_op jit(solution)/shard_map/ppermute | solution.py:184
  34.1 1.7 %collective-permute-done.10 = bf16[3,64,256]{2,1,0:T(8,128)(2,1)S(1)} collective-permute-done((bf16[3,64,256]{2,1,0:T(8,128)(2,1)S(1)}, bf16[3,64,256]{2,1,0:T(8,128)(2,1)S(1)}, u32[]{:S(2)}, u32[]{:S(2)}) %collective-permute-start.10) | collective-permute-done | bytes 98336 | tf_op jit(solution)/shard_map/ppermute | solution.py:184
  35.9 0.1 collective-permute-start.12
  36.0 1.7 %collective-permute-done.12 = f32[6,64,256]{2,1,0:T(8,128)S(1)} collective-permute-done((f32[6,64,256]{2,1,0:T(8,128)S(1)}, f32[6,64,256]{2,1,0:T(8,128)S(1)}, u32[]{:S(2)}, u32[]{:S(2)}) %collective-permute-start.12) | collective-permute-done | bytes 393248 | tf_op jit(solution)/shard_map/ppermute | solution.py:184
  37.7 0.1 broadcast_select_fusion.1
  37.8 0.7 %fusion = (f32[3,64,256]{2,1,0:T(8,128)}, f32[3,64,256]{2,1,0:T(8,128)S(1)}) fusion(f32[6,64,256]{2,1,0:T(8,128)S(1)} %get-tuple-element.34), kind=kLoop, calls=%fused_computation.12 | loop fusion | bytes 786432 | tf_op jit(solution)/shard_map/slice | solution.py:303
  38.5 0.9 %pad_maximum_fusion = f32[9,64,256]{2,1,0:T(8,128)} fusion(f32[3,64,256]{2,1,0:T(8,128)S(1)} %get-tuple-element.36, f32[6,64,256]{2,1,0:T(8,128)S(1)} %get-tuple-element.33), kind=kLoop, calls=%fused_computation | loop fusion | flops 147456 | bytes 1179648 | tf_op jit(solution)/shard_map/concatenate | solution.py:302
  (7 shorter events, 0.1 us)
Async XLA Ops:
  0.6 12.8 %copy-start = (bf16[1,64,512]{2,1,0:T(8,128)(2,1)S(1)}, bf16[1,64,512]{2,1,0:T(8,128)(2,1)}, u32[]{:S(2)}) copy-start(bf16[1,64,512]{2,1,0:T(8,128)(2,1)} %param.7) | copy-start | bytes 196612
  0.6 11.1 %collective-permute-start.1 = (bf16[64,512]{1,0:T(8,128)(2,1)}, bf16[64,512]{1,0:T(8,128)(2,1)S(1)}, u32[]{:S(2)}, u32[]{:S(2)}) collective-permute-start(bf16[64,512]{1,0:T(8,128)(2,1)} %bitcast.5), channel_id=1, source_target_pairs={{0,2},{1,3},{2,0},{3,1},{4,6},{5,7},{6,4},{7,5},{8,10},{9,11},{10,... | collective-permute-start | bytes 196616 | tf_op jit(solution)/shard_map/ppermute | solution.py:184
  4.8 7.0 %collective-permute-start.2 = (bf16[64,512]{1,0:T(8,128)(2,1)}, bf16[64,512]{1,0:T(8,128)(2,1)S(1)}, u32[]{:S(2)}, u32[]{:S(2)}) collective-permute-start(bf16[64,512]{1,0:T(8,128)(2,1)} %bitcast.6), channel_id=1, source_target_pairs={{0,3},{1,2},{2,1},{3,0},{4,7},{5,6},{6,5},{7,4},{8,11},{9,10},{10,... | collective-permute-start | bytes 196616 | tf_op jit(solution)/shard_map/ppermute | solution.py:184
  6.1 7.3 %collective-permute-start = (bf16[64,512]{1,0:T(8,128)(2,1)}, bf16[64,512]{1,0:T(8,128)(2,1)S(1)}, u32[]{:S(2)}, u32[]{:S(2)}) collective-permute-start(bf16[64,512]{1,0:T(8,128)(2,1)} %bitcast.7), channel_id=1, source_target_pairs={{0,1},{1,0},{2,3},{3,2},{4,5},{5,4},{6,7},{7,6},{8,9},{9,8},{10,11... | collective-permute-start | bytes 196616 | tf_op jit(solution)/shard_map/ppermute | solution.py:184
  6.4 1.0 %copy-start.1 = (bf16[2,64,16,128]{3,2,1,0:T(8,128)(2,1)S(1)}, bf16[2,64,16,128]{3,2,1,0:T(8,128)(2,1)}, u32[]{:S(2)}) copy-start(bf16[2,64,16,128]{3,2,1,0:T(8,128)(2,1)} %x_hbm.1) | copy-start | bytes 1572868
  7.4 1.0 %copy-start.2 = (bf16[2,64,16,128]{3,2,1,0:T(8,128)(2,1)S(1)}, bf16[2,64,16,128]{3,2,1,0:T(8,128)(2,1)}, u32[]{:S(2)}) copy-start(bf16[2,64,16,128]{3,2,1,0:T(8,128)(2,1)} %y_hbm.1) | copy-start | bytes 1572868
  8.4 1.0 %copy-start.4 = (bf16[3,3,64,256]{3,2,1,0:T(8,128)(2,1)S(1)}, bf16[3,3,64,256]{3,2,1,0:T(8,128)(2,1)}, u32[]{:S(2)}) copy-start(bf16[3,3,64,256]{3,2,1,0:T(8,128)(2,1)} %sw_hbm.1) | copy-start | bytes 884740
  9.4 11.9 %copy-start.3 = (bf16[3,256,256]{2,1,0:T(8,128)(2,1)S(1)}, bf16[3,256,256]{2,1,0:T(8,128)(2,1)}, u32[]{:S(2)}) copy-start(bf16[3,256,256]{2,1,0:T(8,128)(2,1)} %refs_10_.1) | copy-start | bytes 1179652
  11.8 6.7 %collective-permute-start.4 = (bf16[2,64,512]{2,1,0:T(8,128)(2,1)S(1)}, bf16[2,64,512]{2,1,0:T(8,128)(2,1)S(1)}, u32[]{:S(2)}, u32[]{:S(2)}) collective-permute-start(bf16[2,64,512]{2,1,0:T(8,128)(2,1)S(1)} %pad_maximum_fusion.2), channel_id=1, source_target_pairs={{0,28},{4,8},{8,4},{12,16},{16,12},{20,24},{24,20},{28,0},{1,29},{... | collective-permute-start | bytes 393224 | tf_op jit(solution)/shard_map/ppermute | solution.py:264
  13.2 5.3 %collective-permute-start.6 = (bf16[2,64,512]{2,1,0:T(8,128)(2,1)S(1)}, bf16[2,64,512]{2,1,0:T(8,128)(2,1)S(1)}, u32[]{:S(2)}, u32[]{:S(2)}) collective-permute-start(bf16[2,64,512]{2,1,0:T(8,128)(2,1)S(1)} %pad_maximum_fusion.2), channel_id=1, source_target_pairs={{0,4},{4,0},{8,12},{12,8},{16,20},{20,16},{24,28},{28,24},{1,5},{5... | collective-permute-start | bytes 393224 | tf_op jit(solution)/shard_map/ppermute | solution.py:184
  13.5 7.8 %collective-permute-start.3 = (bf16[2,64,512]{2,1,0:T(8,128)(2,1)S(1)}, bf16[2,64,512]{2,1,0:T(8,128)(2,1)S(1)}, u32[]{:S(2)}, u32[]{:S(2)}) collective-permute-start(bf16[2,64,512]{2,1,0:T(8,128)(2,1)S(1)} %pad_maximum_fusion.1), channel_id=1, source_target_pairs={{0,28},{4,8},{8,4},{12,16},{16,12},{20,24},{24,20},{28,0},{1,29},{... | collective-permute-start | bytes 393224 | tf_op jit(solution)/shard_map/ppermute | solution.py:261
  14.6 6.7 %collective-permute-start.5 = (bf16[2,64,512]{2,1,0:T(8,128)(2,1)S(1)}, bf16[2,64,512]{2,1,0:T(8,128)(2,1)S(1)}, u32[]{:S(2)}, u32[]{:S(2)}) collective-permute-start(bf16[2,64,512]{2,1,0:T(8,128)(2,1)S(1)} %pad_maximum_fusion.1), channel_id=1, source_target_pairs={{0,4},{4,0},{8,12},{12,8},{16,20},{20,16},{24,28},{28,24},{1,5},{5... | collective-permute-start | bytes 393224 | tf_op jit(solution)/shard_map/ppermute | solution.py:184
  22.5 1.8 %collective-permute-start.7 = (f32[6,64,256]{2,1,0:T(8,128)S(1)}, f32[6,64,256]{2,1,0:T(8,128)S(1)}, u32[]{:S(2)}, u32[]{:S(2)}) collective-permute-start(f32[6,64,256]{2,1,0:T(8,128)S(1)} %get-tuple-element.24), channel_id=1, source_target_pairs={{0,4},{4,0},{8,12},{12,8},{16,20},{20,16},{24,28},{28,24},{1,5},{5... | collective-permute-start | bytes 1179656 | tf_op jit(solution)/shard_map/ppermute | solution.py:184
  24.4 4.9 %collective-permute-start.8 = (bf16[3,64,256]{2,1,0:T(8,128)(2,1)S(1)}, bf16[3,64,256]{2,1,0:T(8,128)(2,1)S(1)}, u32[]{:S(2)}, u32[]{:S(2)}) collective-permute-start(bf16[3,64,256]{2,1,0:T(8,128)(2,1)S(1)} %get-tuple-element.40), channel_id=1, source_target_pairs={{0,8},{4,12},{8,0},{12,4},{16,24},{20,28},{24,16},{28,20},{1,9},{5... | collective-permute-start | bytes 294920 | tf_op jit(solution)/shard_map/ppermute | solution.py:184
  24.7 4.6 %collective-permute-start.9 = (bf16[3,64,256]{2,1,0:T(8,128)(2,1)S(1)}, bf16[3,64,256]{2,1,0:T(8,128)(2,1)S(1)}, u32[]{:S(2)}, u32[]{:S(2)}) collective-permute-start(bf16[3,64,256]{2,1,0:T(8,128)(2,1)S(1)} %get-tuple-element.39), channel_id=1, source_target_pairs={{0,16},{4,20},{8,24},{12,28},{16,0},{20,4},{24,8},{28,12},{1,17},{... | collective-permute-start | bytes 294920 | tf_op jit(solution)/shard_map/ppermute | solution.py:184
  29.4 4.7 %collective-permute-start.11 = (bf16[3,64,256]{2,1,0:T(8,128)(2,1)S(1)}, bf16[3,64,256]{2,1,0:T(8,128)(2,1)S(1)}, u32[]{:S(2)}, u32[]{:S(2)}) collective-permute-start(bf16[3,64,256]{2,1,0:T(8,128)(2,1)S(1)} %get-tuple-element.28), channel_id=1, source_target_pairs={{0,8},{4,12},{8,0},{12,4},{16,24},{20,28},{24,16},{28,20},{1,9},{5... | collective-permute-start | bytes 294920 | tf_op jit(solution)/shard_map/ppermute | solution.py:184
  31.2 4.6 %collective-permute-start.10 = (bf16[3,64,256]{2,1,0:T(8,128)(2,1)S(1)}, bf16[3,64,256]{2,1,0:T(8,128)(2,1)S(1)}, u32[]{:S(2)}, u32[]{:S(2)}) collective-permute-start(bf16[3,64,256]{2,1,0:T(8,128)(2,1)S(1)} %get-tuple-element.27), channel_id=1, source_target_pairs={{0,16},{4,20},{8,24},{12,28},{16,0},{20,4},{24,8},{28,12},{1,17},{... | collective-permute-start | bytes 294920 | tf_op jit(solution)/shard_map/ppermute | solution.py:184
  35.9 1.8 %collective-permute-start.12 = (f32[6,64,256]{2,1,0:T(8,128)S(1)}, f32[6,64,256]{2,1,0:T(8,128)S(1)}, u32[]{:S(2)}, u32[]{:S(2)}) collective-permute-start(f32[6,64,256]{2,1,0:T(8,128)S(1)} %constant_dynamic-update-slice_fusion), channel_id=1, source_target_pairs={{0,4},{4,0},{8,12},{12,8},{16,20},{20,16},{24,28},{28,24},{1,5},{5... | collective-permute-start | bytes 1179656 | tf_op jit(solution)/shard_map/ppermute | solution.py:184

commit v3 on v2

--- a/solution.py
+++ b/solution.py
@@ -7,6 +7,7 @@
 from jax.experimental import pallas as pl
 from jax.experimental.pallas import tpu as pltpu
 from jax.sharding import PartitionSpec as P
+
 
 F32, BF16 = jnp.float32, jnp.bfloat16
 LANES = 128
@@ -97,50 +98,97 @@
     return lax.dot_general(a, b, (((1,), (1,)), ((), ())), preferred_element_type=F32)
 
 
-def main_kernel(scale, count, *refs):
-    pieces, rest = refs[:count], refs[count:]
-    outer, inner, rest = rest[:2], rest[2:4], rest[4:]
-    s_ref, p_ref, tw_ref, g_ref, keep_ref, send_ref, cells, part = rest
+def near_kernel(scale, count, *refs):
+    pieces, inner, rest = refs[:count], refs[count : 2 * count], refs[2 * count :]
+    s_ref, p_ref, tw_ref, base_ref, g_ref, part_ref, cells = rest
+    side = lax.rem(lax.axis_index("frames"), 2)
     me = lax.axis_index("chan")
-    at_frame = lax.axis_index("frames")
-    last = lax.axis_size("frames") - 1
     quarter, spots = pieces[0].shape
     channels = count * quarter
-    side = lax.rem(at_frame, 2)
-    has_outer = jnp.where((at_frame > 0) & (at_frame < last), 1.0, 0.0).astype(BF16)
-    cut = outer[0].shape[0]
     for k in range(count):
         at = partner(me, k, count)
         cells[0, at] = pieces[k][...]
-        cells[1 + side, at] = outer[k // cut][k % cut] * has_outer
-        cells[2 - side, at] = inner[k // cut][k % cut]
+        cells[1, at] = inner[k][...]
     now = cells[0].reshape(channels, spots)
-    before = cells[1].reshape(channels, spots)
-    after = cells[2].reshape(channels, spots)
-    w0, w1, w2 = tw_ref[0], tw_ref[1], tw_ref[2]
+    near = cells[1].reshape(channels, spots)
     dot = functools.partial(jnp.dot, preferred_element_type=F32)
-    middle = dot(w1, now)
-    g0 = ((dot(w0, now) + middle + dot(w2, before)) * 0.125).astype(BF16)
-    g1 = ((dot(w2, now) + middle + dot(w0, after)) * 0.125).astype(BF16)
-    g_ref[0] = g0
-    g_ref[1] = g1
-    both_p = p_ref[...].reshape(2 * quarter, spots)
-    e_now, e_before, e_after = (dot_nt(both_p, c) for c in (now, before, after))
+    middle = dot(tw_ref[1], now)
+    base_ref[...] = middle + dot(tw_ref[2 * side], now)
+    g = middle + dot(tw_ref[2 - 2 * side], now) + dot(tw_ref[2 * side], near)
+    g = (g * 0.125).astype(BF16)
+    g_ref[...] = g
+    pairs = p_ref[...].reshape(2 * quarter, spots)
+    e_now, e_near = dot_nt(pairs, now), dot_nt(pairs, near)
     e0, e1 = e_now[:quarter], e_now[quarter:]
     small = scale * 0.125
     taps = s_ref.shape[1] // quarter
-    spatial = (dot_nt(s_ref[0], g0) + dot_nt(s_ref[1], g1)) * scale
-    part[:taps] = spatial.reshape(taps, quarter, channels)
-    part[taps] = (e0 + e_after[quarter:]) * small
-    part[taps + 1] = (e0 + e1) * small
-    part[taps + 2] = (e_before[:quarter] + e1) * small
+    part_ref[:taps] = (dot_nt(s_ref[1 - side], g) * scale).reshape(taps, quarter, channels)
+    part_ref[taps] = e0 * small
+    part_ref[taps + 1] = (e0 + e1) * small
+    part_ref[taps + 2] = e1 * small
+    first = jnp.where(side == 0, e_near[quarter:], e_near[:quarter]) * small
+    part_ref[taps + 2 * side] += first
+
+
+def far_kernel(scale, count, *refs):
+    outer, rest = refs[:count], refs[count:]
+    base_ref, part_ref, s_ref, p_ref, tw_ref, g_ref, keep_ref, send_ref, cells, part = rest
+    at_frame = lax.axis_index("frames")
+    side = lax.rem(at_frame, 2)
+    me = lax.axis_index("chan")
+    last = lax.axis_size("frames") - 1
+    quarter, spots = outer[0].shape
+    channels = count * quarter
+    inside = jnp.where((at_frame > 0) & (at_frame < last), 1.0, 0.0).astype(BF16)
+    for k in range(count):
+        cells[partner(me, k, count)] = outer[k][...] * inside
+    far = cells[...].reshape(channels, spots)
+    g = base_ref[...] + jnp.dot(tw_ref[2 - 2 * side], far, preferred_element_type=F32)
+    g = (g * 0.125).astype(BF16)
+    g_ref[...] = g
+    e_far = dot_nt(p_ref[...].reshape(2 * quarter, spots), far)
+    taps = s_ref.shape[1] // quarter
+    spatial = (dot_nt(s_ref[side], g) * scale).reshape(taps, quarter, channels)
+    part[:taps] = part_ref[:taps] + spatial
+    part[taps:] = part_ref[taps:]
+    part[taps + 2 - 2 * side] += jnp.where(side == 0, e_far[:quarter], e_far[quarter:]) * (
+        scale * 0.125
+    )
     half = part.shape[0] // 2
     keep_ref[...] = part[pl.ds(side * half, half)]
     send_ref[...] = part[pl.ds((1 - side) * half, half)]
 
 
-def back_kernel(g_ref, wc_ref, out_ref, sums, rows):
+def finish_kernel(mine_ref, other_ref, spatial_hbm, temporal_hbm, sem):
+    side = lax.rem(lax.axis_index("frames"), 2)
+    half = mine_ref.shape[0]
+    rest = spatial_hbm.shape[0] - half
+
+    def copy_out(low, high):
+        copies = [
+            pltpu.make_async_copy(low, spatial_hbm.at[:half], sem.at[0]),
+            pltpu.make_async_copy(high.at[:rest], spatial_hbm.at[half:], sem.at[1]),
+            pltpu.make_async_copy(high.at[rest:], temporal_hbm, sem.at[2]),
+        ]
+        for copy in copies:
+            copy.start()
+        for copy in copies:
+            copy.wait()
+
+    @pl.when(side == 0)
+    def _():
+        copy_out(mine_ref, other_ref)
+
+    @pl.when(side == 1)
+    def _():
+        copy_out(other_ref, mine_ref)
+
+
+def back_kernel(near_ref, far_ref, wc_ref, out_ref, g_ref, sums, rows):
     frames, chans, height, cols = out_ref.shape
+    side = lax.rem(lax.axis_index("frames"), 2)
+    g_ref[1 - side] = near_ref[...]
+    g_ref[side] = far_ref[...]
     spread = one_hot_spread(cols)
     pooled = height // 2
     for f in range(frames):
@@ -212,7 +260,7 @@
             shape((frames, quarter, spots), BF16),
             shape((3, 4 * quarter, channels), BF16),
         ),
-        in_specs=[pl.BlockSpec(memory_space=pl.ANY)] * 3,
+        in_specs=[pl.BlockSpec(memory_space=pltpu.HBM)] * 3,
         out_specs=tuple(vmem(3)),
         scratch_shapes=[
             pltpu.VMEM(inputs.shape, BF16),
@@ -228,20 +276,19 @@
     )(inputs, saved, spatial_w)
 
 
-def reduce_frames(keep, send, beside):
+def reduce_frames(keep, send):
     count = lax.axis_size("frames")
-    side = lax.rem(lax.axis_index("frames"), 2)
     total = keep + swap(send, "frames", 1)
     bits = [1 << i for i in range(1, count.bit_length() - 1)]
     cut = total.shape[0] // 2
     a, b = total[:cut], total[cut:]
     for first, second in zip(bits, bits[::-1]):
         a, b = a.astype(BF16), b.astype(BF16)
-        a, b = both(a, swap(a, "frames", first)), both(b, swap(b, "frames", second))
-        a, b, beside = lax.optimization_barrier((a, b, beside))
+        moved_a = swap(a, "frames", first)
+        moved_b = swap(b, "frames", second)
+        a, b = both(a, moved_a), both(b, moved_b)
     mine = jnp.concatenate([a, b])
-    other = swap(mine, "frames", 1)
-    return jnp.where(side == 0, mine, other), jnp.where(side == 0, other, mine), beside
+    return mine, swap(mine, "frames", 1)
 
 
 def shards(inputs, saved, cotangent, spatial_w, temporal_w):
@@ -255,52 +302,69 @@
 
     pieces = [cotangent[0]]
     pieces += [swap(pieces[0], "chan", k) for k in range(1, count)]
-    cut = count // 2
-    parts = [jnp.stack(pieces[:cut]), jnp.stack(pieces[cut:])]
     across = [(i, (i + (1 if i % 2 else -1)) % ring) for i in range(ring)]
-    other_chip = lax.ppermute(parts[0], "frames", across)
-    sums, pooled, combined = prep(inputs, saved, spatial_w)
-    parts[1], sums, pooled = lax.optimization_barrier((parts[1], sums, pooled))
-    outer = [other_chip, lax.ppermute(parts[1], "frames", across)]
-    inner = [swap(part, "frames", 1) for part in parts]
+    held = (pltpu.with_memory_space_constraint(x, pltpu.HBM) for x in (inputs, saved, spatial_w))
+    sums, pooled, combined = prep(*held)
+    outer = [lax.ppermute(piece, "frames", across) for piece in pieces]
+    inner = [swap(piece, "frames", 1) for piece in pieces]
 
     slices = taps + 3
-    grad, keep, send = pl.pallas_call(
-        functools.partial(main_kernel, scale, count),
-        out_shape=(
-            shape((frames, channels, spots), BF16),
-            shape((slices // 2, quarter, channels), F32),
-            shape((slices // 2, quarter, channels), F32),
-        ),
-        in_specs=vmem(count + 7),
+    limit = pltpu.CompilerParams(vmem_limit_bytes=20 << 20)
+    part_shape = shape((slices, quarter, channels), F32)
+    half_shape = shape((slices // 2, quarter, channels), F32)
+    base, g_near, part = pl.pallas_call(
+        functools.partial(near_kernel, scale, count),
+        out_shape=(shape((channels, spots), F32), shape((channels, spots), BF16), part_shape),
+        in_specs=vmem(2 * count + 3),
+        out_specs=tuple(vmem(3)),
+        scratch_shapes=[pltpu.VMEM((2, count, quarter, spots), BF16)],
+        compiler_params=limit,
+        cost_estimate=cost(1 << 30, 4 << 20),
+        name="near",
+    )(*pieces, *inner, sums, pooled, temporal_w)
+    g_far, keep, send = pl.pallas_call(
+        functools.partial(far_kernel, scale, count),
+        out_shape=(shape((channels, spots), BF16), half_shape, half_shape),
+        in_specs=vmem(count + 5),
         out_specs=tuple(vmem(3)),
         scratch_shapes=[
-            pltpu.VMEM((3, count, quarter, spots), BF16),
-            pltpu.VMEM((slices, quarter, channels), F32),
+            pltpu.VMEM((count, quarter, spots), BF16),
+            pltpu.VMEM(part_shape.shape, F32),
         ],
-        compiler_params=pltpu.CompilerParams(vmem_limit_bytes=20 << 20),
-        cost_estimate=cost(1 << 30, 4 << 20),
-        name="main",
-    )(*pieces, *outer, *inner, sums, pooled, temporal_w)
+        compiler_params=limit,
+        cost_estimate=cost(1 << 29, 4 << 20),
+        name="far",
+    )(*outer, base, part, sums, pooled, temporal_w)
 
     input_grad = pl.pallas_call(
         back_kernel,
         out_shape=shape(inputs.shape, BF16),
-        in_specs=vmem(2),
+        in_specs=vmem(3),
         out_specs=vmem(1)[0],
         scratch_shapes=[
+            pltpu.VMEM((frames, channels, spots), BF16),
             pltpu.VMEM((height // 2, 4 * quarter, cols), F32),
             pltpu.VMEM((quarter * height, cols), F32),
         ],
-        compiler_params=pltpu.CompilerParams(vmem_limit_bytes=20 << 20),
+        compiler_params=limit,
         cost_estimate=cost(3 << 30, 4 << 20),
         name="back",
-    )(grad, combined)
-
-    low, high, input_grad = reduce_frames(keep, send, input_grad)
-    rest = taps - slices // 2
-    spatial = jnp.concatenate([low, high[:rest]])
-    return (input_grad, spatial.reshape(spatial_w.shape), high[rest:])
+    )(g_near, g_far, combined)
+
+    spatial, temporal = pl.pallas_call(
+        finish_kernel,
+        out_shape=(
+            shape((taps, quarter, channels), F32),
+            shape((slices - taps, quarter, channels), F32),
+        ),
+        in_specs=vmem(2),
+        out_specs=(pl.BlockSpec(memory_space=pltpu.HBM),) * 2,
+        scratch_shapes=[pltpu.SemaphoreType.DMA((3,))],
+        compiler_params=limit,
+        cost_estimate=cost(0, 4 << 20),
+        name="finish",
+    )(*reduce_frames(keep, send))
+    return (input_grad, spatial.reshape(spatial_w.shape), temporal)
 
 
 def solution(mesh):

time: 39.6 us -> 41.6 us (1.051)
  local copies, waits for them, and re-layouts: 3.8 us -> 0.02 us
  starting transfers between devices: 13.4 us -> 16.2 us
  waiting for transfers between devices: 13.6 us -> 15.7 us
  Pallas kernels: 6.71 us -> 8.62 us
  other arithmetic: 1.09 us -> 0.18 us
    ppermute x11 -> x13, waiting for transfers between devices: 7.47 us -> 12.7 us  [swap(): return lax.ppermute(value, axis, pairs)]
    ppermute x2 -> x4, starting transfers between devices: 2.51 us -> 6.09 us  [shards(): outer = [lax.ppermute(piece, 'frames', across) for piece in pieces]]
    ppermute x2 -> x4, waiting for transfers between devices: 6.09 us -> 2.97 us  [shards(): outer = [lax.ppermute(piece, 'frames', across) for piece in pieces]]
    unnamed x11 -> x4, local copies, waits for them, and re-layouts: 3.07 us -> 0.01 us
    pallas_call x1 -> x3, Pallas kernels: 1.24 us -> 2.46 us  [the longest x1 0.9 us: shards(): pl.pallas_call(finish_kernel, out_shape=(shape((taps, quarter, channels),...]
    concatenate x1, other arithmetic: 0.85 us -> 0.03 us  [reduce_frames(): mine = jnp.concatenate([a, b])]
    ppermute x11 -> x13, starting transfers between devices: 10.9 us -> 10.1 us  [swap(): return lax.ppermute(value, axis, pairs)]
    slice x1 -> x0, local copies, waits for them, and re-layouts: 0.7 us -> none  [shards(): return (input_grad, spatial.reshape(spatial_w.shape), high[rest:])]
  transfers between devices with their start and end apart: 13 -> 17, of which waited for: 8 -> 9; matrix products, arithmetic and copies ran while one was open for 0% -> 0% of each run, Pallas kernels for 14% -> 17%
where the time goes in v3:
time: 41.6 us; the launch traced here: 41.5 us
  starting transfers between devices  16.2 us (39%)
  waiting for transfers between devices  15.7 us (38%)
  Pallas kernels  8.62 us (21%)
  between operations  0.75 us (2%)
    ppermute x13, waiting for transfers between devices, swap(): return lax.ppermute(value, axis, pairs)  12.7 us
    ppermute x13, starting transfers between devices, swap(): return lax.ppermute(value, axis, pairs)  10.1 us
    ppermute x4, starting transfers between devices, shards(): outer = [lax.ppermute(piece, 'frames', across) for piece in pieces]  6.09 us
    pallas_call x1, Pallas kernels, shards(): pl.pallas_call(back_kernel, out_shape=shape(inputs.shape, BF16), in_specs...  3.12 us
    pallas_call x1, Pallas kernels, prep(): pl.pallas_call(prep_kernel, out_shape=(shape((frames, taps * quarter, spo...  3.03 us
    ppermute x4, waiting for transfers between devices, shards(): outer = [lax.ppermute(piece, 'frames', across) for piece in pieces]  2.97 us
    pallas_call x1, Pallas kernels, shards(): pl.pallas_call(finish_kernel, out_shape=(shape((taps, quarter, channels),...  0.9 us
    pallas_call x1, Pallas kernels, shards(): pl.pallas_call(functools.partial(near_kernel, scale, count), out_shape=(s...  0.83 us
  transfers between devices with their start and end apart: 17, of which 9 were waited for; matrix products, arithmetic and copies ran while one was open for 0% of the time, Pallas kernels for 17%

profile of v3, /device:TPU:0, one launch (start us, length us, event | category | flops | bytes accessed | tf_op | source)
XLA Modules:
  0.0 41.5 jit_solution(13059862698249372534)
XLA Ops:
  0.6 0.0 copy-start
  0.6 0.0 copy-start.1
  0.7 5.1 %collective-permute-start.2 = (bf16[64,512]{1,0:T(8,128)(2,1)}, bf16[64,512]{1,0:T(8,128)(2,1)S(1)}, u32[]{:S(2)}, u32[]{:S(2)}) collective-permute-start(bf16[64,512]{1,0:T(8,128)(2,1)} %bitcast.2), channel_id=1, source_target_pairs={{0,3},{1,2},{2,1},{3,0},{4,7},{5,6},{6,5},{7,4},{8,11},{9,10},{10,... | collective-permute-start | bytes 196616 | tf_op jit(solution)/shard_map/ppermute | solution.py:232
  5.8 0.0 collective-permute-start.1
  5.8 0.6 %collective-permute-start = (bf16[64,512]{1,0:T(8,128)(2,1)}, bf16[64,512]{1,0:T(8,128)(2,1)S(1)}, u32[]{:S(2)}, u32[]{:S(2)}) collective-permute-start(bf16[64,512]{1,0:T(8,128)(2,1)} %bitcast.4), channel_id=1, source_target_pairs={{0,1},{1,0},{2,3},{3,2},{4,5},{5,4},{6,7},{7,6},{8,9},{9,8},{10,11... | collective-permute-start | bytes 196616 | tf_op jit(solution)/shard_map/ppermute | solution.py:232
  6.4 1.3 %collective-permute-start.7 = (bf16[64,512]{1,0:T(8,128)(2,1)}, bf16[64,512]{1,0:T(8,128)(2,1)S(1)}, u32[]{:S(2)}, u32[]{:S(2)}) collective-permute-start(bf16[64,512]{1,0:T(8,128)(2,1)} %bitcast.5), channel_id=1, source_target_pairs={{0,28},{4,8},{8,4},{12,16},{16,12},{20,24},{24,20},{28,0},{1,29},{... | collective-permute-start | bytes 196616 | tf_op jit(solution)/shard_map/ppermute | solution.py:308
  7.8 0.4 %collective-permute-start.3 = (bf16[64,512]{1,0:T(8,128)(2,1)}, bf16[64,512]{1,0:T(8,128)(2,1)S(1)}, u32[]{:S(2)}, u32[]{:S(2)}) collective-permute-start(bf16[64,512]{1,0:T(8,128)(2,1)} %bitcast.6), channel_id=1, source_target_pairs={{0,4},{4,0},{8,12},{12,8},{16,20},{20,16},{24,28},{28,24},{1,5},{5... | collective-permute-start | bytes 196616 | tf_op jit(solution)/shard_map/ppermute | solution.py:232
  8.2 0.4 collective-permute-done.2.refs_3_
  8.6 0.0 collective-permute-start.6
  8.6 3.0 %collective-permute-done.1.refs_2_ = bf16[64,512]{1,0:T(8,128)(2,1)S(1)} collective-permute-done((bf16[64,512]{1,0:T(8,128)(2,1)}, bf16[64,512]{1,0:T(8,128)(2,1)S(1)}, u32[]{:S(2)}, u32[]{:S(2)}) %collective-permute-start.1) | collective-permute-done | bytes 65568 | tf_op jit(solution)/shard_map/ppermute | solution.py:232
  11.6 0.0 collective-permute-start.5
  11.6 0.0 collective-permute-done.refs_1_
  11.6 0.5 %collective-permute-start.4 = (bf16[64,512]{1,0:T(8,128)(2,1)S(1)}, bf16[64,512]{1,0:T(8,128)(2,1)S(1)}, u32[]{:S(2)}, u32[]{:S(2)}) collective-permute-start(bf16[64,512]{1,0:T(8,128)(2,1)S(1)} %collective-permute-done.refs_1_), channel_id=1, source_target_pairs={{0,4},{4,0},{8,12},{12,8},{16,20},{20,16},{24,28},{28,24},{1,5},{5... | collective-permute-start | bytes 196616 | tf_op jit(solution)/shard_map/ppermute | solution.py:232
  12.1 3.0 %prep.1 = (bf16[2,576,512]{2,1,0:T(8,128)(2,1)S(1)}, bf16[2,64,512]{2,1,0:T(8,128)(2,1)S(1)}, bf16[3,256,256]{2,1,0:T(8,128)(2,1)S(1)}) custom-call(bf16[2,64,16,128]{3,2,1,0:T(8,128)(2,1)} %x_hbm.1, bf16[2,64,16,128]{3,2,1,0:T(8,128)(2,1)} %y_hbm.1, bf16[3,3,64,256]{3,2,1,0:T(8,128)(2,1)} %sw_hbm.1), custom_call_target="tpu_custom_call" | custom-call | flops 1073741824 | bytes 4194304 | tf_op jit(solution)/shard_map/prep/pallas_call | solution.py:256
  15.2 0.0 collective-permute-done.3.refs_4_
  15.2 2.1 %collective-permute-start.10 = (bf16[64,512]{1,0:T(8,128)(2,1)S(1)}, bf16[64,512]{1,0:T(8,128)(2,1)S(1)}, u32[]{:S(2)}, u32[]{:S(2)}) collective-permute-start(bf16[64,512]{1,0:T(8,128)(2,1)S(1)} %collective-permute-done.2.refs_3_), channel_id=1, source_target_pairs={{0,28},{4,8},{8,4},{12,16},{16,12},{20,24},{24,20},{28,0},{1,29},{... | collective-permute-start | bytes 196616 | tf_op jit(solution)/shard_map/ppermute | solution.py:308
  17.3 0.0 collective-permute-done.6.refs_7_
  17.3 0.6 %collective-permute-start.9 = (bf16[64,512]{1,0:T(8,128)(2,1)S(1)}, bf16[64,512]{1,0:T(8,128)(2,1)S(1)}, u32[]{:S(2)}, u32[]{:S(2)}) collective-permute-start(bf16[64,512]{1,0:T(8,128)(2,1)S(1)} %collective-permute-done.1.refs_2_), channel_id=1, source_target_pairs={{0,28},{4,8},{8,4},{12,16},{16,12},{20,24},{24,20},{28,0},{1,29},{... | collective-permute-start | bytes 196616 | tf_op jit(solution)/shard_map/ppermute | solution.py:308
  17.9 0.0 collective-permute-done.5.refs_6_
  17.9 2.1 %collective-permute-start.8 = (bf16[64,512]{1,0:T(8,128)(2,1)S(1)}, bf16[64,512]{1,0:T(8,128)(2,1)S(1)}, u32[]{:S(2)}, u32[]{:S(2)}) collective-permute-start(bf16[64,512]{1,0:T(8,128)(2,1)S(1)} %collective-permute-done.refs_1_), channel_id=1, source_target_pairs={{0,28},{4,8},{8,4},{12,16},{16,12},{20,24},{24,20},{28,0},{1,29},{... | collective-permute-start | bytes 196616 | tf_op jit(solution)/shard_map/ppermute | solution.py:308
  19.9 0.0 collective-permute-done.4.refs_5_
  19.9 0.0 copy-done
  20.0 0.0 copy-done.1
  20.0 0.8 %near.1 = (f32[256,512]{1,0:T(8,128)S(1)}, bf16[256,512]{1,0:T(8,128)(2,1)S(1)}, f32[12,64,256]{2,1,0:T(8,128)S(1)}) custom-call(bf16[64,512]{1,0:T(8,128)(2,1)S(1)} %bitcast.7, bf16[64,512]{1,0:T(8,128)(2,1)S(1)} %collective-permute-done.refs_1_, bf16[64,512]{1,0:T(8,128)(2,1)S(1)} %collective-permute-done.1.refs_2_, ...), custom_call_target="tpu_custom_call" | custom-call | flops 1073741824 | bytes 4194304 | tf_op jit(solution)/shard_map/near/pallas_call | solution.py:315
  20.8 0.0 collective-permute-done.7.refs_0_
  20.8 0.0 collective-permute-done.10.refs_3_
  20.8 1.8 %collective-permute-done.9.refs_2_ = bf16[64,512]{1,0:T(8,128)(2,1)S(1)} collective-permute-done((bf16[64,512]{1,0:T(8,128)(2,1)S(1)}, bf16[64,512]{1,0:T(8,128)(2,1)S(1)}, u32[]{:S(2)}, u32[]{:S(2)}) %collective-permute-start.9) | collective-permute-done | bytes 65568 | tf_op jit(solution)/shard_map/ppermute | solution.py:308
  22.6 1.2 %collective-permute-done.8.refs_1_ = bf16[64,512]{1,0:T(8,128)(2,1)S(1)} collective-permute-done((bf16[64,512]{1,0:T(8,128)(2,1)S(1)}, bf16[64,512]{1,0:T(8,128)(2,1)S(1)}, u32[]{:S(2)}, u32[]{:S(2)}) %collective-permute-start.8) | collective-permute-done | bytes 65568 | tf_op jit(solution)/shard_map/ppermute | solution.py:308
  23.8 0.7 %far.1 = (bf16[256,512]{1,0:T(8,128)(2,1)S(1)}, f32[6,64,256]{2,1,0:T(8,128)S(1)}, f32[6,64,256]{2,1,0:T(8,128)S(1)}) custom-call(bf16[64,512]{1,0:T(8,128)(2,1)S(1)} %collective-permute-done.7.refs_0_, bf16[64,512]{1,0:T(8,128)(2,1)S(1)} %collective-permute-done.8.refs_1_, bf16[64,512]{1,0:T(8,128)(2,1)S(1)} %collective-permute-done.9.refs_2_, ...), custom_call_target="tpu_custom_call" | custom-call | flops 536870912 | bytes 4194304 | tf_op jit(solution)/shard_map/far/pallas_call | solution.py:325
  24.5 0.1 collective-permute-start.11
  24.6 1.7 %collective-permute-done.11 = f32[6,64,256]{2,1,0:T(8,128)S(1)} collective-permute-done((f32[6,64,256]{2,1,0:T(8,128)S(1)}, f32[6,64,256]{2,1,0:T(8,128)S(1)}, u32[]{:S(2)}, u32[]{:S(2)}) %collective-permute-start.11) | collective-permute-done | bytes 393248 | tf_op jit(solution)/shard_map/ppermute | solution.py:232
  26.3 0.1 add_convert_fusion
  26.4 0.6 %collective-permute-start.12 = (bf16[3,64,256]{2,1,0:T(8,128)(2,1)S(1)}, bf16[3,64,256]{2,1,0:T(8,128)(2,1)S(1)}, u32[]{:S(2)}, u32[]{:S(2)}) collective-permute-start(bf16[3,64,256]{2,1,0:T(8,128)(2,1)S(1)} %get-tuple-element.27), channel_id=1, source_target_pairs={{0,8},{4,12},{8,0},{12,4},{16,24},{20,28},{24,16},{28,20},{1,9},{5... | collective-permute-start | bytes 294920 | tf_op jit(solution)/shard_map/ppermute | solution.py:232
  27.0 0.8 %collective-permute-start.14 = (bf16[3,64,256]{2,1,0:T(8,128)(2,1)S(1)}, bf16[3,64,256]{2,1,0:T(8,128)(2,1)S(1)}, u32[]{:S(2)}, u32[]{:S(2)}) collective-permute-start(bf16[3,64,256]{2,1,0:T(8,128)(2,1)S(1)} %get-tuple-element.28), channel_id=1, source_target_pairs={{0,16},{4,20},{8,24},{12,28},{16,0},{20,4},{24,8},{28,12},{1,17},{... | collective-permute-start | bytes 294920 | tf_op jit(solution)/shard_map/ppermute | solution.py:232
  27.8 3.5 %collective-permute-done.12 = bf16[3,64,256]{2,1,0:T(8,128)(2,1)S(1)} collective-permute-done((bf16[3,64,256]{2,1,0:T(8,128)(2,1)S(1)}, bf16[3,64,256]{2,1,0:T(8,128)(2,1)S(1)}, u32[]{:S(2)}, u32[]{:S(2)}) %collective-permute-start.12) | collective-permute-done | bytes 98336 | tf_op jit(solution)/shard_map/ppermute | solution.py:232
  31.3 0.5 %collective-permute-done.14 = bf16[3,64,256]{2,1,0:T(8,128)(2,1)S(1)} collective-permute-done((bf16[3,64,256]{2,1,0:T(8,128)(2,1)S(1)}, bf16[3,64,256]{2,1,0:T(8,128)(2,1)S(1)}, u32[]{:S(2)}, u32[]{:S(2)}) %collective-permute-start.14) | collective-permute-done | bytes 98336 | tf_op jit(solution)/shard_map/ppermute | solution.py:232
  31.8 0.1 add_convert_fusion.2
  31.9 0.9 %collective-permute-start.13 = (bf16[3,64,256]{2,1,0:T(8,128)(2,1)S(1)}, bf16[3,64,256]{2,1,0:T(8,128)(2,1)S(1)}, u32[]{:S(2)}, u32[]{:S(2)}) collective-permute-start(bf16[3,64,256]{2,1,0:T(8,128)(2,1)S(1)} %get-tuple-element.25), channel_id=1, source_target_pairs={{0,16},{4,20},{8,24},{12,28},{16,0},{20,4},{24,8},{28,12},{1,17},{... | collective-permute-start | bytes 294920 | tf_op jit(solution)/shard_map/ppermute | solution.py:232
  32.7 1.0 %collective-permute-start.15 = (bf16[3,64,256]{2,1,0:T(8,128)(2,1)S(1)}, bf16[3,64,256]{2,1,0:T(8,128)(2,1)S(1)}, u32[]{:S(2)}, u32[]{:S(2)}) collective-permute-start(bf16[3,64,256]{2,1,0:T(8,128)(2,1)S(1)} %get-tuple-element.26), channel_id=1, source_target_pairs={{0,8},{4,12},{8,0},{12,4},{16,24},{20,28},{24,16},{28,20},{1,9},{5... | collective-permute-start | bytes 294920 | tf_op jit(solution)/shard_map/ppermute | solution.py:232
  33.7 2.8 %collective-permute-done.13 = bf16[3,64,256]{2,1,0:T(8,128)(2,1)S(1)} collective-permute-done((bf16[3,64,256]{2,1,0:T(8,128)(2,1)S(1)}, bf16[3,64,256]{2,1,0:T(8,128)(2,1)S(1)}, u32[]{:S(2)}, u32[]{:S(2)}) %collective-permute-start.13) | collective-permute-done | bytes 98336 | tf_op jit(solution)/shard_map/ppermute | solution.py:232
  36.6 0.8 %collective-permute-done.15 = bf16[3,64,256]{2,1,0:T(8,128)(2,1)S(1)} collective-permute-done((bf16[3,64,256]{2,1,0:T(8,128)(2,1)S(1)}, bf16[3,64,256]{2,1,0:T(8,128)(2,1)S(1)}, u32[]{:S(2)}, u32[]{:S(2)}) %collective-permute-start.15) | collective-permute-done | bytes 98336 | tf_op jit(solution)/shard_map/ppermute | solution.py:232
  37.4 0.1 collective-permute-start.16
  37.5 3.1 %back.1 = bf16[2,64,16,128]{3,2,1,0:T(8,128)(2,1)} custom-call(bf16[256,512]{1,0:T(8,128)(2,1)S(1)} %get-tuple-element.16.near_ref, bf16[256,512]{1,0:T(8,128)(2,1)S(1)} %get-tuple-element.19.far_ref, bf16[3,256,256]{2,1,0:T(8,128)(2,1)S(1)} %get-tuple-element.20.wc_ref), custom_call_target="tpu_custom_call" | custom-call | flops 3221225472 | bytes 4194304 | tf_op jit(solution)/shard_map/back/pallas_call | solution.py:339
  40.6 0.0 collective-permute-done.16.other_ref
  40.6 0.9 %finish.1 = (f32[9,64,256]{2,1,0:T(8,128)}, f32[3,64,256]{2,1,0:T(8,128)}) custom-call(f32[6,64,256]{2,1,0:T(8,128)S(1)} %pad_maximum_fusion.mine_ref, f32[6,64,256]{2,1,0:T(8,128)S(1)} %collective-permute-done.16.other_ref), custom_call_target="tpu_custom_call" | custom-call | bytes 4194304 | tf_op jit(solution)/shard_map/finish/pallas_call | solution.py:354
  (4 shorter events, 0.1 us)
Async XLA Ops:
  0.6 19.3 %copy-start = (bf16[3,256,256]{2,1,0:T(8,128)(2,1)S(1)}, bf16[3,256,256]{2,1,0:T(8,128)(2,1)}, u32[]{:S(2)}) copy-start(bf16[3,256,256]{2,1,0:T(8,128)(2,1)} %refs_8_.1) | copy-start | bytes 1179652
  0.6 19.3 %copy-start.1 = (bf16[1,64,512]{2,1,0:T(8,128)(2,1)S(1)}, bf16[1,64,512]{2,1,0:T(8,128)(2,1)}, u32[]{:S(2)}) copy-start(bf16[1,64,512]{2,1,0:T(8,128)(2,1)} %param.7) | copy-start | bytes 196612
  0.7 7.9 %collective-permute-start.2 = (bf16[64,512]{1,0:T(8,128)(2,1)}, bf16[64,512]{1,0:T(8,128)(2,1)S(1)}, u32[]{:S(2)}, u32[]{:S(2)}) collective-permute-start(bf16[64,512]{1,0:T(8,128)(2,1)} %bitcast.2), channel_id=1, source_target_pairs={{0,3},{1,2},{2,1},{3,0},{4,7},{5,6},{6,5},{7,4},{8,11},{9,10},{10,... | collective-permute-start | bytes 196616 | tf_op jit(solution)/shard_map/ppermute | solution.py:232
  5.8 5.8 %collective-permute-start.1 = (bf16[64,512]{1,0:T(8,128)(2,1)}, bf16[64,512]{1,0:T(8,128)(2,1)S(1)}, u32[]{:S(2)}, u32[]{:S(2)}) collective-permute-start(bf16[64,512]{1,0:T(8,128)(2,1)} %bitcast.3), channel_id=1, source_target_pairs={{0,2},{1,3},{2,0},{3,1},{4,6},{5,7},{6,4},{7,5},{8,10},{9,11},{10,... | collective-permute-start | bytes 196616 | tf_op jit(solution)/shard_map/ppermute | solution.py:232
  5.8 5.8 %collective-permute-start = (bf16[64,512]{1,0:T(8,128)(2,1)}, bf16[64,512]{1,0:T(8,128)(2,1)S(1)}, u32[]{:S(2)}, u32[]{:S(2)}) collective-permute-start(bf16[64,512]{1,0:T(8,128)(2,1)} %bitcast.4), channel_id=1, source_target_pairs={{0,1},{1,0},{2,3},{3,2},{4,5},{5,4},{6,7},{7,6},{8,9},{9,8},{10,11... | collective-permute-start | bytes 196616 | tf_op jit(solution)/shard_map/ppermute | solution.py:232
  6.4 14.4 %collective-permute-start.7 = (bf16[64,512]{1,0:T(8,128)(2,1)}, bf16[64,512]{1,0:T(8,128)(2,1)S(1)}, u32[]{:S(2)}, u32[]{:S(2)}) collective-permute-start(bf16[64,512]{1,0:T(8,128)(2,1)} %bitcast.5), channel_id=1, source_target_pairs={{0,28},{4,8},{8,4},{12,16},{16,12},{20,24},{24,20},{28,0},{1,29},{... | collective-permute-start | bytes 196616 | tf_op jit(solution)/shard_map/ppermute | solution.py:308
  7.8 7.4 %collective-permute-start.3 = (bf16[64,512]{1,0:T(8,128)(2,1)}, bf16[64,512]{1,0:T(8,128)(2,1)S(1)}, u32[]{:S(2)}, u32[]{:S(2)}) collective-permute-start(bf16[64,512]{1,0:T(8,128)(2,1)} %bitcast.6), channel_id=1, source_target_pairs={{0,4},{4,0},{8,12},{12,8},{16,20},{20,16},{24,28},{28,24},{1,5},{5... | collective-permute-start | bytes 196616 | tf_op jit(solution)/shard_map/ppermute | solution.py:232
  8.6 8.7 %collective-permute-start.6 = (bf16[64,512]{1,0:T(8,128)(2,1)S(1)}, bf16[64,512]{1,0:T(8,128)(2,1)S(1)}, u32[]{:S(2)}, u32[]{:S(2)}) collective-permute-start(bf16[64,512]{1,0:T(8,128)(2,1)S(1)} %collective-permute-done.2.refs_3_), channel_id=1, source_target_pairs={{0,4},{4,0},{8,12},{12,8},{16,20},{20,16},{24,28},{28,24},{1,5},{5... | collective-permute-start | bytes 196616 | tf_op jit(solution)/shard_map/ppermute | solution.py:232
  11.6 6.3 %collective-permute-start.5 = (bf16[64,512]{1,0:T(8,128)(2,1)S(1)}, bf16[64,512]{1,0:T(8,128)(2,1)S(1)}, u32[]{:S(2)}, u32[]{:S(2)}) collective-permute-start(bf16[64,512]{1,0:T(8,128)(2,1)S(1)} %collective-permute-done.1.refs_2_), channel_id=1, source_target_pairs={{0,4},{4,0},{8,12},{12,8},{16,20},{20,16},{24,28},{28,24},{1,5},{5... | collective-permute-start | bytes 196616 | tf_op jit(solution)/shard_map/ppermute | solution.py:232
  11.6 8.3 %collective-permute-start.4 = (bf16[64,512]{1,0:T(8,128)(2,1)S(1)}, bf16[64,512]{1,0:T(8,128)(2,1)S(1)}, u32[]{:S(2)}, u32[]{:S(2)}) collective-permute-start(bf16[64,512]{1,0:T(8,128)(2,1)S(1)} %collective-permute-done.refs_1_), channel_id=1, source_target_pairs={{0,4},{4,0},{8,12},{12,8},{16,20},{20,16},{24,28},{28,24},{1,5},{5... | collective-permute-start | bytes 196616 | tf_op jit(solution)/shard_map/ppermute | solution.py:232
  15.2 5.6 %collective-permute-start.10 = (bf16[64,512]{1,0:T(8,128)(2,1)S(1)}, bf16[64,512]{1,0:T(8,128)(2,1)S(1)}, u32[]{:S(2)}, u32[]{:S(2)}) collective-permute-start(bf16[64,512]{1,0:T(8,128)(2,1)S(1)} %collective-permute-done.2.refs_3_), channel_id=1, source_target_pairs={{0,28},{4,8},{8,4},{12,16},{16,12},{20,24},{24,20},{28,0},{1,29},{... | collective-permute-start | bytes 196616 | tf_op jit(solution)/shard_map/ppermute | solution.py:308
  17.3 5.3 %collective-permute-start.9 = (bf16[64,512]{1,0:T(8,128)(2,1)S(1)}, bf16[64,512]{1,0:T(8,128)(2,1)S(1)}, u32[]{:S(2)}, u32[]{:S(2)}) collective-permute-start(bf16[64,512]{1,0:T(8,128)(2,1)S(1)} %collective-permute-done.1.refs_2_), channel_id=1, source_target_pairs={{0,28},{4,8},{8,4},{12,16},{16,12},{20,24},{24,20},{28,0},{1,29},{... | collective-permute-start | bytes 196616 | tf_op jit(solution)/shard_map/ppermute | solution.py:308
  17.9 5.9 %collective-permute-start.8 = (bf16[64,512]{1,0:T(8,128)(2,1)S(1)}, bf16[64,512]{1,0:T(8,128)(2,1)S(1)}, u32[]{:S(2)}, u32[]{:S(2)}) collective-permute-start(bf16[64,512]{1,0:T(8,128)(2,1)S(1)} %collective-permute-done.refs_1_), channel_id=1, source_target_pairs={{0,28},{4,8},{8,4},{12,16},{16,12},{20,24},{24,20},{28,0},{1,29},{... | collective-permute-start | bytes 196616 | tf_op jit(solution)/shard_map/ppermute | solution.py:308
  24.5 1.8 %collective-permute-start.11 = (f32[6,64,256]{2,1,0:T(8,128)S(1)}, f32[6,64,256]{2,1,0:T(8,128)S(1)}, u32[]{:S(2)}, u32[]{:S(2)}) collective-permute-start(f32[6,64,256]{2,1,0:T(8,128)S(1)} %get-tuple-element.22), channel_id=1, source_target_pairs={{0,4},{4,0},{8,12},{12,8},{16,20},{20,16},{24,28},{28,24},{1,5},{5... | collective-permute-start | bytes 1179656 | tf_op jit(solution)/shard_map/ppermute | solution.py:232
  26.4 4.9 %collective-permute-start.12 = (bf16[3,64,256]{2,1,0:T(8,128)(2,1)S(1)}, bf16[3,64,256]{2,1,0:T(8,128)(2,1)S(1)}, u32[]{:S(2)}, u32[]{:S(2)}) collective-permute-start(bf16[3,64,256]{2,1,0:T(8,128)(2,1)S(1)} %get-tuple-element.27), channel_id=1, source_target_pairs={{0,8},{4,12},{8,0},{12,4},{16,24},{20,28},{24,16},{28,20},{1,9},{5... | collective-permute-start | bytes 294920 | tf_op jit(solution)/shard_map/ppermute | solution.py:232
  27.0 4.8 %collective-permute-start.14 = (bf16[3,64,256]{2,1,0:T(8,128)(2,1)S(1)}, bf16[3,64,256]{2,1,0:T(8,128)(2,1)S(1)}, u32[]{:S(2)}, u32[]{:S(2)}) collective-permute-start(bf16[3,64,256]{2,1,0:T(8,128)(2,1)S(1)} %get-tuple-element.28), channel_id=1, source_target_pairs={{0,16},{4,20},{8,24},{12,28},{16,0},{20,4},{24,8},{28,12},{1,17},{... | collective-permute-start | bytes 294920 | tf_op jit(solution)/shard_map/ppermute | solution.py:232
  31.9 4.7 %collective-permute-start.13 = (bf16[3,64,256]{2,1,0:T(8,128)(2,1)S(1)}, bf16[3,64,256]{2,1,0:T(8,128)(2,1)S(1)}, u32[]{:S(2)}, u32[]{:S(2)}) collective-permute-start(bf16[3,64,256]{2,1,0:T(8,128)(2,1)S(1)} %get-tuple-element.25), channel_id=1, source_target_pairs={{0,16},{4,20},{8,24},{12,28},{16,0},{20,4},{24,8},{28,12},{1,17},{... | collective-permute-start | bytes 294920 | tf_op jit(solution)/shard_map/ppermute | solution.py:232
  32.7 4.6 %collective-permute-start.15 = (bf16[3,64,256]{2,1,0:T(8,128)(2,1)S(1)}, bf16[3,64,256]{2,1,0:T(8,128)(2,1)S(1)}, u32[]{:S(2)}, u32[]{:S(2)}) collective-permute-start(bf16[3,64,256]{2,1,0:T(8,128)(2,1)S(1)} %get-tuple-element.26), channel_id=1, source_target_pairs={{0,8},{4,12},{8,0},{12,4},{16,24},{20,28},{24,16},{28,20},{1,9},{5... | collective-permute-start | bytes 294920 | tf_op jit(solution)/shard_map/ppermute | solution.py:232
  37.4 3.2 %collective-permute-start.16 = (f32[6,64,256]{2,1,0:T(8,128)S(1)}, f32[6,64,256]{2,1,0:T(8,128)S(1)}, u32[]{:S(2)}, u32[]{:S(2)}) collective-permute-start(f32[6,64,256]{2,1,0:T(8,128)S(1)} %pad_maximum_fusion.mine_ref), channel_id=1, source_target_pairs={{0,4},{4,0},{8,12},{12,8},{16,20},{20,16},{24,28},{28,24},{1,5},{5... | collective-permute-start | bytes 1179656 | tf_op jit(solution)/shard_map/ppermute | solution.py:232

commit v4 on v3

--- a/solution.py
+++ b/solution.py
@@ -36,47 +36,50 @@
     return jnp.where(hit, 1.0, 0.0).astype(BF16)
 
 
-def prep_kernel(x_hbm, y_hbm, sw_hbm, s_ref, p_ref, wc_ref, x_ref, y_ref, sw_ref, sem, rows, left):
+def relayout(src, rows, left, windows):
+    frames, chans, height, cols = src.shape
+    steps = height // 4
+    zero = jnp.zeros((chans, cols), BF16)
+    rows[...] = src[...].reshape(frames * chans * height, cols).astype(F32)
+    for f in range(frames):
+        for h in range(-1, height + 1):
+            value = zero
+            if 0 <= h < height:
+                at = f * chans * height + h
+                value = rows[pl.ds(at, chans, stride=height), :].astype(BF16)
+            for i, start in enumerate(windows):
+                t, slot = (h - start) // 4, (h - start) % 4
+                if 0 <= t < steps:
+                    at = (f * steps + t) * chans
+                    left[i, at : at + chans, slot * cols : (slot + 1) * cols] = value
+
+
+def saved_kernel(x_hbm, y_hbm, sw_hbm, p_ref, x_ref, sw_ref, y_ref, sem, rows, left):
+    frames, chans, height, cols = y_ref.shape
+    steps = height // 4
     fetches = [
         pltpu.make_async_copy(src, dst, sem.at[i])
         for i, (src, dst) in enumerate(((y_hbm, y_ref), (x_hbm, x_ref), (sw_hbm, sw_ref)))
     ]
     for fetch in fetches:
         fetch.start()
-    frames, chans, height, cols = x_ref.shape
-    steps = height // 4
-    zero = jnp.zeros((chans, cols), BF16)
-    pool = one_hot_pool(4, (0, 1, 2), cols)
-
-    def place(a, f, h, value):
-        t, slot = (h - a + 1) // 4, (h - a + 1) % 4
-        if 0 <= t < steps:
-            at = (f * steps + t) * chans
-            left[a, at : at + chans, slot * cols : (slot + 1) * cols] = value
-
+    pool = one_hot_pool(4, (1,), cols)
     fetches[0].wait()
-    rows[...] = y_ref[...].reshape(frames * chans * height, cols).astype(F32)
-    for f in range(frames):
-        for h in range(height):
-            at = f * chans * height + h
-            place(1, f, h, rows[pl.ds(at, chans, stride=height), :].astype(BF16))
-    done = jnp.dot(left[1], pool[:, LANES : 2 * LANES], preferred_element_type=F32).astype(BF16)
+    relayout(y_ref, rows, left, (0,))
+    done = jnp.dot(left[0], pool, preferred_element_type=F32).astype(BF16)
     for f in range(frames):
         for t in range(steps):
             at = (f * steps + t) * chans
             p_ref[f, :, t * LANES : (t + 1) * LANES] = done[at : at + chans]
-
     fetches[1].wait()
-    rows[...] = x_ref[...].reshape(frames * chans * height, cols).astype(F32)
-    for f in range(frames):
-        for h in range(-1, height + 1):
-            if 0 <= h < height:
-                at = f * chans * height + h
-                value = rows[pl.ds(at, chans, stride=height), :].astype(BF16)
-            else:
-                value = zero
-            for a in range(3):
-                place(a, f, h, value)
+    fetches[2].wait()
+
+
+def input_kernel(x_ref, s_ref, rows, left):
+    frames, chans, height, cols = x_ref.shape
+    steps = height // 4
+    pool = one_hot_pool(4, (0, 1, 2), cols)
+    relayout(x_ref, rows, left, (-1, 0, 1))
     for a in range(3):
         done = jnp.dot(left[a], pool, preferred_element_type=F32).astype(BF16)
         for f in range(frames):
@@ -87,19 +90,18 @@
                     s_ref[f, to : to + chans, t * LANES : (t + 1) * LANES] = done[
                         at : at + chans, b * LANES : (b + 1) * LANES
                     ]
-    fetches[2].wait()
-    for b in range(3):
-        w0, w1, w2 = (sw_ref[a, b].astype(F32) for a in range(3))
-        for j, value in enumerate((w0, w0 + w1, w1 + w2, w2)):
-            wc_ref[b, j * chans : (j + 1) * chans, :] = value.astype(BF16)
 
 
 def dot_nt(a, b):
     return lax.dot_general(a, b, (((1,), (1,)), ((), ())), preferred_element_type=F32)
 
 
-def near_kernel(scale, count, *refs):
-    pieces, inner, rest = refs[:count], refs[count : 2 * count], refs[2 * count :]
+def piece_of(refs, place):
+    return refs[place[0]][...] if place[1] is None else refs[place[0]][place[1]]
+
+
+def near_kernel(scale, count, order, sent, *refs):
+    pieces, inner, rest = refs[:count], refs[count : count + sent], refs[count + sent :]
     s_ref, p_ref, tw_ref, base_ref, g_ref, part_ref, cells = rest
     side = lax.rem(lax.axis_index("frames"), 2)
     me = lax.axis_index("chan")
@@ -108,7 +110,7 @@
     for k in range(count):
         at = partner(me, k, count)
         cells[0, at] = pieces[k][...]
-        cells[1, at] = inner[k][...]
+        cells[1, at] = piece_of(inner, order[k])
     now = cells[0].reshape(channels, spots)
     near = cells[1].reshape(channels, spots)
     dot = functools.partial(jnp.dot, preferred_element_type=F32)
@@ -130,8 +132,8 @@
     part_ref[taps + 2 * side] += first
 
 
-def far_kernel(scale, count, *refs):
-    outer, rest = refs[:count], refs[count:]
+def far_kernel(scale, count, order, sent, *refs):
+    outer, rest = refs[:sent], refs[sent:]
     base_ref, part_ref, s_ref, p_ref, tw_ref, g_ref, keep_ref, send_ref, cells, part = rest
     at_frame = lax.axis_index("frames")
     side = lax.rem(at_frame, 2)
@@ -141,7 +143,7 @@
     channels = count * quarter
     inside = jnp.where((at_frame > 0) & (at_frame < last), 1.0, 0.0).astype(BF16)
     for k in range(count):
-        cells[partner(me, k, count)] = outer[k][...] * inside
+        cells[partner(me, k, count)] = piece_of(outer, order[k]) * inside
     far = cells[...].reshape(channels, spots)
     g = base_ref[...] + jnp.dot(tw_ref[2 - 2 * side], far, preferred_element_type=F32)
     g = (g * 0.125).astype(BF16)
@@ -159,33 +161,44 @@
     send_ref[...] = part[pl.ds((1 - side) * half, half)]
 
 
-def finish_kernel(mine_ref, other_ref, spatial_hbm, temporal_hbm, sem):
-    side = lax.rem(lax.axis_index("frames"), 2)
-    half = mine_ref.shape[0]
+def copy_half(low, half_ref, spatial_hbm, temporal_hbm, sem):
+    half = half_ref.shape[0]
     rest = spatial_hbm.shape[0] - half
 
-    def copy_out(low, high):
+    @pl.when(low)
+    def _():
+        copy = pltpu.make_async_copy(half_ref, spatial_hbm.at[:half], sem.at[0])
+        copy.start()
+        copy.wait()
+
+    @pl.when(jnp.logical_not(low))
+    def _():
         copies = [
-            pltpu.make_async_copy(low, spatial_hbm.at[:half], sem.at[0]),
-            pltpu.make_async_copy(high.at[:rest], spatial_hbm.at[half:], sem.at[1]),
-            pltpu.make_async_copy(high.at[rest:], temporal_hbm, sem.at[2]),
+            pltpu.make_async_copy(half_ref.at[:rest], spatial_hbm.at[half:], sem.at[0]),
+            pltpu.make_async_copy(half_ref.at[rest:], temporal_hbm, sem.at[1]),
         ]
         for copy in copies:
             copy.start()
         for copy in copies:
             copy.wait()
 
-    @pl.when(side == 0)
-    def _():
-        copy_out(mine_ref, other_ref)
-
-    @pl.when(side == 1)
-    def _():
-        copy_out(other_ref, mine_ref)
-
-
-def back_kernel(near_ref, far_ref, wc_ref, out_ref, g_ref, sums, rows):
+
+def early_kernel(mine_ref, spatial_hbm, temporal_hbm, sem):
+    side = lax.rem(lax.axis_index("frames"), 2)
+    copy_half(side == 0, mine_ref, spatial_hbm, temporal_hbm, sem)
+
+
+def finish_kernel(other_ref, spatial_in, temporal_in, spatial_hbm, temporal_hbm, sem):
+    side = lax.rem(lax.axis_index("frames"), 2)
+    copy_half(side == 1, other_ref, spatial_hbm, temporal_hbm, sem)
+
+
+def back_kernel(near_ref, far_ref, sw_ref, out_ref, g_ref, sums, rows, wc_ref):
     frames, chans, height, cols = out_ref.shape
+    for b in range(3):
+        w0, w1, w2 = (sw_ref[a, b].astype(F32) for a in range(3))
+        for j, value in enumerate((w0, w0 + w1, w1 + w2, w2)):
+            wc_ref[b, j * chans : (j + 1) * chans, :] = value.astype(BF16)
     side = lax.rem(lax.axis_index("frames"), 2)
     g_ref[1 - side] = near_ref[...]
     g_ref[side] = far_ref[...]
@@ -251,29 +264,40 @@
 def prep(inputs, saved, spatial_w):
     frames, quarter, height, cols = inputs.shape
     taps = spatial_w.shape[0] * spatial_w.shape[1]
-    channels = spatial_w.shape[3]
-    steps, spots = height // 4, height * cols // 4
-    return pl.pallas_call(
-        prep_kernel,
+    groups, spots = frames * height // 4 * quarter, height * cols // 4
+    rows = pltpu.VMEM((frames * quarter * height, cols), F32)
+    limit = pltpu.CompilerParams(vmem_limit_bytes=20 << 20)
+    held = [pltpu.with_memory_space_constraint(x, pltpu.HBM) for x in (inputs, saved, spatial_w)]
+    pooled, staged, weights = pl.pallas_call(
+        saved_kernel,
         out_shape=(
-            shape((frames, taps * quarter, spots), BF16),
             shape((frames, quarter, spots), BF16),
-            shape((3, 4 * quarter, channels), BF16),
+            shape(inputs.shape, BF16),
+            shape(spatial_w.shape, BF16),
         ),
         in_specs=[pl.BlockSpec(memory_space=pltpu.HBM)] * 3,
         out_specs=tuple(vmem(3)),
         scratch_shapes=[
             pltpu.VMEM(inputs.shape, BF16),
-            pltpu.VMEM(inputs.shape, BF16),
-            pltpu.VMEM(spatial_w.shape, BF16),
             pltpu.SemaphoreType.DMA((3,)),
-            pltpu.VMEM((frames * quarter * height, cols), F32),
-            pltpu.VMEM((3, frames * steps * quarter, 4 * cols), BF16),
+            rows,
+            pltpu.VMEM((1, groups, 4 * cols), BF16),
         ],
-        compiler_params=pltpu.CompilerParams(vmem_limit_bytes=20 << 20),
+        compiler_params=limit,
+        cost_estimate=cost(1 << 29, 4 << 20),
+        name="prep_saved",
+    )(*held)
+    sums = pl.pallas_call(
+        input_kernel,
+        out_shape=shape((frames, taps * quarter, spots), BF16),
+        in_specs=vmem(1),
+        out_specs=vmem(1)[0],
+        scratch_shapes=[rows, pltpu.VMEM((3, groups, 4 * cols), BF16)],
+        compiler_params=limit,
         cost_estimate=cost(1 << 30, 4 << 20),
-        name="prep",
-    )(inputs, saved, spatial_w)
+        name="prep_inputs",
+    )(staged)
+    return sums, pooled, weights
 
 
 def reduce_frames(keep, send):
@@ -303,19 +327,23 @@
     pieces = [cotangent[0]]
     pieces += [swap(pieces[0], "chan", k) for k in range(1, count)]
     across = [(i, (i + (1 if i % 2 else -1)) % ring) for i in range(ring)]
-    held = (pltpu.with_memory_space_constraint(x, pltpu.HBM) for x in (inputs, saved, spatial_w))
-    sums, pooled, combined = prep(*held)
-    outer = [lax.ppermute(piece, "frames", across) for piece in pieces]
-    inner = [swap(piece, "frames", 1) for piece in pieces]
+    sums, pooled, weights = prep(inputs, saved, spatial_w)
+    groups = [[k] for k in range(count)]
+    order = {k: (i, j if len(g) > 1 else None) for i, g in enumerate(groups) for j, k in enumerate(g)}
+    outer, inner = [], []
+    for group in groups:
+        value = pieces[group[0]] if len(group) == 1 else jnp.stack([pieces[k] for k in group])
+        outer.append(lax.ppermute(value, "frames", across))
+        inner.append(swap(value, "frames", 1))
 
     slices = taps + 3
     limit = pltpu.CompilerParams(vmem_limit_bytes=20 << 20)
     part_shape = shape((slices, quarter, channels), F32)
     half_shape = shape((slices // 2, quarter, channels), F32)
     base, g_near, part = pl.pallas_call(
-        functools.partial(near_kernel, scale, count),
+        functools.partial(near_kernel, scale, count, order, len(inner)),
         out_shape=(shape((channels, spots), F32), shape((channels, spots), BF16), part_shape),
-        in_specs=vmem(2 * count + 3),
+        in_specs=vmem(count + len(inner) + 3),
         out_specs=tuple(vmem(3)),
         scratch_shapes=[pltpu.VMEM((2, count, quarter, spots), BF16)],
         compiler_params=limit,
@@ -323,9 +351,9 @@
         name="near",
     )(*pieces, *inner, sums, pooled, temporal_w)
     g_far, keep, send = pl.pallas_call(
-        functools.partial(far_kernel, scale, count),
+        functools.partial(far_kernel, scale, count, order, len(outer)),
         out_shape=(shape((channels, spots), BF16), half_shape, half_shape),
-        in_specs=vmem(count + 5),
+        in_specs=vmem(len(outer) + 5),
         out_specs=tuple(vmem(3)),
         scratch_shapes=[
             pltpu.VMEM((count, quarter, spots), BF16),
@@ -345,25 +373,32 @@
             pltpu.VMEM((frames, channels, spots), BF16),
             pltpu.VMEM((height // 2, 4 * quarter, cols), F32),
             pltpu.VMEM((quarter * height, cols), F32),
+            pltpu.VMEM((3, 4 * quarter, channels), BF16),
         ],
         compiler_params=limit,
         cost_estimate=cost(3 << 30, 4 << 20),
         name="back",
-    )(g_near, g_far, combined)
-
-    spatial, temporal = pl.pallas_call(
-        finish_kernel,
+    )(g_near, g_far, weights)
+
+    mine, other = reduce_frames(keep, send)
+    sums_out = dict(
         out_shape=(
             shape((taps, quarter, channels), F32),
             shape((slices - taps, quarter, channels), F32),
         ),
-        in_specs=vmem(2),
         out_specs=(pl.BlockSpec(memory_space=pltpu.HBM),) * 2,
-        scratch_shapes=[pltpu.SemaphoreType.DMA((3,))],
+        scratch_shapes=[pltpu.SemaphoreType.DMA((2,))],
         compiler_params=limit,
         cost_estimate=cost(0, 4 << 20),
+    )
+    begun = pl.pallas_call(early_kernel, in_specs=vmem(1), name="early", **sums_out)(mine)
+    spatial, temporal = pl.pallas_call(
+        finish_kernel,
+        in_specs=vmem(1) + [pl.BlockSpec(memory_space=pltpu.HBM)] * 2,
+        input_output_aliases={1: 0, 2: 1},
         name="finish",
-    )(*reduce_frames(keep, send))
+        **sums_out,
+    )(other, *begun)
     return (input_grad, spatial.reshape(spatial_w.shape), temporal)
 
 

time: 41.6 us -> 40.6 us (0.976)
  waiting for transfers between devices: 15.7 us -> 13.8 us
  Pallas kernels: 8.62 us -> 9.31 us
    ppermute x13, waiting for transfers between devices: 12.7 us -> 10.9 us  [swap(): return lax.ppermute(value, axis, pairs)]
    pallas_call x4 -> x6, Pallas kernels: 5.49 us -> 6.17 us  [the longest x1 1.69 us: prep(): pl.pallas_call(saved_kernel, out_shape=(shape((frames, quarter, spots), B...]
  transfers between devices with their start and end apart: 17 -> 17, of which waited for: 9 -> 8; matrix products, arithmetic and copies ran while one was open for 0% -> 0% of each run, Pallas kernels for 17% -> 19%
where the time goes in v4:
time: 40.6 us; the launch traced here: 40.5 us
  starting transfers between devices  16.4 us (40%)
  waiting for transfers between devices  13.8 us (34%)
  Pallas kernels  9.31 us (23%)
  between operations  0.77 us (2%)
    ppermute x13, waiting for transfers between devices, swap(): return lax.ppermute(value, axis, pairs)  10.9 us
    ppermute x13, starting transfers between devices, swap(): return lax.ppermute(value, axis, pairs)  10.3 us
    ppermute x4, starting transfers between devices, shards(): outer.append(lax.ppermute(value, 'frames', across))  6.11 us
    pallas_call x1, Pallas kernels, shards(): pl.pallas_call(back_kernel, out_shape=shape(inputs.shape, BF16), in_specs...  3.14 us
    ppermute x4, waiting for transfers between devices, shards(): outer.append(lax.ppermute(value, 'frames', across))  2.96 us
    pallas_call x1, Pallas kernels, prep(): pl.pallas_call(saved_kernel, out_shape=(shape((frames, quarter, spots), B...  1.69 us
    pallas_call x1, Pallas kernels, prep(): pl.pallas_call(input_kernel, out_shape=shape((frames, taps * quarter, spo...  1.37 us
    pallas_call x1, Pallas kernels, shards(): pl.pallas_call(functools.partial(near_kernel, scale, count, order, len(in...  0.83 us
  transfers between devices with their start and end apart: 17, of which 8 were waited for; matrix products, arithmetic and copies ran while one was open for 0% of the time, Pallas kernels for 19%

profile of v4, /device:TPU:0, one launch (start us, length us, event | category | flops | bytes accessed | tf_op | source)
XLA Modules:
  0.0 40.5 jit_solution(10392482399707613724)
XLA Ops:
  0.6 5.1 %collective-permute-start.2 = (bf16[64,512]{1,0:T(8,128)(2,1)}, bf16[64,512]{1,0:T(8,128)(2,1)S(1)}, u32[]{:S(2)}, u32[]{:S(2)}) collective-permute-start(bf16[64,512]{1,0:T(8,128)(2,1)} %bitcast.2), channel_id=1, source_target_pairs={{0,3},{1,2},{2,1},{3,0},{4,7},{5,6},{6,5},{7,4},{8,11},{9,10},{10,... | collective-permute-start | bytes 196616 | tf_op jit(solution)/shard_map/ppermute | solution.py:245
  5.8 0.0 collective-permute-start.1
  5.8 0.6 %collective-permute-start = (bf16[64,512]{1,0:T(8,128)(2,1)}, bf16[64,512]{1,0:T(8,128)(2,1)S(1)}, u32[]{:S(2)}, u32[]{:S(2)}) collective-permute-start(bf16[64,512]{1,0:T(8,128)(2,1)} %bitcast.4), channel_id=1, source_target_pairs={{0,1},{1,0},{2,3},{3,2},{4,5},{5,4},{6,7},{7,6},{8,9},{9,8},{10,11... | collective-permute-start | bytes 196616 | tf_op jit(solution)/shard_map/ppermute | solution.py:245
  6.4 1.3 %collective-permute-start.7 = (bf16[64,512]{1,0:T(8,128)(2,1)}, bf16[64,512]{1,0:T(8,128)(2,1)S(1)}, u32[]{:S(2)}, u32[]{:S(2)}) collective-permute-start(bf16[64,512]{1,0:T(8,128)(2,1)} %bitcast.5), channel_id=1, source_target_pairs={{0,28},{4,8},{8,4},{12,16},{16,12},{20,24},{24,20},{28,0},{1,29},{... | collective-permute-start | bytes 196616 | tf_op jit(solution)/shard_map/ppermute | solution.py:336
  7.7 0.4 %collective-permute-start.3 = (bf16[64,512]{1,0:T(8,128)(2,1)}, bf16[64,512]{1,0:T(8,128)(2,1)S(1)}, u32[]{:S(2)}, u32[]{:S(2)}) collective-permute-start(bf16[64,512]{1,0:T(8,128)(2,1)} %bitcast.6), channel_id=1, source_target_pairs={{0,4},{4,0},{8,12},{12,8},{16,20},{20,16},{24,28},{28,24},{1,5},{5... | collective-permute-start | bytes 196616 | tf_op jit(solution)/shard_map/ppermute | solution.py:245
  8.2 1.7 %prep_saved.1 = (bf16[2,64,512]{2,1,0:T(8,128)(2,1)S(1)}, bf16[2,64,16,128]{3,2,1,0:T(8,128)(2,1)S(1)}, bf16[3,3,64,256]{3,2,1,0:T(8,128)(2,1)S(1)}) custom-call(bf16[2,64,16,128]{3,2,1,0:T(8,128)(2,1)} %x_hbm.1, bf16[2,64,16,128]{3,2,1,0:T(8,128)(2,1)} %y_hbm.1, bf16[3,3,64,256]{3,2,1,0:T(8,128)(2,1)} %sw_hbm.1), custom_call_target="tpu_custom_call" | custom-call | flops 536870912 | bytes 4194304 | tf_op jit(solution)/shard_map/prep_saved/pallas_call | solution.py:271
  9.9 0.0 collective-permute-done.2.refs_3_
  9.9 0.2 collective-permute-start.6
  10.0 1.6 %collective-permute-done.1.refs_2_ = bf16[64,512]{1,0:T(8,128)(2,1)S(1)} collective-permute-done((bf16[64,512]{1,0:T(8,128)(2,1)}, bf16[64,512]{1,0:T(8,128)(2,1)S(1)}, u32[]{:S(2)}, u32[]{:S(2)}) %collective-permute-start.1) | collective-permute-done | bytes 65568 | tf_op jit(solution)/shard_map/ppermute | solution.py:245
  11.6 0.0 collective-permute-start.5
  11.6 0.0 collective-permute-done.refs_1_
  11.6 0.5 %collective-permute-start.4 = (bf16[64,512]{1,0:T(8,128)(2,1)S(1)}, bf16[64,512]{1,0:T(8,128)(2,1)S(1)}, u32[]{:S(2)}, u32[]{:S(2)}) collective-permute-start(bf16[64,512]{1,0:T(8,128)(2,1)S(1)} %collective-permute-done.refs_1_), channel_id=1, source_target_pairs={{0,4},{4,0},{8,12},{12,8},{16,20},{20,16},{24,28},{28,24},{1,5},{5... | collective-permute-start | bytes 196616 | tf_op jit(solution)/shard_map/ppermute | solution.py:245
  12.1 0.0 copy-start
  12.1 0.0 copy-start.1
  12.1 1.4 %prep_inputs.1.refs_8_.refs_6_ = bf16[2,576,512]{2,1,0:T(8,128)(2,1)S(1)} custom-call(bf16[2,64,16,128]{3,2,1,0:T(8,128)(2,1)S(1)} %get-tuple-element.16.x_ref), custom_call_target="tpu_custom_call" | custom-call | flops 1073741824 | bytes 4194304 | tf_op jit(solution)/shard_map/prep_inputs/pallas_call | solution.py:290
  13.5 0.0 collective-permute-done.3.refs_4_
  13.5 2.1 %collective-permute-start.10 = (bf16[64,512]{1,0:T(8,128)(2,1)S(1)}, bf16[64,512]{1,0:T(8,128)(2,1)S(1)}, u32[]{:S(2)}, u32[]{:S(2)}) collective-permute-start(bf16[64,512]{1,0:T(8,128)(2,1)S(1)} %collective-permute-done.2.refs_3_), channel_id=1, source_target_pairs={{0,28},{4,8},{8,4},{12,16},{16,12},{20,24},{24,20},{28,0},{1,29},{... | collective-permute-start | bytes 196616 | tf_op jit(solution)/shard_map/ppermute | solution.py:336
  15.6 0.0 collective-permute-done.6.refs_7_
  15.6 0.6 %collective-permute-start.9 = (bf16[64,512]{1,0:T(8,128)(2,1)S(1)}, bf16[64,512]{1,0:T(8,128)(2,1)S(1)}, u32[]{:S(2)}, u32[]{:S(2)}) collective-permute-start(bf16[64,512]{1,0:T(8,128)(2,1)S(1)} %collective-permute-done.1.refs_2_), channel_id=1, source_target_pairs={{0,28},{4,8},{8,4},{12,16},{16,12},{20,24},{24,20},{28,0},{1,29},{... | collective-permute-start | bytes 196616 | tf_op jit(solution)/shard_map/ppermute | solution.py:336
  16.2 0.0 collective-permute-done.5.refs_6_
  16.2 2.1 %collective-permute-start.8 = (bf16[64,512]{1,0:T(8,128)(2,1)S(1)}, bf16[64,512]{1,0:T(8,128)(2,1)S(1)}, u32[]{:S(2)}, u32[]{:S(2)}) collective-permute-start(bf16[64,512]{1,0:T(8,128)(2,1)S(1)} %collective-permute-done.refs_1_), channel_id=1, source_target_pairs={{0,28},{4,8},{8,4},{12,16},{16,12},{20,24},{24,20},{28,0},{1,29},{... | collective-permute-start | bytes 196616 | tf_op jit(solution)/shard_map/ppermute | solution.py:336
  18.3 0.0 collective-permute-done.4.refs_5_
  18.3 0.0 copy-done
  18.3 0.0 copy-done.1
  18.3 0.8 %near.1 = (f32[256,512]{1,0:T(8,128)S(1)}, bf16[256,512]{1,0:T(8,128)(2,1)S(1)}, f32[12,64,256]{2,1,0:T(8,128)S(1)}) custom-call(bf16[64,512]{1,0:T(8,128)(2,1)S(1)} %bitcast.7, bf16[64,512]{1,0:T(8,128)(2,1)S(1)} %collective-permute-done.refs_1_, bf16[64,512]{1,0:T(8,128)(2,1)S(1)} %collective-permute-done.1.refs_2_, ...), custom_call_target="tpu_custom_call" | custom-call | flops 1073741824 | bytes 4194304 | tf_op jit(solution)/shard_map/near/pallas_call | solution.py:343
  19.1 0.0 collective-permute-done.7.refs_0_
  19.1 0.0 collective-permute-done.10.refs_3_
  19.2 1.8 %collective-permute-done.9.refs_2_ = bf16[64,512]{1,0:T(8,128)(2,1)S(1)} collective-permute-done((bf16[64,512]{1,0:T(8,128)(2,1)S(1)}, bf16[64,512]{1,0:T(8,128)(2,1)S(1)}, u32[]{:S(2)}, u32[]{:S(2)}) %collective-permute-start.9) | collective-permute-done | bytes 65568 | tf_op jit(solution)/shard_map/ppermute | solution.py:336
  20.9 1.2 %collective-permute-done.8.refs_1_ = bf16[64,512]{1,0:T(8,128)(2,1)S(1)} collective-permute-done((bf16[64,512]{1,0:T(8,128)(2,1)S(1)}, bf16[64,512]{1,0:T(8,128)(2,1)S(1)}, u32[]{:S(2)}, u32[]{:S(2)}) %collective-permute-start.8) | collective-permute-done | bytes 65568 | tf_op jit(solution)/shard_map/ppermute | solution.py:336
  22.1 0.7 %far.1 = (bf16[256,512]{1,0:T(8,128)(2,1)S(1)}, f32[6,64,256]{2,1,0:T(8,128)S(1)}, f32[6,64,256]{2,1,0:T(8,128)S(1)}) custom-call(bf16[64,512]{1,0:T(8,128)(2,1)S(1)} %collective-permute-done.7.refs_0_, bf16[64,512]{1,0:T(8,128)(2,1)S(1)} %collective-permute-done.8.refs_1_, bf16[64,512]{1,0:T(8,128)(2,1)S(1)} %collective-permute-done.9.refs_2_, ...), custom_call_target="tpu_custom_call" | custom-call | flops 536870912 | bytes 4194304 | tf_op jit(solution)/shard_map/far/pallas_call | solution.py:353
  22.9 0.1 collective-permute-start.11
  22.9 1.7 %collective-permute-done.11 = f32[6,64,256]{2,1,0:T(8,128)S(1)} collective-permute-done((f32[6,64,256]{2,1,0:T(8,128)S(1)}, f32[6,64,256]{2,1,0:T(8,128)S(1)}, u32[]{:S(2)}, u32[]{:S(2)}) %collective-permute-start.11) | collective-permute-done | bytes 393248 | tf_op jit(solution)/shard_map/ppermute | solution.py:245
  24.6 0.1 add_convert_fusion
  24.7 0.6 %collective-permute-start.12 = (bf16[3,64,256]{2,1,0:T(8,128)(2,1)S(1)}, bf16[3,64,256]{2,1,0:T(8,128)(2,1)S(1)}, u32[]{:S(2)}, u32[]{:S(2)}) collective-permute-start(bf16[3,64,256]{2,1,0:T(8,128)(2,1)S(1)} %get-tuple-element.31), channel_id=1, source_target_pairs={{0,8},{4,12},{8,0},{12,4},{16,24},{20,28},{24,16},{28,20},{1,9},{5... | collective-permute-start | bytes 294920 | tf_op jit(solution)/shard_map/ppermute | solution.py:245
  25.3 0.8 %collective-permute-start.14 = (bf16[3,64,256]{2,1,0:T(8,128)(2,1)S(1)}, bf16[3,64,256]{2,1,0:T(8,128)(2,1)S(1)}, u32[]{:S(2)}, u32[]{:S(2)}) collective-permute-start(bf16[3,64,256]{2,1,0:T(8,128)(2,1)S(1)} %get-tuple-element.32), channel_id=1, source_target_pairs={{0,16},{4,20},{8,24},{12,28},{16,0},{20,4},{24,8},{28,12},{1,17},{... | collective-permute-start | bytes 294920 | tf_op jit(solution)/shard_map/ppermute | solution.py:245
  26.1 3.5 %collective-permute-done.12 = bf16[3,64,256]{2,1,0:T(8,128)(2,1)S(1)} collective-permute-done((bf16[3,64,256]{2,1,0:T(8,128)(2,1)S(1)}, bf16[3,64,256]{2,1,0:T(8,128)(2,1)S(1)}, u32[]{:S(2)}, u32[]{:S(2)}) %collective-permute-start.12) | collective-permute-done | bytes 98336 | tf_op jit(solution)/shard_map/ppermute | solution.py:245
  29.6 0.5 %collective-permute-done.14 = bf16[3,64,256]{2,1,0:T(8,128)(2,1)S(1)} collective-permute-done((bf16[3,64,256]{2,1,0:T(8,128)(2,1)S(1)}, bf16[3,64,256]{2,1,0:T(8,128)(2,1)S(1)}, u32[]{:S(2)}, u32[]{:S(2)}) %collective-permute-start.14) | collective-permute-done | bytes 98336 | tf_op jit(solution)/shard_map/ppermute | solution.py:245
  30.1 0.1 add_convert_fusion.2
  30.2 0.9 %collective-permute-start.13 = (bf16[3,64,256]{2,1,0:T(8,128)(2,1)S(1)}, bf16[3,64,256]{2,1,0:T(8,128)(2,1)S(1)}, u32[]{:S(2)}, u32[]{:S(2)}) collective-permute-start(bf16[3,64,256]{2,1,0:T(8,128)(2,1)S(1)} %get-tuple-element.29), channel_id=1, source_target_pairs={{0,16},{4,20},{8,24},{12,28},{16,0},{20,4},{24,8},{28,12},{1,17},{... | collective-permute-start | bytes 294920 | tf_op jit(solution)/shard_map/ppermute | solution.py:245
  31.0 1.0 %collective-permute-start.15 = (bf16[3,64,256]{2,1,0:T(8,128)(2,1)S(1)}, bf16[3,64,256]{2,1,0:T(8,128)(2,1)S(1)}, u32[]{:S(2)}, u32[]{:S(2)}) collective-permute-start(bf16[3,64,256]{2,1,0:T(8,128)(2,1)S(1)} %get-tuple-element.30), channel_id=1, source_target_pairs={{0,8},{4,12},{8,0},{12,4},{16,24},{20,28},{24,16},{28,20},{1,9},{5... | collective-permute-start | bytes 294920 | tf_op jit(solution)/shard_map/ppermute | solution.py:245
  32.0 2.8 %collective-permute-done.13 = bf16[3,64,256]{2,1,0:T(8,128)(2,1)S(1)} collective-permute-done((bf16[3,64,256]{2,1,0:T(8,128)(2,1)S(1)}, bf16[3,64,256]{2,1,0:T(8,128)(2,1)S(1)}, u32[]{:S(2)}, u32[]{:S(2)}) %collective-permute-start.13) | collective-permute-done | bytes 98336 | tf_op jit(solution)/shard_map/ppermute | solution.py:245
  34.9 0.8 %collective-permute-done.15 = bf16[3,64,256]{2,1,0:T(8,128)(2,1)S(1)} collective-permute-done((bf16[3,64,256]{2,1,0:T(8,128)(2,1)S(1)}, bf16[3,64,256]{2,1,0:T(8,128)(2,1)S(1)}, u32[]{:S(2)}, u32[]{:S(2)}) %collective-permute-start.15) | collective-permute-done | bytes 98336 | tf_op jit(solution)/shard_map/ppermute | solution.py:245
  35.7 0.1 collective-permute-start.16
  35.8 3.1 %back.1 = bf16[2,64,16,128]{3,2,1,0:T(8,128)(2,1)} custom-call(bf16[256,512]{1,0:T(8,128)(2,1)S(1)} %get-tuple-element.18.near_ref, bf16[256,512]{1,0:T(8,128)(2,1)S(1)} %get-tuple-element.21.far_ref, bf16[3,3,64,256]{3,2,1,0:T(8,128)(2,1)S(1)} %get-tuple-element.22.sw_ref), custom_call_target="tpu_custom_call" | custom-call | flops 3221225472 | bytes 4194304 | tf_op jit(solution)/shard_map/back/pallas_call | solution.py:367
  38.9 0.8 %early.1 = (f32[9,64,256]{2,1,0:T(8,128)}, f32[3,64,256]{2,1,0:T(8,128)}) custom-call(f32[6,64,256]{2,1,0:T(8,128)S(1)} %pad_maximum_fusion.mine_ref), custom_call_target="tpu_custom_call" | custom-call | bytes 4194304 | tf_op jit(solution)/shard_map/early/pallas_call | solution.py:394
  39.7 0.0 collective-permute-done.16.other_ref
  39.7 0.8 %finish.1 = (f32[9,64,256]{2,1,0:T(8,128)}, f32[3,64,256]{2,1,0:T(8,128)}) custom-call(f32[6,64,256]{2,1,0:T(8,128)S(1)} %collective-permute-done.16.other_ref, f32[9,64,256]{2,1,0:T(8,128)} %get-tuple-element.25.spatial_in, f32[3,64,256]{2,1,0:T(8,128)} %get-tuple-element.26.temporal_in), custom_call_target="tpu_custom_call", output_to_operand_aliasing={{0}: (1, {}), {1}: (2, {})} | custom-call | bytes 4194304 | tf_op jit(solution)/shard_map/finish/pallas_call | solution.py:395
  (4 shorter events, 0.1 us)
Async XLA Ops:
  0.6 9.2 %collective-permute-start.2 = (bf16[64,512]{1,0:T(8,128)(2,1)}, bf16[64,512]{1,0:T(8,128)(2,1)S(1)}, u32[]{:S(2)}, u32[]{:S(2)}) collective-permute-start(bf16[64,512]{1,0:T(8,128)(2,1)} %bitcast.2), channel_id=1, source_target_pairs={{0,3},{1,2},{2,1},{3,0},{4,7},{5,6},{6,5},{7,4},{8,11},{9,10},{10,... | collective-permute-start | bytes 196616 | tf_op jit(solution)/shard_map/ppermute | solution.py:245
  5.8 5.8 %collective-permute-start.1 = (bf16[64,512]{1,0:T(8,128)(2,1)}, bf16[64,512]{1,0:T(8,128)(2,1)S(1)}, u32[]{:S(2)}, u32[]{:S(2)}) collective-permute-start(bf16[64,512]{1,0:T(8,128)(2,1)} %bitcast.3), channel_id=1, source_target_pairs={{0,2},{1,3},{2,0},{3,1},{4,6},{5,7},{6,4},{7,5},{8,10},{9,11},{10,... | collective-permute-start | bytes 196616 | tf_op jit(solution)/shard_map/ppermute | solution.py:245
  5.8 5.8 %collective-permute-start = (bf16[64,512]{1,0:T(8,128)(2,1)}, bf16[64,512]{1,0:T(8,128)(2,1)S(1)}, u32[]{:S(2)}, u32[]{:S(2)}) collective-permute-start(bf16[64,512]{1,0:T(8,128)(2,1)} %bitcast.4), channel_id=1, source_target_pairs={{0,1},{1,0},{2,3},{3,2},{4,5},{5,4},{6,7},{7,6},{8,9},{9,8},{10,11... | collective-permute-start | bytes 196616 | tf_op jit(solution)/shard_map/ppermute | solution.py:245
  6.4 12.7 %collective-permute-start.7 = (bf16[64,512]{1,0:T(8,128)(2,1)}, bf16[64,512]{1,0:T(8,128)(2,1)S(1)}, u32[]{:S(2)}, u32[]{:S(2)}) collective-permute-start(bf16[64,512]{1,0:T(8,128)(2,1)} %bitcast.5), channel_id=1, source_target_pairs={{0,28},{4,8},{8,4},{12,16},{16,12},{20,24},{24,20},{28,0},{1,29},{... | collective-permute-start | bytes 196616 | tf_op jit(solution)/shard_map/ppermute | solution.py:336
  7.7 5.7 %collective-permute-start.3 = (bf16[64,512]{1,0:T(8,128)(2,1)}, bf16[64,512]{1,0:T(8,128)(2,1)S(1)}, u32[]{:S(2)}, u32[]{:S(2)}) collective-permute-start(bf16[64,512]{1,0:T(8,128)(2,1)} %bitcast.6), channel_id=1, source_target_pairs={{0,4},{4,0},{8,12},{12,8},{16,20},{20,16},{24,28},{28,24},{1,5},{5... | collective-permute-start | bytes 196616 | tf_op jit(solution)/shard_map/ppermute | solution.py:245
  9.9 5.8 %collective-permute-start.6 = (bf16[64,512]{1,0:T(8,128)(2,1)S(1)}, bf16[64,512]{1,0:T(8,128)(2,1)S(1)}, u32[]{:S(2)}, u32[]{:S(2)}) collective-permute-start(bf16[64,512]{1,0:T(8,128)(2,1)S(1)} %collective-permute-done.2.refs_3_), channel_id=1, source_target_pairs={{0,4},{4,0},{8,12},{12,8},{16,20},{20,16},{24,28},{28,24},{1,5},{5... | collective-permute-start | bytes 196616 | tf_op jit(solution)/shard_map/ppermute | solution.py:245
  11.6 4.6 %collective-permute-start.5 = (bf16[64,512]{1,0:T(8,128)(2,1)S(1)}, bf16[64,512]{1,0:T(8,128)(2,1)S(1)}, u32[]{:S(2)}, u32[]{:S(2)}) collective-permute-start(bf16[64,512]{1,0:T(8,128)(2,1)S(1)} %collective-permute-done.1.refs_2_), channel_id=1, source_target_pairs={{0,4},{4,0},{8,12},{12,8},{16,20},{20,16},{24,28},{28,24},{1,5},{5... | collective-permute-start | bytes 196616 | tf_op jit(solution)/shard_map/ppermute | solution.py:245
  11.6 6.7 %collective-permute-start.4 = (bf16[64,512]{1,0:T(8,128)(2,1)S(1)}, bf16[64,512]{1,0:T(8,128)(2,1)S(1)}, u32[]{:S(2)}, u32[]{:S(2)}) collective-permute-start(bf16[64,512]{1,0:T(8,128)(2,1)S(1)} %collective-permute-done.refs_1_), channel_id=1, source_target_pairs={{0,4},{4,0},{8,12},{12,8},{16,20},{20,16},{24,28},{28,24},{1,5},{5... | collective-permute-start | bytes 196616 | tf_op jit(solution)/shard_map/ppermute | solution.py:245
  12.1 6.2 %copy-start = (bf16[3,256,256]{2,1,0:T(8,128)(2,1)S(1)}, bf16[3,256,256]{2,1,0:T(8,128)(2,1)}, u32[]{:S(2)}) copy-start(bf16[3,256,256]{2,1,0:T(8,128)(2,1)} %refs_8_.1) | copy-start | bytes 1179652
  12.1 6.2 %copy-start.1 = (bf16[1,64,512]{2,1,0:T(8,128)(2,1)S(1)}, bf16[1,64,512]{2,1,0:T(8,128)(2,1)}, u32[]{:S(2)}) copy-start(bf16[1,64,512]{2,1,0:T(8,128)(2,1)} %param.7) | copy-start | bytes 196612
  13.5 5.7 %collective-permute-start.10 = (bf16[64,512]{1,0:T(8,128)(2,1)S(1)}, bf16[64,512]{1,0:T(8,128)(2,1)S(1)}, u32[]{:S(2)}, u32[]{:S(2)}) collective-permute-start(bf16[64,512]{1,0:T(8,128)(2,1)S(1)} %collective-permute-done.2.refs_3_), channel_id=1, source_target_pairs={{0,28},{4,8},{8,4},{12,16},{16,12},{20,24},{24,20},{28,0},{1,29},{... | collective-permute-start | bytes 196616 | tf_op jit(solution)/shard_map/ppermute | solution.py:336
  15.6 5.3 %collective-permute-start.9 = (bf16[64,512]{1,0:T(8,128)(2,1)S(1)}, bf16[64,512]{1,0:T(8,128)(2,1)S(1)}, u32[]{:S(2)}, u32[]{:S(2)}) collective-permute-start(bf16[64,512]{1,0:T(8,128)(2,1)S(1)} %collective-permute-done.1.refs_2_), channel_id=1, source_target_pairs={{0,28},{4,8},{8,4},{12,16},{16,12},{20,24},{24,20},{28,0},{1,29},{... | collective-permute-start | bytes 196616 | tf_op jit(solution)/shard_map/ppermute | solution.py:336
  16.2 5.9 %collective-permute-start.8 = (bf16[64,512]{1,0:T(8,128)(2,1)S(1)}, bf16[64,512]{1,0:T(8,128)(2,1)S(1)}, u32[]{:S(2)}, u32[]{:S(2)}) collective-permute-start(bf16[64,512]{1,0:T(8,128)(2,1)S(1)} %collective-permute-done.refs_1_), channel_id=1, source_target_pairs={{0,28},{4,8},{8,4},{12,16},{16,12},{20,24},{24,20},{28,0},{1,29},{... | collective-permute-start | bytes 196616 | tf_op jit(solution)/shard_map/ppermute | solution.py:336
  22.9 1.8 %collective-permute-start.11 = (f32[6,64,256]{2,1,0:T(8,128)S(1)}, f32[6,64,256]{2,1,0:T(8,128)S(1)}, u32[]{:S(2)}, u32[]{:S(2)}) collective-permute-start(f32[6,64,256]{2,1,0:T(8,128)S(1)} %get-tuple-element.24), channel_id=1, source_target_pairs={{0,4},{4,0},{8,12},{12,8},{16,20},{20,16},{24,28},{28,24},{1,5},{5... | collective-permute-start | bytes 1179656 | tf_op jit(solution)/shard_map/ppermute | solution.py:245
  24.7 4.9 %collective-permute-start.12 = (bf16[3,64,256]{2,1,0:T(8,128)(2,1)S(1)}, bf16[3,64,256]{2,1,0:T(8,128)(2,1)S(1)}, u32[]{:S(2)}, u32[]{:S(2)}) collective-permute-start(bf16[3,64,256]{2,1,0:T(8,128)(2,1)S(1)} %get-tuple-element.31), channel_id=1, source_target_pairs={{0,8},{4,12},{8,0},{12,4},{16,24},{20,28},{24,16},{28,20},{1,9},{5... | collective-permute-start | bytes 294920 | tf_op jit(solution)/shard_map/ppermute | solution.py:245
  25.3 4.8 %collective-permute-start.14 = (bf16[3,64,256]{2,1,0:T(8,128)(2,1)S(1)}, bf16[3,64,256]{2,1,0:T(8,128)(2,1)S(1)}, u32[]{:S(2)}, u32[]{:S(2)}) collective-permute-start(bf16[3,64,256]{2,1,0:T(8,128)(2,1)S(1)} %get-tuple-element.32), channel_id=1, source_target_pairs={{0,16},{4,20},{8,24},{12,28},{16,0},{20,4},{24,8},{28,12},{1,17},{... | collective-permute-start | bytes 294920 | tf_op jit(solution)/shard_map/ppermute | solution.py:245
  30.2 4.7 %collective-permute-start.13 = (bf16[3,64,256]{2,1,0:T(8,128)(2,1)S(1)}, bf16[3,64,256]{2,1,0:T(8,128)(2,1)S(1)}, u32[]{:S(2)}, u32[]{:S(2)}) collective-permute-start(bf16[3,64,256]{2,1,0:T(8,128)(2,1)S(1)} %get-tuple-element.29), channel_id=1, source_target_pairs={{0,16},{4,20},{8,24},{12,28},{16,0},{20,4},{24,8},{28,12},{1,17},{... | collective-permute-start | bytes 294920 | tf_op jit(solution)/shard_map/ppermute | solution.py:245
  31.0 4.6 %collective-permute-start.15 = (bf16[3,64,256]{2,1,0:T(8,128)(2,1)S(1)}, bf16[3,64,256]{2,1,0:T(8,128)(2,1)S(1)}, u32[]{:S(2)}, u32[]{:S(2)}) collective-permute-start(bf16[3,64,256]{2,1,0:T(8,128)(2,1)S(1)} %get-tuple-element.30), channel_id=1, source_target_pairs={{0,8},{4,12},{8,0},{12,4},{16,24},{20,28},{24,16},{28,20},{1,9},{5... | collective-permute-start | bytes 294920 | tf_op jit(solution)/shard_map/ppermute | solution.py:245
  35.7 4.0 %collective-permute-start.16 = (f32[6,64,256]{2,1,0:T(8,128)S(1)}, f32[6,64,256]{2,1,0:T(8,128)S(1)}, u32[]{:S(2)}, u32[]{:S(2)}) collective-permute-start(f32[6,64,256]{2,1,0:T(8,128)S(1)} %pad_maximum_fusion.mine_ref), channel_id=1, source_target_pairs={{0,4},{4,0},{8,12},{12,8},{16,20},{20,16},{24,28},{28,24},{1,5},{5... | collective-permute-start | bytes 1179656 | tf_op jit(solution)/shard_map/ppermute | solution.py:245

commit v5 on v4

--- a/solution.py
+++ b/solution.py
@@ -132,102 +132,141 @@
     part_ref[taps + 2 * side] += first
 
 
+def add_half(low, a_ref, b_ref, scale, part_ref, s_ref, p_ref, g, far):
+    side = lax.rem(lax.axis_index("frames"), 2)
+    cut, quarter, channels = a_ref.shape
+    half = cut + b_ref.shape[0]
+    edge = half * quarter
+    taps = s_ref.shape[1] // quarter
+    rows = s_ref[side, :edge] if low else s_ref[side, edge:]
+    spatial = (dot_nt(rows, g) * scale).reshape(-1, quarter, channels)
+    first = 0 if low else half
+    a_ref[...] = part_ref[first : first + cut] + spatial[:cut]
+    if low:
+        b_ref[...] = part_ref[cut:half] + spatial[cut:]
+        return
+    e_far = dot_nt(p_ref[...].reshape(2 * quarter, far.shape[1]), far) * (scale * 0.125)
+    b_ref[...] = part_ref[taps:]
+    b_ref[2 - 2 * side] += jnp.where(side == 0, e_far[:quarter], e_far[quarter:])
+
+
 def far_kernel(scale, count, order, sent, *refs):
     outer, rest = refs[:sent], refs[sent:]
-    base_ref, part_ref, s_ref, p_ref, tw_ref, g_ref, keep_ref, send_ref, cells, part = rest
+    base_ref, part_ref, s_ref, p_ref, tw_ref, g_ref, send_a, send_b, cells_ref = rest
     at_frame = lax.axis_index("frames")
     side = lax.rem(at_frame, 2)
     me = lax.axis_index("chan")
     last = lax.axis_size("frames") - 1
     quarter, spots = outer[0].shape
-    channels = count * quarter
     inside = jnp.where((at_frame > 0) & (at_frame < last), 1.0, 0.0).astype(BF16)
     for k in range(count):
-        cells[partner(me, k, count)] = piece_of(outer, order[k]) * inside
-    far = cells[...].reshape(channels, spots)
+        cells_ref[partner(me, k, count)] = piece_of(outer, order[k]) * inside
+    far = cells_ref[...].reshape(count * quarter, spots)
     g = base_ref[...] + jnp.dot(tw_ref[2 - 2 * side], far, preferred_element_type=F32)
     g = (g * 0.125).astype(BF16)
     g_ref[...] = g
-    e_far = dot_nt(p_ref[...].reshape(2 * quarter, spots), far)
-    taps = s_ref.shape[1] // quarter
-    spatial = (dot_nt(s_ref[side], g) * scale).reshape(taps, quarter, channels)
-    part[:taps] = part_ref[:taps] + spatial
-    part[taps:] = part_ref[taps:]
-    part[taps + 2 - 2 * side] += jnp.where(side == 0, e_far[:quarter], e_far[quarter:]) * (
-        scale * 0.125
-    )
-    half = part.shape[0] // 2
-    keep_ref[...] = part[pl.ds(side * half, half)]
-    send_ref[...] = part[pl.ds((1 - side) * half, half)]
-
-
-def copy_half(low, half_ref, spatial_hbm, temporal_hbm, sem):
-    half = half_ref.shape[0]
-    rest = spatial_hbm.shape[0] - half
-
-    @pl.when(low)
-    def _():
-        copy = pltpu.make_async_copy(half_ref, spatial_hbm.at[:half], sem.at[0])
-        copy.start()
-        copy.wait()
-
-    @pl.when(jnp.logical_not(low))
-    def _():
-        copies = [
-            pltpu.make_async_copy(half_ref.at[:rest], spatial_hbm.at[half:], sem.at[0]),
-            pltpu.make_async_copy(half_ref.at[rest:], temporal_hbm, sem.at[1]),
-        ]
+    for low in (True, False):
+
+        @pl.when(side == int(low))
+        def _(low=low):
+            add_half(low, send_a, send_b, scale, part_ref, s_ref, p_ref, g_ref[...], far)
+
+
+def keep_kernel(scale, part_ref, s_ref, p_ref, g_ref, cells_ref, keep_a, keep_b):
+    side = lax.rem(lax.axis_index("frames"), 2)
+    count, quarter, spots = cells_ref.shape
+    for low in (True, False):
+
+        @pl.when(side == 1 - int(low))
+        def _(low=low):
+            far = cells_ref[...].reshape(count * quarter, spots)
+            add_half(low, keep_a, keep_b, scale, part_ref, s_ref, p_ref, g_ref[...], far)
+
+
+def early_kernel(a_ref, b_ref, other_a, spatial_hbm, temporal_hbm, sem):
+    side = lax.rem(lax.axis_index("frames"), 2)
+    cut, half = a_ref.shape[0], a_ref.shape[0] + b_ref.shape[0]
+
+    def copy_out(*moves):
+        copies = [pltpu.make_async_copy(*move, sem.at[i]) for i, move in enumerate(moves)]
         for copy in copies:
             copy.start()
         for copy in copies:
             copy.wait()
 
-
-def early_kernel(mine_ref, spatial_hbm, temporal_hbm, sem):
-    side = lax.rem(lax.axis_index("frames"), 2)
-    copy_half(side == 0, mine_ref, spatial_hbm, temporal_hbm, sem)
-
-
-def finish_kernel(other_ref, spatial_in, temporal_in, spatial_hbm, temporal_hbm, sem):
-    side = lax.rem(lax.axis_index("frames"), 2)
-    copy_half(side == 1, other_ref, spatial_hbm, temporal_hbm, sem)
-
-
-def back_kernel(near_ref, far_ref, sw_ref, out_ref, g_ref, sums, rows, wc_ref):
-    frames, chans, height, cols = out_ref.shape
+    low, high = spatial_hbm.at[:cut], spatial_hbm.at[half:]
+
+    @pl.when(side == 0)
+    def _():
+        copy_out((a_ref, low), (b_ref, spatial_hbm.at[cut:half]), (other_a, high))
+
+    @pl.when(side == 1)
+    def _():
+        copy_out((a_ref, high), (b_ref, temporal_hbm), (other_a, low))
+
+
+def finish_kernel(b_ref, spatial_in, temporal_in, spatial_hbm, temporal_hbm, sem):
+    side = lax.rem(lax.axis_index("frames"), 2)
+    rest = b_ref.shape[0]
+    cut = spatial_hbm.shape[0] - 2 * rest
+
+    def copy_out(to):
+        copy = pltpu.make_async_copy(b_ref, to, sem.at[0])
+        copy.start()
+        copy.wait()
+
+    @pl.when(side == 0)
+    def _():
+        copy_out(temporal_hbm)
+
+    @pl.when(side == 1)
+    def _():
+        copy_out(spatial_hbm.at[cut : cut + rest])
+
+
+def back_frame(g_ref, wc_ref, out_hbm, frame, sums, rows, staged, sem):
+    chans, height, cols = staged.shape
+    spread = one_hot_spread(cols)
+    pooled = height // 2
+    for t in range(height // 4):
+        wide = jnp.dot(
+            g_ref[:, t * LANES : (t + 1) * LANES], spread, preferred_element_type=F32
+        ).astype(BF16)
+        total = jnp.dot(wc_ref[0], wide[:, : 2 * cols], preferred_element_type=F32)
+        for b in (1, 2):
+            total = total + jnp.dot(
+                wc_ref[b], wide[:, b * 2 * cols : (b + 1) * 2 * cols], preferred_element_type=F32
+            )
+        sums[2 * t] = total[:, :cols]
+        sums[2 * t + 1] = total[:, cols:]
+    for p in range(pooled):
+        even = sums[p, chans : 2 * chans, :]
+        if p > 0:
+            even = even + sums[p - 1, 3 * chans :, :]
+        odd = sums[p, 2 * chans : 3 * chans, :]
+        if p < pooled - 1:
+            odd = odd + sums[p + 1, :chans, :]
+        rows[pl.ds(2 * p, chans, stride=height), :] = even
+        rows[pl.ds(2 * p + 1, chans, stride=height), :] = odd
+    staged[...] = rows[...].reshape(chans, height, cols).astype(BF16)
+    copy = pltpu.make_async_copy(staged, out_hbm.at[frame], sem)
+    copy.start()
+    copy.wait()
+
+
+def back_near_kernel(g_ref, sw_ref, out_hbm, wc_ref, *scratch):
+    chans = sw_ref.shape[2]
     for b in range(3):
         w0, w1, w2 = (sw_ref[a, b].astype(F32) for a in range(3))
         for j, value in enumerate((w0, w0 + w1, w1 + w2, w2)):
             wc_ref[b, j * chans : (j + 1) * chans, :] = value.astype(BF16)
     side = lax.rem(lax.axis_index("frames"), 2)
-    g_ref[1 - side] = near_ref[...]
-    g_ref[side] = far_ref[...]
-    spread = one_hot_spread(cols)
-    pooled = height // 2
-    for f in range(frames):
-        for t in range(height // 4):
-            wide = jnp.dot(
-                g_ref[f, :, t * LANES : (t + 1) * LANES], spread, preferred_element_type=F32
-            ).astype(BF16)
-            total = jnp.dot(wc_ref[0], wide[:, : 2 * cols], preferred_element_type=F32)
-            for b in (1, 2):
-                total = total + jnp.dot(
-                    wc_ref[b],
-                    wide[:, b * 2 * cols : (b + 1) * 2 * cols],
-                    preferred_element_type=F32,
-                )
-            sums[2 * t] = total[:, :cols]
-            sums[2 * t + 1] = total[:, cols:]
-        for p in range(pooled):
-            even = sums[p, chans : 2 * chans, :]
-            if p > 0:
-                even = even + sums[p - 1, 3 * chans :, :]
-            odd = sums[p, 2 * chans : 3 * chans, :]
-            if p < pooled - 1:
-                odd = odd + sums[p + 1, :chans, :]
-            rows[pl.ds(2 * p, chans, stride=height), :] = even
-            rows[pl.ds(2 * p + 1, chans, stride=height), :] = odd
-        out_ref[f] = rows[...].reshape(chans, height, cols).astype(BF16)
+    back_frame(g_ref, wc_ref, out_hbm, 1 - side, *scratch)
+
+
+def back_far_kernel(g_ref, wc_ref, out_in, out_hbm, *scratch):
+    side = lax.rem(lax.axis_index("frames"), 2)
+    back_frame(g_ref, wc_ref, out_hbm, side, *scratch)
 
 
 def partner(me, k, count):
@@ -300,19 +339,25 @@
     return sums, pooled, weights
 
 
+def apart(value, other):
+    return lax.optimization_barrier((value, other))[0]
+
+
 def reduce_frames(keep, send):
     count = lax.axis_size("frames")
-    total = keep + swap(send, "frames", 1)
     bits = [1 << i for i in range(1, count.bit_length() - 1)]
-    cut = total.shape[0] // 2
-    a, b = total[:cut], total[cut:]
+    a, b = keep
+    moved_a = swap(send[0], "frames", 1)
+    moved_b = swap(send[1], "frames", 1)
     for first, second in zip(bits, bits[::-1]):
-        a, b = a.astype(BF16), b.astype(BF16)
+        a = both(a, moved_a).astype(BF16)
+        b = both(b, apart(moved_b, a)).astype(BF16)
         moved_a = swap(a, "frames", first)
         moved_b = swap(b, "frames", second)
-        a, b = both(a, moved_a), both(b, moved_b)
-    mine = jnp.concatenate([a, b])
-    return mine, swap(mine, "frames", 1)
+    a = both(a, moved_a)
+    b = both(b, apart(moved_b, a))
+    others = (swap(a, "frames", 1), swap(b, "frames", 1))
+    return (a, b), others
 
 
 def shards(inputs, saved, cotangent, spatial_w, temporal_w):
@@ -339,7 +384,7 @@
     slices = taps + 3
     limit = pltpu.CompilerParams(vmem_limit_bytes=20 << 20)
     part_shape = shape((slices, quarter, channels), F32)
-    half_shape = shape((slices // 2, quarter, channels), F32)
+    half_shapes = [shape((n, quarter, channels), F32) for n in (taps - slices // 2, slices - taps)]
     base, g_near, part = pl.pallas_call(
         functools.partial(near_kernel, scale, count, order, len(inner)),
         out_shape=(shape((channels, spots), F32), shape((channels, spots), BF16), part_shape),
@@ -350,55 +395,77 @@
         cost_estimate=cost(1 << 30, 4 << 20),
         name="near",
     )(*pieces, *inner, sums, pooled, temporal_w)
-    g_far, keep, send = pl.pallas_call(
+    g_far, send_a, send_b, cells = pl.pallas_call(
         functools.partial(far_kernel, scale, count, order, len(outer)),
-        out_shape=(shape((channels, spots), BF16), half_shape, half_shape),
+        out_shape=(
+            shape((channels, spots), BF16),
+            *half_shapes,
+            shape((count, quarter, spots), BF16),
+        ),
         in_specs=vmem(len(outer) + 5),
-        out_specs=tuple(vmem(3)),
-        scratch_shapes=[
-            pltpu.VMEM((count, quarter, spots), BF16),
-            pltpu.VMEM(part_shape.shape, F32),
-        ],
+        out_specs=tuple(vmem(4)),
         compiler_params=limit,
         cost_estimate=cost(1 << 29, 4 << 20),
         name="far",
     )(*outer, base, part, sums, pooled, temporal_w)
-
-    input_grad = pl.pallas_call(
-        back_kernel,
-        out_shape=shape(inputs.shape, BF16),
-        in_specs=vmem(3),
-        out_specs=vmem(1)[0],
+    keep = pl.pallas_call(
+        functools.partial(keep_kernel, scale),
+        out_shape=tuple(half_shapes),
+        in_specs=vmem(5),
+        out_specs=tuple(vmem(2)),
+        compiler_params=limit,
+        cost_estimate=cost(1 << 28, 4 << 20),
+        name="keep",
+    )(part, sums, pooled, g_far, cells)
+
+    hbm = pl.BlockSpec(memory_space=pltpu.HBM)
+    back = dict(
         scratch_shapes=[
-            pltpu.VMEM((frames, channels, spots), BF16),
             pltpu.VMEM((height // 2, 4 * quarter, cols), F32),
             pltpu.VMEM((quarter * height, cols), F32),
-            pltpu.VMEM((3, 4 * quarter, channels), BF16),
+            pltpu.VMEM((quarter, height, cols), BF16),
+            pltpu.SemaphoreType.DMA,
         ],
         compiler_params=limit,
-        cost_estimate=cost(3 << 30, 4 << 20),
-        name="back",
-    )(g_near, g_far, weights)
-
-    mine, other = reduce_frames(keep, send)
+        cost_estimate=cost(3 << 29, 2 << 20),
+    )
+    input_grad, combined = pl.pallas_call(
+        back_near_kernel,
+        out_shape=(shape(inputs.shape, BF16), shape((3, 4 * quarter, channels), BF16)),
+        in_specs=vmem(2),
+        out_specs=(hbm, *vmem(1)),
+        name="back_near",
+        **back,
+    )(g_near, weights)
+    input_grad = pl.pallas_call(
+        back_far_kernel,
+        out_shape=shape(inputs.shape, BF16),
+        in_specs=[*vmem(2), hbm],
+        out_specs=hbm,
+        input_output_aliases={2: 0},
+        name="back_far",
+        **back,
+    )(g_far, combined, input_grad)
+
+    mine, other = reduce_frames(keep, (send_a, send_b))
     sums_out = dict(
         out_shape=(
             shape((taps, quarter, channels), F32),
             shape((slices - taps, quarter, channels), F32),
         ),
         out_specs=(pl.BlockSpec(memory_space=pltpu.HBM),) * 2,
-        scratch_shapes=[pltpu.SemaphoreType.DMA((2,))],
+        scratch_shapes=[pltpu.SemaphoreType.DMA((3,))],
         compiler_params=limit,
         cost_estimate=cost(0, 4 << 20),
     )
-    begun = pl.pallas_call(early_kernel, in_specs=vmem(1), name="early", **sums_out)(mine)
+    begun = pl.pallas_call(early_kernel, in_specs=vmem(3), name="early", **sums_out)(*mine, other[0])
     spatial, temporal = pl.pallas_call(
         finish_kernel,
         in_specs=vmem(1) + [pl.BlockSpec(memory_space=pltpu.HBM)] * 2,
         input_output_aliases={1: 0, 2: 1},
         name="finish",
         **sums_out,
-    )(other, *begun)
+    )(other[1], *begun)
     return (input_grad, spatial.reshape(spatial_w.shape), temporal)
 
 

time: 40.6 us -> 40.6 us (level)
  waiting for transfers between devices: 13.8 us -> 10.9 us
  starting transfers between devices: 16.4 us -> 18 us
  Pallas kernels: 9.31 us -> 10.6 us
    ppermute x13 -> x15, waiting for transfers between devices: 10.9 us -> 7.92 us  [swap(): return lax.ppermute(value, axis, pairs)]
    pallas_call x2 -> x4, Pallas kernels: 3.9 us -> 5.39 us  [the longest x1 2.12 us: shards(): pl.pallas_call(back_far_kernel, out_shape=shape(inputs.shape, BF16), in_s...]
    ppermute x4, starting transfers between devices: 6.11 us -> 7.48 us  [shards(): outer.append(lax.ppermute(value, 'frames', across))]
    ppermute x13 -> x15, starting transfers between devices: 10.3 us -> 10.5 us  [swap(): return lax.ppermute(value, axis, pairs)]
  transfers between devices with their start and end apart: 17 -> 19, of which waited for: 8 -> 7; matrix products, arithmetic and copies ran while one was open for 0% -> 0% of each run, Pallas kernels for 19% -> 23%
where the time goes in v5:
time: 40.6 us; the launch traced here: 40.4 us
  starting transfers between devices  18 us (44%)
  waiting for transfers between devices  10.9 us (27%)
  Pallas kernels  10.6 us (26%)
  between operations  0.81 us (2%)
    ppermute x15, starting transfers between devices, swap(): return lax.ppermute(value, axis, pairs)  10.5 us
    ppermute x15, waiting for transfers between devices, swap(): return lax.ppermute(value, axis, pairs)  7.92 us
    ppermute x4, starting transfers between devices, shards(): outer.append(lax.ppermute(value, 'frames', across))  7.48 us
    ppermute x4, waiting for transfers between devices, shards(): outer.append(lax.ppermute(value, 'frames', across))  2.96 us
    pallas_call x1, Pallas kernels, shards(): pl.pallas_call(back_far_kernel, out_shape=shape(inputs.shape, BF16), in_s...  2.12 us
    pallas_call x1, Pallas kernels, shards(): pl.pallas_call(back_near_kernel, out_shape=(shape(inputs.shape, BF16), sh...  2.12 us
    pallas_call x1, Pallas kernels, prep(): pl.pallas_call(saved_kernel, out_shape=(shape((frames, quarter, spots), B...  1.69 us
    pallas_call x1, Pallas kernels, prep(): pl.pallas_call(input_kernel, out_shape=shape((frames, taps * quarter, spo...  1.37 us
  transfers between devices with their start and end apart: 19, of which 7 were waited for; matrix products, arithmetic and copies ran while one was open for 0% of the time, Pallas kernels for 23%

profile of v5, /device:TPU:0, one launch (start us, length us, event | category | flops | bytes accessed | tf_op | source)
XLA Modules:
  0.0 40.4 jit_solution(16384055285282548024)
XLA Ops:
  0.6 5.1 %collective-permute-start.5 = (bf16[64,512]{1,0:T(8,128)(2,1)}, bf16[64,512]{1,0:T(8,128)(2,1)S(1)}, u32[]{:S(2)}, u32[]{:S(2)}) collective-permute-start(bf16[64,512]{1,0:T(8,128)(2,1)} %bitcast.2), channel_id=1, source_target_pairs={{0,3},{1,2},{2,1},{3,0},{4,7},{5,6},{6,5},{7,4},{8,11},{9,10},{10,... | collective-permute-start | bytes 196616 | tf_op jit(solution)/shard_map/ppermute | solution.py:284
  5.8 0.0 collective-permute-start.3
  5.8 0.6 %collective-permute-start.1 = (bf16[64,512]{1,0:T(8,128)(2,1)}, bf16[64,512]{1,0:T(8,128)(2,1)S(1)}, u32[]{:S(2)}, u32[]{:S(2)}) collective-permute-start(bf16[64,512]{1,0:T(8,128)(2,1)} %bitcast.4), channel_id=1, source_target_pairs={{0,1},{1,0},{2,3},{3,2},{4,5},{5,4},{6,7},{7,6},{8,9},{9,8},{10,11... | collective-permute-start | bytes 196616 | tf_op jit(solution)/shard_map/ppermute | solution.py:284
  6.4 0.0 collective-permute-start.7
  6.4 2.7 %collective-permute-start = (bf16[64,512]{1,0:T(8,128)(2,1)}, bf16[64,512]{1,0:T(8,128)(2,1)S(1)}, u32[]{:S(2)}, u32[]{:S(2)}) collective-permute-start(bf16[64,512]{1,0:T(8,128)(2,1)} %bitcast.6), channel_id=1, source_target_pairs={{0,28},{4,8},{8,4},{12,16},{16,12},{20,24},{24,20},{28,0},{1,29},{... | collective-permute-start | bytes 196616 | tf_op jit(solution)/shard_map/ppermute | solution.py:381
  9.1 1.7 %prep_saved.1 = (bf16[2,64,512]{2,1,0:T(8,128)(2,1)S(1)}, bf16[2,64,16,128]{3,2,1,0:T(8,128)(2,1)S(1)}, bf16[3,3,64,256]{3,2,1,0:T(8,128)(2,1)S(1)}) custom-call(bf16[2,64,16,128]{3,2,1,0:T(8,128)(2,1)} %x_hbm.1, bf16[2,64,16,128]{3,2,1,0:T(8,128)(2,1)} %y_hbm.1, bf16[3,3,64,256]{3,2,1,0:T(8,128)(2,1)} %sw_hbm.1), custom_call_target="tpu_custom_call" | custom-call | flops 536870912 | bytes 4194304 | tf_op jit(solution)/shard_map/prep_saved/pallas_call | solution.py:310
  10.8 0.0 collective-permute-done.5.refs_3_
  10.8 0.1 collective-permute-start.10
  10.9 0.7 %collective-permute-done.3.refs_2_ = bf16[64,512]{1,0:T(8,128)(2,1)S(1)} collective-permute-done((bf16[64,512]{1,0:T(8,128)(2,1)}, bf16[64,512]{1,0:T(8,128)(2,1)S(1)}, u32[]{:S(2)}, u32[]{:S(2)}) %collective-permute-start.3) | collective-permute-done | bytes 65568 | tf_op jit(solution)/shard_map/ppermute | solution.py:284
  11.6 0.0 collective-permute-start.9
  11.6 0.0 collective-permute-done.1.refs_1_
  11.6 0.5 %collective-permute-start.8 = (bf16[64,512]{1,0:T(8,128)(2,1)S(1)}, bf16[64,512]{1,0:T(8,128)(2,1)S(1)}, u32[]{:S(2)}, u32[]{:S(2)}) collective-permute-start(bf16[64,512]{1,0:T(8,128)(2,1)S(1)} %collective-permute-done.1.refs_1_), channel_id=1, source_target_pairs={{0,4},{4,0},{8,12},{12,8},{16,20},{20,16},{24,28},{28,24},{1,5},{5... | collective-permute-start | bytes 196616 | tf_op jit(solution)/shard_map/ppermute | solution.py:284
  12.1 1.4 %prep_inputs.1.refs_8_.refs_6_.s_ref = bf16[2,576,512]{2,1,0:T(8,128)(2,1)S(1)} custom-call(bf16[2,64,16,128]{3,2,1,0:T(8,128)(2,1)S(1)} %get-tuple-element.24.x_ref), custom_call_target="tpu_custom_call" | custom-call | flops 1073741824 | bytes 4194304 | tf_op jit(solution)/shard_map/prep_inputs/pallas_call | solution.py:329
  13.5 0.0 collective-permute-done.7.refs_4_
  13.5 2.1 %collective-permute-start.6 = (bf16[64,512]{1,0:T(8,128)(2,1)S(1)}, bf16[64,512]{1,0:T(8,128)(2,1)S(1)}, u32[]{:S(2)}, u32[]{:S(2)}) collective-permute-start(bf16[64,512]{1,0:T(8,128)(2,1)S(1)} %collective-permute-done.5.refs_3_), channel_id=1, source_target_pairs={{0,28},{4,8},{8,4},{12,16},{16,12},{20,24},{24,20},{28,0},{1,29},{... | collective-permute-start | bytes 196616 | tf_op jit(solution)/shard_map/ppermute | solution.py:381
  15.6 0.0 collective-permute-done.10.refs_7_
  15.6 0.6 %collective-permute-start.4 = (bf16[64,512]{1,0:T(8,128)(2,1)S(1)}, bf16[64,512]{1,0:T(8,128)(2,1)S(1)}, u32[]{:S(2)}, u32[]{:S(2)}) collective-permute-start(bf16[64,512]{1,0:T(8,128)(2,1)S(1)} %collective-permute-done.3.refs_2_), channel_id=1, source_target_pairs={{0,28},{4,8},{8,4},{12,16},{16,12},{20,24},{24,20},{28,0},{1,29},{... | collective-permute-start | bytes 196616 | tf_op jit(solution)/shard_map/ppermute | solution.py:381
  16.2 0.0 collective-permute-done.9.refs_6_
  16.2 2.1 %collective-permute-start.2 = (bf16[64,512]{1,0:T(8,128)(2,1)S(1)}, bf16[64,512]{1,0:T(8,128)(2,1)S(1)}, u32[]{:S(2)}, u32[]{:S(2)}) collective-permute-start(bf16[64,512]{1,0:T(8,128)(2,1)S(1)} %collective-permute-done.1.refs_1_), channel_id=1, source_target_pairs={{0,28},{4,8},{8,4},{12,16},{16,12},{20,24},{24,20},{28,0},{1,29},{... | collective-permute-start | bytes 196616 | tf_op jit(solution)/shard_map/ppermute | solution.py:381
  18.3 0.0 collective-permute-done.8.refs_5_
  18.3 0.0 copy-done.1
  18.3 0.8 %near.1 = (f32[256,512]{1,0:T(8,128)S(1)}, bf16[256,512]{1,0:T(8,128)(2,1)S(1)}, f32[12,64,256]{2,1,0:T(8,128)S(1)}) custom-call(bf16[64,512]{1,0:T(8,128)(2,1)S(1)} %bitcast.7, bf16[64,512]{1,0:T(8,128)(2,1)S(1)} %collective-permute-done.1.refs_1_, bf16[64,512]{1,0:T(8,128)(2,1)S(1)} %collective-permute-done.3.refs_2_, ...), custom_call_target="tpu_custom_call" | custom-call | flops 1073741824 | bytes 4194304 | tf_op jit(solution)/shard_map/near/pallas_call | solution.py:388
  19.1 0.0 collective-permute-done.refs_0_
  19.1 0.0 collective-permute-done.6.refs_3_
  19.2 1.8 %collective-permute-done.4.refs_2_ = bf16[64,512]{1,0:T(8,128)(2,1)S(1)} collective-permute-done((bf16[64,512]{1,0:T(8,128)(2,1)S(1)}, bf16[64,512]{1,0:T(8,128)(2,1)S(1)}, u32[]{:S(2)}, u32[]{:S(2)}) %collective-permute-start.4) | collective-permute-done | bytes 65568 | tf_op jit(solution)/shard_map/ppermute | solution.py:381
  20.9 1.2 %collective-permute-done.2.refs_1_ = bf16[64,512]{1,0:T(8,128)(2,1)S(1)} collective-permute-done((bf16[64,512]{1,0:T(8,128)(2,1)S(1)}, bf16[64,512]{1,0:T(8,128)(2,1)S(1)}, u32[]{:S(2)}, u32[]{:S(2)}) %collective-permute-start.2) | collective-permute-done | bytes 65568 | tf_op jit(solution)/shard_map/ppermute | solution.py:381
  22.1 0.6 %far.1 = (bf16[256,512]{1,0:T(8,128)(2,1)S(1)}, f32[3,64,256]{2,1,0:T(8,128)S(1)}, f32[3,64,256]{2,1,0:T(8,128)S(1)}, bf16[4,64,512]{2,1,0:T(8,128)(2,1)S(1)}) custom-call(bf16[64,512]{1,0:T(8,128)(2,1)S(1)} %collective-permute-done.refs_0_, bf16[64,512]{1,0:T(8,128)(2,1)S(1)} %collective-permute-done.2.refs_1_, ...), custom_call_target="tpu_custom_call" | custom-call | flops 536870912 | bytes 4194304 | tf_op jit(solution)/shard_map/far/pallas_call | solution.py:398
  22.7 0.1 collective-permute-start.12
  22.8 0.5 %collective-permute-start.11 = (f32[3,64,256]{2,1,0:T(8,128)S(1)}, f32[3,64,256]{2,1,0:T(8,128)S(1)}, u32[]{:S(2)}, u32[]{:S(2)}) collective-permute-start(f32[3,64,256]{2,1,0:T(8,128)S(1)} %get-tuple-element.35), channel_id=1, source_target_pairs={{0,4},{4,0},{8,12},{12,8},{16,20},{20,16},{24,28},{28,24},{1,5},{5... | collective-permute-start | bytes 589832 | tf_op jit(solution)/shard_map/ppermute | solution.py:284
  23.3 0.3 keep.1
  23.6 0.6 %collective-permute-done.12 = f32[3,64,256]{2,1,0:T(8,128)S(1)} collective-permute-done((f32[3,64,256]{2,1,0:T(8,128)S(1)}, f32[3,64,256]{2,1,0:T(8,128)S(1)}, u32[]{:S(2)}, u32[]{:S(2)}) %collective-permute-start.12) | collective-permute-done | bytes 196640 | tf_op jit(solution)/shard_map/ppermute | solution.py:284
  24.2 0.6 %collective-permute-start.14 = (bf16[3,64,256]{2,1,0:T(8,128)(2,1)S(1)}, bf16[3,64,256]{2,1,0:T(8,128)(2,1)S(1)}, u32[]{:S(2)}, u32[]{:S(2)}) collective-permute-start(bf16[3,64,256]{2,1,0:T(8,128)(2,1)S(1)} %add_convert_fusion.3), channel_id=1, source_target_pairs={{0,8},{4,12},{8,0},{12,4},{16,24},{20,28},{24,16},{28,20},{1,9},{5... | collective-permute-start | bytes 294920 | tf_op jit(solution)/shard_map/ppermute | solution.py:284
  24.8 0.0 collective-permute-done.11
  24.9 0.9 %collective-permute-start.13 = (bf16[3,64,256]{2,1,0:T(8,128)(2,1)S(1)}, bf16[3,64,256]{2,1,0:T(8,128)(2,1)S(1)}, u32[]{:S(2)}, u32[]{:S(2)}) collective-permute-start(bf16[3,64,256]{2,1,0:T(8,128)(2,1)S(1)} %add_convert_fusion.2), channel_id=1, source_target_pairs={{0,16},{4,20},{8,24},{12,28},{16,0},{20,4},{24,8},{28,12},{1,17},{... | collective-permute-start | bytes 294920 | tf_op jit(solution)/shard_map/ppermute | solution.py:284
  25.8 3.4 %collective-permute-done.14 = bf16[3,64,256]{2,1,0:T(8,128)(2,1)S(1)} collective-permute-done((bf16[3,64,256]{2,1,0:T(8,128)(2,1)S(1)}, bf16[3,64,256]{2,1,0:T(8,128)(2,1)S(1)}, u32[]{:S(2)}, u32[]{:S(2)}) %collective-permute-start.14) | collective-permute-done | bytes 98336 | tf_op jit(solution)/shard_map/ppermute | solution.py:284
  29.2 0.6 %collective-permute-start.16 = (bf16[3,64,256]{2,1,0:T(8,128)(2,1)S(1)}, bf16[3,64,256]{2,1,0:T(8,128)(2,1)S(1)}, u32[]{:S(2)}, u32[]{:S(2)}) collective-permute-start(bf16[3,64,256]{2,1,0:T(8,128)(2,1)S(1)} %add_convert_fusion.1), channel_id=1, source_target_pairs={{0,16},{4,20},{8,24},{12,28},{16,0},{20,4},{24,8},{28,12},{1,17},{... | collective-permute-start | bytes 294920 | tf_op jit(solution)/shard_map/ppermute | solution.py:284
  29.7 0.0 collective-permute-done.13
  29.8 1.4 %collective-permute-start.15 = (bf16[3,64,256]{2,1,0:T(8,128)(2,1)S(1)}, bf16[3,64,256]{2,1,0:T(8,128)(2,1)S(1)}, u32[]{:S(2)}, u32[]{:S(2)}) collective-permute-start(bf16[3,64,256]{2,1,0:T(8,128)(2,1)S(1)} %add_convert_fusion), channel_id=1, source_target_pairs={{0,8},{4,12},{8,0},{12,4},{16,24},{20,28},{24,16},{28,20},{1,9},{5... | collective-permute-start | bytes 294920 | tf_op jit(solution)/shard_map/ppermute | solution.py:284
  31.1 2.7 %collective-permute-done.16 = bf16[3,64,256]{2,1,0:T(8,128)(2,1)S(1)} collective-permute-done((bf16[3,64,256]{2,1,0:T(8,128)(2,1)S(1)}, bf16[3,64,256]{2,1,0:T(8,128)(2,1)S(1)}, u32[]{:S(2)}, u32[]{:S(2)}) %collective-permute-start.16) | collective-permute-done | bytes 98336 | tf_op jit(solution)/shard_map/ppermute | solution.py:284
  33.9 0.1 collective-permute-start.18
  34.0 0.5 %collective-permute-done.15 = bf16[3,64,256]{2,1,0:T(8,128)(2,1)S(1)} collective-permute-done((bf16[3,64,256]{2,1,0:T(8,128)(2,1)S(1)}, bf16[3,64,256]{2,1,0:T(8,128)(2,1)S(1)}, u32[]{:S(2)}, u32[]{:S(2)}) %collective-permute-start.15) | collective-permute-done | bytes 98336 | tf_op jit(solution)/shard_map/ppermute | solution.py:284
  34.5 0.1 collective-permute-start.17
  34.6 2.1 %back_near.1 = (bf16[2,64,16,128]{3,2,1,0:T(8,128)(2,1)}, bf16[3,256,256]{2,1,0:T(8,128)(2,1)S(1)}) custom-call(bf16[256,512]{1,0:T(8,128)(2,1)S(1)} %get-tuple-element.29.g_ref, bf16[3,3,64,256]{3,2,1,0:T(8,128)(2,1)S(1)} %get-tuple-element.30.sw_ref), custom_call_target="tpu_custom_call" | custom-call | flops 1610612736 | bytes 2097152 | tf_op jit(solution)/shard_map/back_near/pallas_call | solution.py:432
  36.7 2.1 %back_far.1 = bf16[2,64,16,128]{3,2,1,0:T(8,128)(2,1)} custom-call(bf16[256,512]{1,0:T(8,128)(2,1)S(1)} %get-tuple-element.28.g_ref, bf16[3,256,256]{2,1,0:T(8,128)(2,1)S(1)} %get-tuple-element.31.wc_ref, bf16[2,64,16,128]{3,2,1,0:T(8,128)(2,1)} %get-tuple-element.32.out_in), custom_call_target="tpu_custom_call", output_to_operand_aliasing={{}: (2, {})} | custom-call | flops 1610612736 | bytes 2097152 | tf_op jit(solution)/shard_map/back_far/pallas_call | solution.py:440
  38.8 0.0 collective-permute-done.18.other_a
  38.8 0.8 %early.1 = (f32[9,64,256]{2,1,0:T(8,128)}, f32[3,64,256]{2,1,0:T(8,128)}) custom-call(f32[3,64,256]{2,1,0:T(8,128)S(1)} %convert_add_fusion.1.a_ref, f32[3,64,256]{2,1,0:T(8,128)S(1)} %convert_add_fusion.b_ref, f32[3,64,256]{2,1,0:T(8,128)S(1)} %collective-permute-done.18.other_a), custom_call_target="tpu_custom_call" | custom-call | bytes 4194304 | tf_op jit(solution)/shard_map/early/pallas_call | solution.py:461
  39.7 0.0 collective-permute-done.17.b_ref
  39.7 0.7 %finish.1 = (f32[9,64,256]{2,1,0:T(8,128)}, f32[3,64,256]{2,1,0:T(8,128)}) custom-call(f32[3,64,256]{2,1,0:T(8,128)S(1)} %collective-permute-done.17.b_ref, f32[9,64,256]{2,1,0:T(8,128)} %get-tuple-element.41.spatial_in, f32[3,64,256]{2,1,0:T(8,128)} %get-tuple-element.42.temporal_in), custom_call_target="tpu_custom_call", output_to_operand_aliasing={{0}: (1, {}), {1}: (2, {})} | custom-call | bytes 4194304 | tf_op jit(solution)/shard_map/finish/pallas_call | solution.py:462
  (9 shorter events, 0.2 us)
Async XLA Ops:
  0.6 10.2 %collective-permute-start.5 = (bf16[64,512]{1,0:T(8,128)(2,1)}, bf16[64,512]{1,0:T(8,128)(2,1)S(1)}, u32[]{:S(2)}, u32[]{:S(2)}) collective-permute-start(bf16[64,512]{1,0:T(8,128)(2,1)} %bitcast.2), channel_id=1, source_target_pairs={{0,3},{1,2},{2,1},{3,0},{4,7},{5,6},{6,5},{7,4},{8,11},{9,10},{10,... | collective-permute-start | bytes 196616 | tf_op jit(solution)/shard_map/ppermute | solution.py:284
  5.8 5.8 %collective-permute-start.3 = (bf16[64,512]{1,0:T(8,128)(2,1)}, bf16[64,512]{1,0:T(8,128)(2,1)S(1)}, u32[]{:S(2)}, u32[]{:S(2)}) collective-permute-start(bf16[64,512]{1,0:T(8,128)(2,1)} %bitcast.3), channel_id=1, source_target_pairs={{0,2},{1,3},{2,0},{3,1},{4,6},{5,7},{6,4},{7,5},{8,10},{9,11},{10,... | collective-permute-start | bytes 196616 | tf_op jit(solution)/shard_map/ppermute | solution.py:284
  5.8 5.8 %collective-permute-start.1 = (bf16[64,512]{1,0:T(8,128)(2,1)}, bf16[64,512]{1,0:T(8,128)(2,1)S(1)}, u32[]{:S(2)}, u32[]{:S(2)}) collective-permute-start(bf16[64,512]{1,0:T(8,128)(2,1)} %bitcast.4), channel_id=1, source_target_pairs={{0,1},{1,0},{2,3},{3,2},{4,5},{5,4},{6,7},{7,6},{8,9},{9,8},{10,11... | collective-permute-start | bytes 196616 | tf_op jit(solution)/shard_map/ppermute | solution.py:284
  6.4 7.1 %collective-permute-start.7 = (bf16[64,512]{1,0:T(8,128)(2,1)}, bf16[64,512]{1,0:T(8,128)(2,1)S(1)}, u32[]{:S(2)}, u32[]{:S(2)}) collective-permute-start(bf16[64,512]{1,0:T(8,128)(2,1)} %bitcast.5), channel_id=1, source_target_pairs={{0,4},{4,0},{8,12},{12,8},{16,20},{20,16},{24,28},{28,24},{1,5},{5... | collective-permute-start | bytes 196616 | tf_op jit(solution)/shard_map/ppermute | solution.py:284
  6.4 12.7 %collective-permute-start = (bf16[64,512]{1,0:T(8,128)(2,1)}, bf16[64,512]{1,0:T(8,128)(2,1)S(1)}, u32[]{:S(2)}, u32[]{:S(2)}) collective-permute-start(bf16[64,512]{1,0:T(8,128)(2,1)} %bitcast.6), channel_id=1, source_target_pairs={{0,28},{4,8},{8,4},{12,16},{16,12},{20,24},{24,20},{28,0},{1,29},{... | collective-permute-start | bytes 196616 | tf_op jit(solution)/shard_map/ppermute | solution.py:381
  10.8 4.8 %collective-permute-start.10 = (bf16[64,512]{1,0:T(8,128)(2,1)S(1)}, bf16[64,512]{1,0:T(8,128)(2,1)S(1)}, u32[]{:S(2)}, u32[]{:S(2)}) collective-permute-start(bf16[64,512]{1,0:T(8,128)(2,1)S(1)} %collective-permute-done.5.refs_3_), channel_id=1, source_target_pairs={{0,4},{4,0},{8,12},{12,8},{16,20},{20,16},{24,28},{28,24},{1,5},{5... | collective-permute-start | bytes 196616 | tf_op jit(solution)/shard_map/ppermute | solution.py:284
  11.6 4.6 %collective-permute-start.9 = (bf16[64,512]{1,0:T(8,128)(2,1)S(1)}, bf16[64,512]{1,0:T(8,128)(2,1)S(1)}, u32[]{:S(2)}, u32[]{:S(2)}) collective-permute-start(bf16[64,512]{1,0:T(8,128)(2,1)S(1)} %collective-permute-done.3.refs_2_), channel_id=1, source_target_pairs={{0,4},{4,0},{8,12},{12,8},{16,20},{20,16},{24,28},{28,24},{1,5},{5... | collective-permute-start | bytes 196616 | tf_op jit(solution)/shard_map/ppermute | solution.py:284
  11.6 6.7 %collective-permute-start.8 = (bf16[64,512]{1,0:T(8,128)(2,1)S(1)}, bf16[64,512]{1,0:T(8,128)(2,1)S(1)}, u32[]{:S(2)}, u32[]{:S(2)}) collective-permute-start(bf16[64,512]{1,0:T(8,128)(2,1)S(1)} %collective-permute-done.1.refs_1_), channel_id=1, source_target_pairs={{0,4},{4,0},{8,12},{12,8},{16,20},{20,16},{24,28},{28,24},{1,5},{5... | collective-permute-start | bytes 196616 | tf_op jit(solution)/shard_map/ppermute | solution.py:284
  12.1 6.2 %copy-start = (bf16[3,256,256]{2,1,0:T(8,128)(2,1)S(1)}, bf16[3,256,256]{2,1,0:T(8,128)(2,1)}, u32[]{:S(2)}) copy-start(bf16[3,256,256]{2,1,0:T(8,128)(2,1)} %refs_8_.1) | copy-start | bytes 1179652
  12.1 6.2 %copy-start.1 = (bf16[1,64,512]{2,1,0:T(8,128)(2,1)S(1)}, bf16[1,64,512]{2,1,0:T(8,128)(2,1)}, u32[]{:S(2)}) copy-start(bf16[1,64,512]{2,1,0:T(8,128)(2,1)} %param.7) | copy-start | bytes 196612
  13.5 5.7 %collective-permute-start.6 = (bf16[64,512]{1,0:T(8,128)(2,1)S(1)}, bf16[64,512]{1,0:T(8,128)(2,1)S(1)}, u32[]{:S(2)}, u32[]{:S(2)}) collective-permute-start(bf16[64,512]{1,0:T(8,128)(2,1)S(1)} %collective-permute-done.5.refs_3_), channel_id=1, source_target_pairs={{0,28},{4,8},{8,4},{12,16},{16,12},{20,24},{24,20},{28,0},{1,29},{... | collective-permute-start | bytes 196616 | tf_op jit(solution)/shard_map/ppermute | solution.py:381
  15.6 5.3 %collective-permute-start.4 = (bf16[64,512]{1,0:T(8,128)(2,1)S(1)}, bf16[64,512]{1,0:T(8,128)(2,1)S(1)}, u32[]{:S(2)}, u32[]{:S(2)}) collective-permute-start(bf16[64,512]{1,0:T(8,128)(2,1)S(1)} %collective-permute-done.3.refs_2_), channel_id=1, source_target_pairs={{0,28},{4,8},{8,4},{12,16},{16,12},{20,24},{24,20},{28,0},{1,29},{... | collective-permute-start | bytes 196616 | tf_op jit(solution)/shard_map/ppermute | solution.py:381
  16.2 5.9 %collective-permute-start.2 = (bf16[64,512]{1,0:T(8,128)(2,1)S(1)}, bf16[64,512]{1,0:T(8,128)(2,1)S(1)}, u32[]{:S(2)}, u32[]{:S(2)}) collective-permute-start(bf16[64,512]{1,0:T(8,128)(2,1)S(1)} %collective-permute-done.1.refs_1_), channel_id=1, source_target_pairs={{0,28},{4,8},{8,4},{12,16},{16,12},{20,24},{24,20},{28,0},{1,29},{... | collective-permute-start | bytes 196616 | tf_op jit(solution)/shard_map/ppermute | solution.py:381
  22.7 1.5 %collective-permute-start.12 = (f32[3,64,256]{2,1,0:T(8,128)S(1)}, f32[3,64,256]{2,1,0:T(8,128)S(1)}, u32[]{:S(2)}, u32[]{:S(2)}) collective-permute-start(f32[3,64,256]{2,1,0:T(8,128)S(1)} %get-tuple-element.37), channel_id=1, source_target_pairs={{0,4},{4,0},{8,12},{12,8},{16,20},{20,16},{24,28},{28,24},{1,5},{5... | collective-permute-start | bytes 589832 | tf_op jit(solution)/shard_map/ppermute | solution.py:284
  22.8 2.1 %collective-permute-start.11 = (f32[3,64,256]{2,1,0:T(8,128)S(1)}, f32[3,64,256]{2,1,0:T(8,128)S(1)}, u32[]{:S(2)}, u32[]{:S(2)}) collective-permute-start(f32[3,64,256]{2,1,0:T(8,128)S(1)} %get-tuple-element.35), channel_id=1, source_target_pairs={{0,4},{4,0},{8,12},{12,8},{16,20},{20,16},{24,28},{28,24},{1,5},{5... | collective-permute-start | bytes 589832 | tf_op jit(solution)/shard_map/ppermute | solution.py:284
  24.2 4.9 %collective-permute-start.14 = (bf16[3,64,256]{2,1,0:T(8,128)(2,1)S(1)}, bf16[3,64,256]{2,1,0:T(8,128)(2,1)S(1)}, u32[]{:S(2)}, u32[]{:S(2)}) collective-permute-start(bf16[3,64,256]{2,1,0:T(8,128)(2,1)S(1)} %add_convert_fusion.3), channel_id=1, source_target_pairs={{0,8},{4,12},{8,0},{12,4},{16,24},{20,28},{24,16},{28,20},{1,9},{5... | collective-permute-start | bytes 294920 | tf_op jit(solution)/shard_map/ppermute | solution.py:284
  24.9 4.9 %collective-permute-start.13 = (bf16[3,64,256]{2,1,0:T(8,128)(2,1)S(1)}, bf16[3,64,256]{2,1,0:T(8,128)(2,1)S(1)}, u32[]{:S(2)}, u32[]{:S(2)}) collective-permute-start(bf16[3,64,256]{2,1,0:T(8,128)(2,1)S(1)} %add_convert_fusion.2), channel_id=1, source_target_pairs={{0,16},{4,20},{8,24},{12,28},{16,0},{20,4},{24,8},{28,12},{1,17},{... | collective-permute-start | bytes 294920 | tf_op jit(solution)/shard_map/ppermute | solution.py:284
  29.2 4.7 %collective-permute-start.16 = (bf16[3,64,256]{2,1,0:T(8,128)(2,1)S(1)}, bf16[3,64,256]{2,1,0:T(8,128)(2,1)S(1)}, u32[]{:S(2)}, u32[]{:S(2)}) collective-permute-start(bf16[3,64,256]{2,1,0:T(8,128)(2,1)S(1)} %add_convert_fusion.1), channel_id=1, source_target_pairs={{0,16},{4,20},{8,24},{12,28},{16,0},{20,4},{24,8},{28,12},{1,17},{... | collective-permute-start | bytes 294920 | tf_op jit(solution)/shard_map/ppermute | solution.py:284
  29.8 4.7 %collective-permute-start.15 = (bf16[3,64,256]{2,1,0:T(8,128)(2,1)S(1)}, bf16[3,64,256]{2,1,0:T(8,128)(2,1)S(1)}, u32[]{:S(2)}, u32[]{:S(2)}) collective-permute-start(bf16[3,64,256]{2,1,0:T(8,128)(2,1)S(1)} %add_convert_fusion), channel_id=1, source_target_pairs={{0,8},{4,12},{8,0},{12,4},{16,24},{20,28},{24,16},{28,20},{1,9},{5... | collective-permute-start | bytes 294920 | tf_op jit(solution)/shard_map/ppermute | solution.py:284
  33.9 4.9 %collective-permute-start.18 = (f32[3,64,256]{2,1,0:T(8,128)S(1)}, f32[3,64,256]{2,1,0:T(8,128)S(1)}, u32[]{:S(2)}, u32[]{:S(2)}) collective-permute-start(f32[3,64,256]{2,1,0:T(8,128)S(1)} %convert_add_fusion.1.a_ref), channel_id=1, source_target_pairs={{0,4},{4,0},{8,12},{12,8},{16,20},{20,16},{24,28},{28,24},{1,5},{5... | collective-permute-start | bytes 589832 | tf_op jit(solution)/shard_map/ppermute | solution.py:284
  34.5 5.2 %collective-permute-start.17 = (f32[3,64,256]{2,1,0:T(8,128)S(1)}, f32[3,64,256]{2,1,0:T(8,128)S(1)}, u32[]{:S(2)}, u32[]{:S(2)}) collective-permute-start(f32[3,64,256]{2,1,0:T(8,128)S(1)} %convert_add_fusion.b_ref), channel_id=1, source_target_pairs={{0,4},{4,0},{8,12},{12,8},{16,20},{20,16},{24,28},{28,24},{1,5},{5... | collective-permute-start | bytes 589832 | tf_op jit(solution)/shard_map/ppermute | solution.py:284

commit v6 on v5

--- a/solution.py
+++ b/solution.py
@@ -54,7 +54,9 @@
                     left[i, at : at + chans, slot * cols : (slot + 1) * cols] = value
 
 
-def saved_kernel(x_hbm, y_hbm, sw_hbm, p_ref, x_ref, sw_ref, y_ref, sem, rows, left):
+def saved_kernel(
+    x_hbm, y_hbm, sw_hbm, p_ref, x_ref, sw_ref, pool_ref, y_ref, sem, rows, left
+):
     frames, chans, height, cols = y_ref.shape
     steps = height // 4
     fetches = [
@@ -63,10 +65,11 @@
     ]
     for fetch in fetches:
         fetch.start()
-    pool = one_hot_pool(4, (1,), cols)
+    pool_ref[...] = one_hot_pool(4, (0, 1, 2), cols)
     fetches[0].wait()
     relayout(y_ref, rows, left, (0,))
-    done = jnp.dot(left[0], pool, preferred_element_type=F32).astype(BF16)
+    middle = pool_ref[:, LANES : 2 * LANES]
+    done = jnp.dot(left[0], middle, preferred_element_type=F32).astype(BF16)
     for f in range(frames):
         for t in range(steps):
             at = (f * steps + t) * chans
@@ -75,13 +78,12 @@
     fetches[2].wait()
 
 
-def input_kernel(x_ref, s_ref, rows, left):
-    frames, chans, height, cols = x_ref.shape
+def input_kernel(x_ref, pool_ref, s_ref, rows, left):
+    frames, chans, height, _ = x_ref.shape
     steps = height // 4
-    pool = one_hot_pool(4, (0, 1, 2), cols)
     relayout(x_ref, rows, left, (-1, 0, 1))
     for a in range(3):
-        done = jnp.dot(left[a], pool, preferred_element_type=F32).astype(BF16)
+        done = jnp.dot(left[a], pool_ref[...], preferred_element_type=F32).astype(BF16)
         for f in range(frames):
             for t in range(steps):
                 at = (f * steps + t) * chans
@@ -102,7 +104,7 @@
 
 def near_kernel(scale, count, order, sent, *refs):
     pieces, inner, rest = refs[:count], refs[count : count + sent], refs[count + sent :]
-    s_ref, p_ref, tw_ref, base_ref, g_ref, part_ref, cells = rest
+    s_ref, p_ref, tw_ref, base_ref, g_ref, sent_ref, temporal_ref, cells = rest
     side = lax.rem(lax.axis_index("frames"), 2)
     me = lax.axis_index("chan")
     quarter, spots = pieces[0].shape
@@ -114,45 +116,51 @@
     now = cells[0].reshape(channels, spots)
     near = cells[1].reshape(channels, spots)
     dot = functools.partial(jnp.dot, preferred_element_type=F32)
-    middle = dot(tw_ref[1], now)
-    base_ref[...] = middle + dot(tw_ref[2 * side], now)
-    g = middle + dot(tw_ref[2 - 2 * side], now) + dot(tw_ref[2 * side], near)
+    taps_now = dot(tw_ref[...].reshape(3 * channels, channels), now)
+    first, middle, third = (taps_now[k * channels : (k + 1) * channels] for k in range(3))
+    base_ref[...] = middle + jnp.where(side == 0, first, third)
+    g = middle + jnp.where(side == 0, third, first) + dot(tw_ref[2 * side], near)
     g = (g * 0.125).astype(BF16)
     g_ref[...] = g
     pairs = p_ref[...].reshape(2 * quarter, spots)
     e_now, e_near = dot_nt(pairs, now), dot_nt(pairs, near)
     e0, e1 = e_now[:quarter], e_now[quarter:]
     small = scale * 0.125
-    taps = s_ref.shape[1] // quarter
-    part_ref[:taps] = (dot_nt(s_ref[1 - side], g) * scale).reshape(taps, quarter, channels)
-    part_ref[taps] = e0 * small
-    part_ref[taps + 1] = (e0 + e1) * small
-    part_ref[taps + 2] = e1 * small
-    first = jnp.where(side == 0, e_near[quarter:], e_near[:quarter]) * small
-    part_ref[taps + 2 * side] += first
-
-
-def add_half(low, a_ref, b_ref, scale, part_ref, s_ref, p_ref, g, far):
-    side = lax.rem(lax.axis_index("frames"), 2)
+    temporal_ref[0] = e0 * small
+    temporal_ref[1] = (e0 + e1) * small
+    temporal_ref[2] = e1 * small
+    temporal_ref[2 * side] += jnp.where(side == 0, e_near[quarter:], e_near[:quarter]) * small
+    edge = sent_ref.shape[0] * quarter
+    for low in (True, False):
+
+        @pl.when(side == int(low))
+        def _(low=low):
+            spatial = dot_nt(half_rows(low, s_ref, 1 - side, edge), g_ref[...]) * scale
+            spatial = spatial.reshape(-1, quarter, channels)
+            sent_ref[: spatial.shape[0]] = spatial
+
+
+def half_rows(low, s_ref, frame, edge):
+    return s_ref[frame, :edge] if low else s_ref[frame, edge:]
+
+
+def put_half(low, a_ref, b_ref, spatial, scale, temporal_ref, p_ref, far):
     cut, quarter, channels = a_ref.shape
-    half = cut + b_ref.shape[0]
-    edge = half * quarter
-    taps = s_ref.shape[1] // quarter
-    rows = s_ref[side, :edge] if low else s_ref[side, edge:]
-    spatial = (dot_nt(rows, g) * scale).reshape(-1, quarter, channels)
-    first = 0 if low else half
-    a_ref[...] = part_ref[first : first + cut] + spatial[:cut]
+    spatial = spatial.reshape(-1, quarter, channels)
+    a_ref[...] = spatial[:cut]
     if low:
-        b_ref[...] = part_ref[cut:half] + spatial[cut:]
+        b_ref[...] = spatial[cut:]
         return
+    side = lax.rem(lax.axis_index("frames"), 2)
     e_far = dot_nt(p_ref[...].reshape(2 * quarter, far.shape[1]), far) * (scale * 0.125)
-    b_ref[...] = part_ref[taps:]
+    b_ref[...] = temporal_ref[...]
     b_ref[2 - 2 * side] += jnp.where(side == 0, e_far[:quarter], e_far[quarter:])
 
 
 def far_kernel(scale, count, order, sent, *refs):
     outer, rest = refs[:sent], refs[sent:]
-    base_ref, part_ref, s_ref, p_ref, tw_ref, g_ref, send_a, send_b, cells_ref = rest
+    base_ref, sent_ref, temporal_ref, s_ref, p_ref, tw_ref = rest[:6]
+    g_ref, send_a, send_b, cells_ref = rest[6:]
     at_frame = lax.axis_index("frames")
     side = lax.rem(at_frame, 2)
     me = lax.axis_index("chan")
@@ -169,10 +177,15 @@
 
         @pl.when(side == int(low))
         def _(low=low):
-            add_half(low, send_a, send_b, scale, part_ref, s_ref, p_ref, g_ref[...], far)
-
-
-def keep_kernel(scale, part_ref, s_ref, p_ref, g_ref, cells_ref, keep_a, keep_b):
+            half, _, channels = sent_ref.shape
+            spatial = dot_nt(half_rows(low, s_ref, side, half * quarter), g_ref[...]) * scale
+            known = sent_ref[: spatial.shape[0] // quarter].reshape(-1, channels)
+            put_half(low, send_a, send_b, known + spatial, scale, temporal_ref, p_ref, far)
+
+
+def keep_kernel(
+    scale, temporal_ref, s_ref, p_ref, near_ref, far_ref, cells_ref, keep_a, keep_b
+):
     side = lax.rem(lax.axis_index("frames"), 2)
     count, quarter, spots = cells_ref.shape
     for low in (True, False):
@@ -180,7 +193,10 @@
         @pl.when(side == 1 - int(low))
         def _(low=low):
             far = cells_ref[...].reshape(count * quarter, spots)
-            add_half(low, keep_a, keep_b, scale, part_ref, s_ref, p_ref, g_ref[...], far)
+            edge = (keep_a.shape[0] + keep_b.shape[0]) * quarter
+            spatial = dot_nt(half_rows(low, s_ref, 1 - side, edge), near_ref[...])
+            spatial += dot_nt(half_rows(low, s_ref, side, edge), far_ref[...])
+            put_half(low, keep_a, keep_b, spatial * scale, scale, temporal_ref, p_ref, far)
 
 
 def early_kernel(a_ref, b_ref, other_a, spatial_hbm, temporal_hbm, sem):
@@ -307,15 +323,16 @@
     rows = pltpu.VMEM((frames * quarter * height, cols), F32)
     limit = pltpu.CompilerParams(vmem_limit_bytes=20 << 20)
     held = [pltpu.with_memory_space_constraint(x, pltpu.HBM) for x in (inputs, saved, spatial_w)]
-    pooled, staged, weights = pl.pallas_call(
+    pooled, staged, weights, pool = pl.pallas_call(
         saved_kernel,
         out_shape=(
             shape((frames, quarter, spots), BF16),
             shape(inputs.shape, BF16),
             shape(spatial_w.shape, BF16),
+            shape((4 * cols, 3 * LANES), BF16),
         ),
         in_specs=[pl.BlockSpec(memory_space=pltpu.HBM)] * 3,
-        out_specs=tuple(vmem(3)),
+        out_specs=tuple(vmem(4)),
         scratch_shapes=[
             pltpu.VMEM(inputs.shape, BF16),
             pltpu.SemaphoreType.DMA((3,)),
@@ -329,13 +346,13 @@
     sums = pl.pallas_call(
         input_kernel,
         out_shape=shape((frames, taps * quarter, spots), BF16),
-        in_specs=vmem(1),
+        in_specs=vmem(2),
         out_specs=vmem(1)[0],
         scratch_shapes=[rows, pltpu.VMEM((3, groups, 4 * cols), BF16)],
         compiler_params=limit,
         cost_estimate=cost(1 << 30, 4 << 20),
         name="prep_inputs",
-    )(staged)
+    )(staged, pool)
     return sums, pooled, weights
 
 
@@ -375,21 +392,31 @@
     sums, pooled, weights = prep(inputs, saved, spatial_w)
     groups = [[k] for k in range(count)]
     order = {k: (i, j if len(g) > 1 else None) for i, g in enumerate(groups) for j, k in enumerate(g)}
-    outer, inner = [], []
+    outer = []
     for group in groups:
         value = pieces[group[0]] if len(group) == 1 else jnp.stack([pieces[k] for k in group])
-        outer.append(lax.ppermute(value, "frames", across))
-        inner.append(swap(value, "frames", 1))
+        if group == [1]:
+            outer.append(swap(outer[0], "chan", 1))
+        else:
+            outer.append(lax.ppermute(value, "frames", across))
+
+    near = [pieces[0], jnp.stack(pieces[1:])]
+    inner = [swap(value, "frames", 1) for value in near]
+    near_order = {k: (0, None) if k == 0 else (1, k - 1) for k in range(count)}
 
     slices = taps + 3
     limit = pltpu.CompilerParams(vmem_limit_bytes=20 << 20)
-    part_shape = shape((slices, quarter, channels), F32)
     half_shapes = [shape((n, quarter, channels), F32) for n in (taps - slices // 2, slices - taps)]
-    base, g_near, part = pl.pallas_call(
-        functools.partial(near_kernel, scale, count, order, len(inner)),
-        out_shape=(shape((channels, spots), F32), shape((channels, spots), BF16), part_shape),
+    base, g_near, sent, temporal_near = pl.pallas_call(
+        functools.partial(near_kernel, scale, count, near_order, len(inner)),
+        out_shape=(
+            shape((channels, spots), F32),
+            shape((channels, spots), BF16),
+            shape((slices // 2, quarter, channels), F32),
+            half_shapes[1],
+        ),
         in_specs=vmem(count + len(inner) + 3),
-        out_specs=tuple(vmem(3)),
+        out_specs=tuple(vmem(4)),
         scratch_shapes=[pltpu.VMEM((2, count, quarter, spots), BF16)],
         compiler_params=limit,
         cost_estimate=cost(1 << 30, 4 << 20),
@@ -402,21 +429,21 @@
             *half_shapes,
             shape((count, quarter, spots), BF16),
         ),
-        in_specs=vmem(len(outer) + 5),
+        in_specs=vmem(len(outer) + 6),
         out_specs=tuple(vmem(4)),
         compiler_params=limit,
         cost_estimate=cost(1 << 29, 4 << 20),
         name="far",
-    )(*outer, base, part, sums, pooled, temporal_w)
+    )(*outer, base, sent, temporal_near, sums, pooled, temporal_w)
     keep = pl.pallas_call(
         functools.partial(keep_kernel, scale),
         out_shape=tuple(half_shapes),
-        in_specs=vmem(5),
+        in_specs=vmem(6),
         out_specs=tuple(vmem(2)),
         compiler_params=limit,
         cost_estimate=cost(1 << 28, 4 << 20),
         name="keep",
-    )(part, sums, pooled, g_far, cells)
+    )(temporal_near, sums, pooled, g_near, g_far, cells)
 
     hbm = pl.BlockSpec(memory_space=pltpu.HBM)
     back = dict(

time: 40.6 us -> 44.1 us (1.086)
  waiting for transfers between devices: 10.9 us -> 17.7 us
  starting transfers between devices: 18 us -> 14.6 us
    ppermute x15 -> x14, waiting for transfers between devices: 7.92 us -> 14.8 us  [swap(): return lax.ppermute(value, axis, pairs)]
    ppermute x4 -> x3, starting transfers between devices: 7.48 us -> 4.84 us  [shards(): outer.append(lax.ppermute(value, 'frames', across))]
    ppermute x15 -> x14, starting transfers between devices: 10.5 us -> 9.76 us  [swap(): return lax.ppermute(value, axis, pairs)]
    ppermute x4 -> x3, waiting for transfers between devices: 2.96 us -> 2.82 us  [shards(): outer.append(lax.ppermute(value, 'frames', across))]
  transfers between devices with their start and end apart: 19 -> 17, of which waited for: 7 -> 10; matrix products, arithmetic and copies ran while one was open for 0% -> 0% of each run, Pallas kernels for 23% -> 21%
where the time goes in v6:
time: 44.1 us; the launch traced here: 43.9 us
  waiting for transfers between devices  17.7 us (40%)
  starting transfers between devices  14.6 us (33%)
  Pallas kernels  10.7 us (24%)
  between operations  0.83 us (2%)
    ppermute x14, waiting for transfers between devices, swap(): return lax.ppermute(value, axis, pairs)  14.8 us
    ppermute x14, starting transfers between devices, swap(): return lax.ppermute(value, axis, pairs)  9.76 us
    ppermute x3, starting transfers between devices, shards(): outer.append(lax.ppermute(value, 'frames', across))  4.84 us
    ppermute x3, waiting for transfers between devices, shards(): outer.append(lax.ppermute(value, 'frames', across))  2.82 us
    pallas_call x1, Pallas kernels, shards(): pl.pallas_call(back_far_kernel, out_shape=shape(inputs.shape, BF16), in_s...  2.12 us
    pallas_call x1, Pallas kernels, shards(): pl.pallas_call(back_near_kernel, out_shape=(shape(inputs.shape, BF16), sh...  2.12 us
    pallas_call x1, Pallas kernels, prep(): pl.pallas_call(saved_kernel, out_shape=(shape((frames, quarter, spots), B...  1.69 us
    pallas_call x1, Pallas kernels, prep(): pl.pallas_call(input_kernel, out_shape=shape((frames, taps * quarter, spo...  1.28 us
  transfers between devices with their start and end apart: 17, of which 10 were waited for; matrix products, arithmetic and copies ran while one was open for 0% of the time, Pallas kernels for 21%

profile of v6, /device:TPU:0, one launch (start us, length us, event | category | flops | bytes accessed | tf_op | source)
XLA Modules:
  0.0 43.9 jit_solution(3444766145565914058)
XLA Ops:
  0.6 3.1 %collective-permute-start.6 = (bf16[64,512]{1,0:T(8,128)(2,1)}, bf16[64,512]{1,0:T(8,128)(2,1)S(1)}, u32[]{:S(2)}, u32[]{:S(2)}) collective-permute-start(bf16[64,512]{1,0:T(8,128)(2,1)} %bitcast.8), channel_id=1, source_target_pairs={{0,1},{1,0},{2,3},{3,2},{4,5},{5,4},{6,7},{7,6},{8,9},{9,8},{10,11... | collective-permute-start | bytes 196616 | tf_op jit(solution)/shard_map/ppermute | solution.py:300
  3.7 2.5 %collective-permute-start.4 = (bf16[64,512]{1,0:T(8,128)(2,1)}, bf16[64,512]{1,0:T(8,128)(2,1)S(1)}, u32[]{:S(2)}, u32[]{:S(2)}) collective-permute-start(bf16[64,512]{1,0:T(8,128)(2,1)} %bitcast.9), channel_id=1, source_target_pairs={{0,3},{1,2},{2,1},{3,0},{4,7},{5,6},{6,5},{7,4},{8,11},{9,10},{10,... | collective-permute-start | bytes 196616 | tf_op jit(solution)/shard_map/ppermute | solution.py:300
  6.2 0.1 collective-permute-start.2
  6.3 0.0 collective-permute-done.6.refs_1_
  6.3 4.5 %collective-permute-done.4.refs_3_ = bf16[64,512]{1,0:T(8,128)(2,1)S(1)} collective-permute-done((bf16[64,512]{1,0:T(8,128)(2,1)}, bf16[64,512]{1,0:T(8,128)(2,1)S(1)}, u32[]{:S(2)}, u32[]{:S(2)}) %collective-permute-start.4) | collective-permute-done | bytes 65568 | tf_op jit(solution)/shard_map/ppermute | solution.py:300
  10.8 2.1 %collective-permute-done.2.refs_2_ = bf16[64,512]{1,0:T(8,128)(2,1)S(1)} collective-permute-done((bf16[64,512]{1,0:T(8,128)(2,1)}, bf16[64,512]{1,0:T(8,128)(2,1)S(1)}, u32[]{:S(2)}, u32[]{:S(2)}) %collective-permute-start.2) | collective-permute-done | bytes 65568 | tf_op jit(solution)/shard_map/ppermute | solution.py:300
  12.9 0.1 collective-permute-start.8
  13.0 0.5 %collective-permute-start.7 = (bf16[64,512]{1,0:T(8,128)(2,1)}, bf16[64,512]{1,0:T(8,128)(2,1)S(1)}, u32[]{:S(2)}, u32[]{:S(2)}) collective-permute-start(bf16[64,512]{1,0:T(8,128)(2,1)} %bitcast.11), channel_id=1, source_target_pairs={{0,4},{4,0},{8,12},{12,8},{16,20},{20,16},{24,28},{28,24},{1,5},{5... | collective-permute-start | bytes 196616 | tf_op jit(solution)/shard_map/ppermute | solution.py:300
  13.5 2.1 %collective-permute-start = (bf16[64,512]{1,0:T(8,128)(2,1)}, bf16[64,512]{1,0:T(8,128)(2,1)S(1)}, u32[]{:S(2)}, u32[]{:S(2)}) collective-permute-start(bf16[64,512]{1,0:T(8,128)(2,1)} %bitcast.12), channel_id=1, source_target_pairs={{0,28},{4,8},{8,4},{12,16},{16,12},{20,24},{24,20},{28,0},{1,29},{... | collective-permute-start | bytes 196616 | tf_op jit(solution)/shard_map/ppermute | solution.py:401
  15.6 1.7 %prep_saved.1 = (bf16[2,64,512]{2,1,0:T(8,128)(2,1)S(1)}, bf16[2,64,16,128]{3,2,1,0:T(8,128)(2,1)S(1)}, bf16[3,3,64,256]{3,2,1,0:T(8,128)(2,1)S(1)}, bf16[512,384]{1,0:T(8,128)(2,1)S(1)}) custom-call(bf16[2,64,16,128]{3,2,1,0:T(8,128)(2,1)} %x_hbm.1, bf16[2,64,16,128]{3,2,1,0:T(8,128)(2,1)} %y_hbm.1, bf16[3,3,64,256]{3,2,1,0:T(8,128)(2,1)} %sw_hbm.1), custom_call_target="tpu_custom_call" | custom-call | flops 536870912 | bytes 4194304 | tf_op jit(solution)/shard_map/prep_saved/pallas_call | solution.py:326
  17.3 0.0 copy-start
  17.3 0.0 copy-start.1
  17.4 1.3 %prep_inputs.1.refs_6_.refs_7_.s_ref = bf16[2,576,512]{2,1,0:T(8,128)(2,1)S(1)} custom-call(bf16[2,64,16,128]{3,2,1,0:T(8,128)(2,1)S(1)} %get-tuple-element.26.x_ref, bf16[512,384]{1,0:T(8,128)(2,1)S(1)} %get-tuple-element.27.pool_ref), custom_call_target="tpu_custom_call" | custom-call | flops 1073741824 | bytes 4194304 | tf_op jit(solution)/shard_map/prep_inputs/pallas_call | solution.py:346
  18.6 0.6 %collective-permute-start.5 = (bf16[64,512]{1,0:T(8,128)(2,1)S(1)}, bf16[64,512]{1,0:T(8,128)(2,1)S(1)}, u32[]{:S(2)}, u32[]{:S(2)}) collective-permute-start(bf16[64,512]{1,0:T(8,128)(2,1)S(1)} %collective-permute-done.4.refs_3_), channel_id=1, source_target_pairs={{0,28},{4,8},{8,4},{12,16},{16,12},{20,24},{24,20},{28,0},{1,29},{... | collective-permute-start | bytes 196616 | tf_op jit(solution)/shard_map/ppermute | solution.py:401
  19.2 2.1 %collective-permute-start.3 = (bf16[64,512]{1,0:T(8,128)(2,1)S(1)}, bf16[64,512]{1,0:T(8,128)(2,1)S(1)}, u32[]{:S(2)}, u32[]{:S(2)}) collective-permute-start(bf16[64,512]{1,0:T(8,128)(2,1)S(1)} %collective-permute-done.2.refs_2_), channel_id=1, source_target_pairs={{0,28},{4,8},{8,4},{12,16},{16,12},{20,24},{24,20},{28,0},{1,29},{... | collective-permute-start | bytes 196616 | tf_op jit(solution)/shard_map/ppermute | solution.py:401
  21.3 0.0 collective-permute-done.refs_0_
  21.4 0.0 collective-permute-start.1
  21.4 0.0 collective-permute-done.7.refs_4_
  21.4 0.0 collective-permute-done.8.refs_5_
  21.4 0.0 copy-done
  21.4 0.0 copy-done.1
  21.4 0.9 %near.1 = (f32[256,512]{1,0:T(8,128)S(1)}, bf16[256,512]{1,0:T(8,128)(2,1)S(1)}, f32[6,64,256]{2,1,0:T(8,128)S(1)}, f32[3,64,256]{2,1,0:T(8,128)S(1)}) custom-call(bf16[64,512]{1,0:T(8,128)(2,1)S(1)} %bitcast.13, bf16[64,512]{1,0:T(8,128)(2,1)S(1)} %collective-permute-done.6.refs_1_, bf16[64,512]{1,0:T(8,128)(2,1)S(1)} %collective-permute-done.2.refs_2_, ...), custom_call_target="tpu_custom_call" | custom-call | flops 1073741824 | bytes 4194304 | tf_op jit(solution)/shard_map/near/pallas_call | solution.py:410
  22.3 1.7 %collective-permute-done.5.refs_3_ = bf16[64,512]{1,0:T(8,128)(2,1)S(1)} collective-permute-done((bf16[64,512]{1,0:T(8,128)(2,1)S(1)}, bf16[64,512]{1,0:T(8,128)(2,1)S(1)}, u32[]{:S(2)}, u32[]{:S(2)}) %collective-permute-start.5) | collective-permute-done | bytes 65568 | tf_op jit(solution)/shard_map/ppermute | solution.py:401
  24.0 1.1 %collective-permute-done.3.refs_2_ = bf16[64,512]{1,0:T(8,128)(2,1)S(1)} collective-permute-done((bf16[64,512]{1,0:T(8,128)(2,1)S(1)}, bf16[64,512]{1,0:T(8,128)(2,1)S(1)}, u32[]{:S(2)}, u32[]{:S(2)}) %collective-permute-start.3) | collective-permute-done | bytes 65568 | tf_op jit(solution)/shard_map/ppermute | solution.py:401
  25.1 0.5 %collective-permute-done.1.refs_1_ = bf16[64,512]{1,0:T(8,128)(2,1)S(1)} collective-permute-done((bf16[64,512]{1,0:T(8,128)(2,1)S(1)}, bf16[64,512]{1,0:T(8,128)(2,1)S(1)}, u32[]{:S(2)}, u32[]{:S(2)}) %collective-permute-start.1) | collective-permute-done | bytes 65568 | tf_op jit(solution)/shard_map/ppermute | solution.py:300
  25.6 0.6 %far.1 = (bf16[256,512]{1,0:T(8,128)(2,1)S(1)}, f32[3,64,256]{2,1,0:T(8,128)S(1)}, f32[3,64,256]{2,1,0:T(8,128)S(1)}, bf16[4,64,512]{2,1,0:T(8,128)(2,1)S(1)}) custom-call(bf16[64,512]{1,0:T(8,128)(2,1)S(1)} %collective-permute-done.refs_0_, bf16[64,512]{1,0:T(8,128)(2,1)S(1)} %collective-permute-done.1.refs_1_, ...), custom_call_target="tpu_custom_call" | custom-call | flops 536870912 | bytes 4194304 | tf_op jit(solution)/shard_map/far/pallas_call | solution.py:425
  26.2 0.1 collective-permute-start.10
  26.3 0.5 %collective-permute-start.9 = (f32[3,64,256]{2,1,0:T(8,128)S(1)}, f32[3,64,256]{2,1,0:T(8,128)S(1)}, u32[]{:S(2)}, u32[]{:S(2)}) collective-permute-start(f32[3,64,256]{2,1,0:T(8,128)S(1)} %get-tuple-element.39), channel_id=1, source_target_pairs={{0,4},{4,0},{8,12},{12,8},{16,20},{20,16},{24,28},{28,24},{1,5},{5... | collective-permute-start | bytes 589832 | tf_op jit(solution)/shard_map/ppermute | solution.py:300
  26.8 0.4 keep.1
  27.2 0.5 %collective-permute-done.10 = f32[3,64,256]{2,1,0:T(8,128)S(1)} collective-permute-done((f32[3,64,256]{2,1,0:T(8,128)S(1)}, f32[3,64,256]{2,1,0:T(8,128)S(1)}, u32[]{:S(2)}, u32[]{:S(2)}) %collective-permute-start.10) | collective-permute-done | bytes 196640 | tf_op jit(solution)/shard_map/ppermute | solution.py:300
  27.7 0.1 collective-permute-start.12
  27.8 0.2 collective-permute-done.9
  28.0 0.8 %collective-permute-start.11 = (bf16[3,64,256]{2,1,0:T(8,128)(2,1)S(1)}, bf16[3,64,256]{2,1,0:T(8,128)(2,1)S(1)}, u32[]{:S(2)}, u32[]{:S(2)}) collective-permute-start(bf16[3,64,256]{2,1,0:T(8,128)(2,1)S(1)} %add_convert_fusion.2), channel_id=1, source_target_pairs={{0,16},{4,20},{8,24},{12,28},{16,0},{20,4},{24,8},{28,12},{1,17},{... | collective-permute-start | bytes 294920 | tf_op jit(solution)/shard_map/ppermute | solution.py:300
  28.8 3.9 %collective-permute-done.12 = bf16[3,64,256]{2,1,0:T(8,128)(2,1)S(1)} collective-permute-done((bf16[3,64,256]{2,1,0:T(8,128)(2,1)S(1)}, bf16[3,64,256]{2,1,0:T(8,128)(2,1)S(1)}, u32[]{:S(2)}, u32[]{:S(2)}) %collective-permute-start.12) | collective-permute-done | bytes 98336 | tf_op jit(solution)/shard_map/ppermute | solution.py:300
  32.7 0.6 %collective-permute-start.14 = (bf16[3,64,256]{2,1,0:T(8,128)(2,1)S(1)}, bf16[3,64,256]{2,1,0:T(8,128)(2,1)S(1)}, u32[]{:S(2)}, u32[]{:S(2)}) collective-permute-start(bf16[3,64,256]{2,1,0:T(8,128)(2,1)S(1)} %add_convert_fusion.1), channel_id=1, source_target_pairs={{0,16},{4,20},{8,24},{12,28},{16,0},{20,4},{24,8},{28,12},{1,17},{... | collective-permute-start | bytes 294920 | tf_op jit(solution)/shard_map/ppermute | solution.py:300
  33.3 0.0 collective-permute-done.11
  33.3 1.4 %collective-permute-start.13 = (bf16[3,64,256]{2,1,0:T(8,128)(2,1)S(1)}, bf16[3,64,256]{2,1,0:T(8,128)(2,1)S(1)}, u32[]{:S(2)}, u32[]{:S(2)}) collective-permute-start(bf16[3,64,256]{2,1,0:T(8,128)(2,1)S(1)} %add_convert_fusion), channel_id=1, source_target_pairs={{0,8},{4,12},{8,0},{12,4},{16,24},{20,28},{24,16},{28,20},{1,9},{5... | collective-permute-start | bytes 294920 | tf_op jit(solution)/shard_map/ppermute | solution.py:300
  34.6 2.7 %collective-permute-done.14 = bf16[3,64,256]{2,1,0:T(8,128)(2,1)S(1)} collective-permute-done((bf16[3,64,256]{2,1,0:T(8,128)(2,1)S(1)}, bf16[3,64,256]{2,1,0:T(8,128)(2,1)S(1)}, u32[]{:S(2)}, u32[]{:S(2)}) %collective-permute-start.14) | collective-permute-done | bytes 98336 | tf_op jit(solution)/shard_map/ppermute | solution.py:300
  37.4 0.1 collective-permute-start.16
  37.5 0.5 %collective-permute-done.13 = bf16[3,64,256]{2,1,0:T(8,128)(2,1)S(1)} collective-permute-done((bf16[3,64,256]{2,1,0:T(8,128)(2,1)S(1)}, bf16[3,64,256]{2,1,0:T(8,128)(2,1)S(1)}, u32[]{:S(2)}, u32[]{:S(2)}) %collective-permute-start.13) | collective-permute-done | bytes 98336 | tf_op jit(solution)/shard_map/ppermute | solution.py:300
  38.0 0.1 collective-permute-start.15
  38.1 2.1 %back_near.1 = (bf16[2,64,16,128]{3,2,1,0:T(8,128)(2,1)}, bf16[3,256,256]{2,1,0:T(8,128)(2,1)S(1)}) custom-call(bf16[256,512]{1,0:T(8,128)(2,1)S(1)} %get-tuple-element.33.g_ref.near_ref, bf16[3,3,64,256]{3,2,1,0:T(8,128)(2,1)S(1)} %get-tuple-element.34.sw_ref), custom_call_target="tpu_custom_call" | custom-call | flops 1610612736 | bytes 2097152 | tf_op jit(solution)/shard_map/back_near/pallas_call | solution.py:459
  40.2 2.1 %back_far.1 = bf16[2,64,16,128]{3,2,1,0:T(8,128)(2,1)} custom-call(bf16[256,512]{1,0:T(8,128)(2,1)S(1)} %get-tuple-element.32.g_ref.far_ref, bf16[3,256,256]{2,1,0:T(8,128)(2,1)S(1)} %get-tuple-element.35.wc_ref, bf16[2,64,16,128]{3,2,1,0:T(8,128)(2,1)} %get-tuple-element.36.out_in), custom_call_target="tpu_custom_call", output_to_operand_aliasing={{}: (2, {})} | custom-call | flops 1610612736 | bytes 2097152 | tf_op jit(solution)/shard_map/back_far/pallas_call | solution.py:467
  42.3 0.0 collective-permute-done.16.other_a
  42.3 0.8 %early.1 = (f32[9,64,256]{2,1,0:T(8,128)}, f32[3,64,256]{2,1,0:T(8,128)}) custom-call(f32[3,64,256]{2,1,0:T(8,128)S(1)} %convert_add_fusion.1.a_ref, f32[3,64,256]{2,1,0:T(8,128)S(1)} %convert_add_fusion.b_ref, f32[3,64,256]{2,1,0:T(8,128)S(1)} %collective-permute-done.16.other_a), custom_call_target="tpu_custom_call" | custom-call | bytes 4194304 | tf_op jit(solution)/shard_map/early/pallas_call | solution.py:488
  43.2 0.0 collective-permute-done.15.b_ref
  43.2 0.7 %finish.1 = (f32[9,64,256]{2,1,0:T(8,128)}, f32[3,64,256]{2,1,0:T(8,128)}) custom-call(f32[3,64,256]{2,1,0:T(8,128)S(1)} %collective-permute-done.15.b_ref, f32[9,64,256]{2,1,0:T(8,128)} %get-tuple-element.45.spatial_in, f32[3,64,256]{2,1,0:T(8,128)} %get-tuple-element.46.temporal_in), custom_call_target="tpu_custom_call", output_to_operand_aliasing={{0}: (1, {}), {1}: (2, {})} | custom-call | bytes 4194304 | tf_op jit(solution)/shard_map/finish/pallas_call | solution.py:489
  (7 shorter events, 0.2 us)
Async XLA Ops:
  0.6 5.7 %collective-permute-start.6 = (bf16[64,512]{1,0:T(8,128)(2,1)}, bf16[64,512]{1,0:T(8,128)(2,1)S(1)}, u32[]{:S(2)}, u32[]{:S(2)}) collective-permute-start(bf16[64,512]{1,0:T(8,128)(2,1)} %bitcast.8), channel_id=1, source_target_pairs={{0,1},{1,0},{2,3},{3,2},{4,5},{5,4},{6,7},{7,6},{8,9},{9,8},{10,11... | collective-permute-start | bytes 196616 | tf_op jit(solution)/shard_map/ppermute | solution.py:300
  3.7 7.1 %collective-permute-start.4 = (bf16[64,512]{1,0:T(8,128)(2,1)}, bf16[64,512]{1,0:T(8,128)(2,1)S(1)}, u32[]{:S(2)}, u32[]{:S(2)}) collective-permute-start(bf16[64,512]{1,0:T(8,128)(2,1)} %bitcast.9), channel_id=1, source_target_pairs={{0,3},{1,2},{2,1},{3,0},{4,7},{5,6},{6,5},{7,4},{8,11},{9,10},{10,... | collective-permute-start | bytes 196616 | tf_op jit(solution)/shard_map/ppermute | solution.py:300
  6.2 6.7 %collective-permute-start.2 = (bf16[64,512]{1,0:T(8,128)(2,1)}, bf16[64,512]{1,0:T(8,128)(2,1)S(1)}, u32[]{:S(2)}, u32[]{:S(2)}) collective-permute-start(bf16[64,512]{1,0:T(8,128)(2,1)} %bitcast.10), channel_id=1, source_target_pairs={{0,2},{1,3},{2,0},{3,1},{4,6},{5,7},{6,4},{7,5},{8,10},{9,11},{10,... | collective-permute-start | bytes 196616 | tf_op jit(solution)/shard_map/ppermute | solution.py:300
  12.9 8.4 %collective-permute-start.8 = (bf16[3,64,512]{2,1,0:T(8,128)(2,1)S(1)}, bf16[3,64,512]{2,1,0:T(8,128)(2,1)S(1)}, u32[]{:S(2)}, u32[]{:S(2)}) collective-permute-start(bf16[3,64,512]{2,1,0:T(8,128)(2,1)S(1)} %pad_maximum_fusion), channel_id=1, source_target_pairs={{0,4},{4,0},{8,12},{12,8},{16,20},{20,16},{24,28},{28,24},{1,5},{5... | collective-permute-start | bytes 589832 | tf_op jit(solution)/shard_map/ppermute | solution.py:300
  13.0 8.4 %collective-permute-start.7 = (bf16[64,512]{1,0:T(8,128)(2,1)}, bf16[64,512]{1,0:T(8,128)(2,1)S(1)}, u32[]{:S(2)}, u32[]{:S(2)}) collective-permute-start(bf16[64,512]{1,0:T(8,128)(2,1)} %bitcast.11), channel_id=1, source_target_pairs={{0,4},{4,0},{8,12},{12,8},{16,20},{20,16},{24,28},{28,24},{1,5},{5... | collective-permute-start | bytes 196616 | tf_op jit(solution)/shard_map/ppermute | solution.py:300
  13.5 7.9 %collective-permute-start = (bf16[64,512]{1,0:T(8,128)(2,1)}, bf16[64,512]{1,0:T(8,128)(2,1)S(1)}, u32[]{:S(2)}, u32[]{:S(2)}) collective-permute-start(bf16[64,512]{1,0:T(8,128)(2,1)} %bitcast.12), channel_id=1, source_target_pairs={{0,28},{4,8},{8,4},{12,16},{16,12},{20,24},{24,20},{28,0},{1,29},{... | collective-permute-start | bytes 196616 | tf_op jit(solution)/shard_map/ppermute | solution.py:401
  17.3 4.0 %copy-start = (bf16[3,256,256]{2,1,0:T(8,128)(2,1)S(1)}, bf16[3,256,256]{2,1,0:T(8,128)(2,1)}, u32[]{:S(2)}) copy-start(bf16[3,256,256]{2,1,0:T(8,128)(2,1)} %refs_9_.1) | copy-start | bytes 1179652
  17.3 4.0 %copy-start.1 = (bf16[1,64,512]{2,1,0:T(8,128)(2,1)S(1)}, bf16[1,64,512]{2,1,0:T(8,128)(2,1)}, u32[]{:S(2)}) copy-start(bf16[1,64,512]{2,1,0:T(8,128)(2,1)} %param.7) | copy-start | bytes 196612
  18.6 5.4 %collective-permute-start.5 = (bf16[64,512]{1,0:T(8,128)(2,1)S(1)}, bf16[64,512]{1,0:T(8,128)(2,1)S(1)}, u32[]{:S(2)}, u32[]{:S(2)}) collective-permute-start(bf16[64,512]{1,0:T(8,128)(2,1)S(1)} %collective-permute-done.4.refs_3_), channel_id=1, source_target_pairs={{0,28},{4,8},{8,4},{12,16},{16,12},{20,24},{24,20},{28,0},{1,29},{... | collective-permute-start | bytes 196616 | tf_op jit(solution)/shard_map/ppermute | solution.py:401
  19.2 5.9 %collective-permute-start.3 = (bf16[64,512]{1,0:T(8,128)(2,1)S(1)}, bf16[64,512]{1,0:T(8,128)(2,1)S(1)}, u32[]{:S(2)}, u32[]{:S(2)}) collective-permute-start(bf16[64,512]{1,0:T(8,128)(2,1)S(1)} %collective-permute-done.2.refs_2_), channel_id=1, source_target_pairs={{0,28},{4,8},{8,4},{12,16},{16,12},{20,24},{24,20},{28,0},{1,29},{... | collective-permute-start | bytes 196616 | tf_op jit(solution)/shard_map/ppermute | solution.py:401
  21.4 4.3 %collective-permute-start.1 = (bf16[64,512]{1,0:T(8,128)(2,1)S(1)}, bf16[64,512]{1,0:T(8,128)(2,1)S(1)}, u32[]{:S(2)}, u32[]{:S(2)}) collective-permute-start(bf16[64,512]{1,0:T(8,128)(2,1)S(1)} %collective-permute-done.refs_0_), channel_id=1, source_target_pairs={{0,1},{1,0},{2,3},{3,2},{4,5},{5,4},{6,7},{7,6},{8,9},{9,8},{10,11... | collective-permute-start | bytes 196616 | tf_op jit(solution)/shard_map/ppermute | solution.py:300
  26.2 1.5 %collective-permute-start.10 = (f32[3,64,256]{2,1,0:T(8,128)S(1)}, f32[3,64,256]{2,1,0:T(8,128)S(1)}, u32[]{:S(2)}, u32[]{:S(2)}) collective-permute-start(f32[3,64,256]{2,1,0:T(8,128)S(1)} %get-tuple-element.41), channel_id=1, source_target_pairs={{0,4},{4,0},{8,12},{12,8},{16,20},{20,16},{24,28},{28,24},{1,5},{5... | collective-permute-start | bytes 589832 | tf_op jit(solution)/shard_map/ppermute | solution.py:300
  26.3 1.7 %collective-permute-start.9 = (f32[3,64,256]{2,1,0:T(8,128)S(1)}, f32[3,64,256]{2,1,0:T(8,128)S(1)}, u32[]{:S(2)}, u32[]{:S(2)}) collective-permute-start(f32[3,64,256]{2,1,0:T(8,128)S(1)} %get-tuple-element.39), channel_id=1, source_target_pairs={{0,4},{4,0},{8,12},{12,8},{16,20},{20,16},{24,28},{28,24},{1,5},{5... | collective-permute-start | bytes 589832 | tf_op jit(solution)/shard_map/ppermute | solution.py:300
  27.7 4.9 %collective-permute-start.12 = (bf16[3,64,256]{2,1,0:T(8,128)(2,1)S(1)}, bf16[3,64,256]{2,1,0:T(8,128)(2,1)S(1)}, u32[]{:S(2)}, u32[]{:S(2)}) collective-permute-start(bf16[3,64,256]{2,1,0:T(8,128)(2,1)S(1)} %add_convert_fusion.3), channel_id=1, source_target_pairs={{0,8},{4,12},{8,0},{12,4},{16,24},{20,28},{24,16},{28,20},{1,9},{5... | collective-permute-start | bytes 294920 | tf_op jit(solution)/shard_map/ppermute | solution.py:300
  28.0 5.2 %collective-permute-start.11 = (bf16[3,64,256]{2,1,0:T(8,128)(2,1)S(1)}, bf16[3,64,256]{2,1,0:T(8,128)(2,1)S(1)}, u32[]{:S(2)}, u32[]{:S(2)}) collective-permute-start(bf16[3,64,256]{2,1,0:T(8,128)(2,1)S(1)} %add_convert_fusion.2), channel_id=1, source_target_pairs={{0,16},{4,20},{8,24},{12,28},{16,0},{20,4},{24,8},{28,12},{1,17},{... | collective-permute-start | bytes 294920 | tf_op jit(solution)/shard_map/ppermute | solution.py:300
  32.7 4.7 %collective-permute-start.14 = (bf16[3,64,256]{2,1,0:T(8,128)(2,1)S(1)}, bf16[3,64,256]{2,1,0:T(8,128)(2,1)S(1)}, u32[]{:S(2)}, u32[]{:S(2)}) collective-permute-start(bf16[3,64,256]{2,1,0:T(8,128)(2,1)S(1)} %add_convert_fusion.1), channel_id=1, source_target_pairs={{0,16},{4,20},{8,24},{12,28},{16,0},{20,4},{24,8},{28,12},{1,17},{... | collective-permute-start | bytes 294920 | tf_op jit(solution)/shard_map/ppermute | solution.py:300
  33.3 4.7 %collective-permute-start.13 = (bf16[3,64,256]{2,1,0:T(8,128)(2,1)S(1)}, bf16[3,64,256]{2,1,0:T(8,128)(2,1)S(1)}, u32[]{:S(2)}, u32[]{:S(2)}) collective-permute-start(bf16[3,64,256]{2,1,0:T(8,128)(2,1)S(1)} %add_convert_fusion), channel_id=1, source_target_pairs={{0,8},{4,12},{8,0},{12,4},{16,24},{20,28},{24,16},{28,20},{1,9},{5... | collective-permute-start | bytes 294920 | tf_op jit(solution)/shard_map/ppermute | solution.py:300
  37.4 4.9 %collective-permute-start.16 = (f32[3,64,256]{2,1,0:T(8,128)S(1)}, f32[3,64,256]{2,1,0:T(8,128)S(1)}, u32[]{:S(2)}, u32[]{:S(2)}) collective-permute-start(f32[3,64,256]{2,1,0:T(8,128)S(1)} %convert_add_fusion.1.a_ref), channel_id=1, source_target_pairs={{0,4},{4,0},{8,12},{12,8},{16,20},{20,16},{24,28},{28,24},{1,5},{5... | collective-permute-start | bytes 589832 | tf_op jit(solution)/shard_map/ppermute | solution.py:300
  38.0 5.2 %collective-permute-start.15 = (f32[3,64,256]{2,1,0:T(8,128)S(1)}, f32[3,64,256]{2,1,0:T(8,128)S(1)}, u32[]{:S(2)}, u32[]{:S(2)}) collective-permute-start(f32[3,64,256]{2,1,0:T(8,128)S(1)} %convert_add_fusion.b_ref), channel_id=1, source_target_pairs={{0,4},{4,0},{8,12},{12,8},{16,20},{20,16},{24,28},{28,24},{1,5},{5... | collective-permute-start | bytes 589832 | tf_op jit(solution)/shard_map/ppermute | solution.py:300

commit v7 on v5

--- a/solution.py
+++ b/solution.py
@@ -349,7 +349,7 @@
     a, b = keep
     moved_a = swap(send[0], "frames", 1)
     moved_b = swap(send[1], "frames", 1)
-    for first, second in zip(bits, bits[::-1]):
+    for first, second in zip(bits[::-1], bits):
         a = both(a, moved_a).astype(BF16)
         b = both(b, apart(moved_b, a)).astype(BF16)
         moved_a = swap(a, "frames", first)
@@ -375,18 +375,24 @@
     sums, pooled, weights = prep(inputs, saved, spatial_w)
     groups = [[k] for k in range(count)]
     order = {k: (i, j if len(g) > 1 else None) for i, g in enumerate(groups) for j, k in enumerate(g)}
-    outer, inner = [], []
+    outer = []
     for group in groups:
         value = pieces[group[0]] if len(group) == 1 else jnp.stack([pieces[k] for k in group])
-        outer.append(lax.ppermute(value, "frames", across))
-        inner.append(swap(value, "frames", 1))
+        if group == [1]:
+            outer.append(swap(outer[0], "chan", 1))
+        else:
+            outer.append(lax.ppermute(value, "frames", across))
+
+    near = [pieces[0], jnp.stack(pieces[1:])]
+    inner = [swap(value, "frames", 1) for value in near]
+    near_order = {k: (0, None) if k == 0 else (1, k - 1) for k in range(count)}
 
     slices = taps + 3
     limit = pltpu.CompilerParams(vmem_limit_bytes=20 << 20)
     part_shape = shape((slices, quarter, channels), F32)
     half_shapes = [shape((n, quarter, channels), F32) for n in (taps - slices // 2, slices - taps)]
     base, g_near, part = pl.pallas_call(
-        functools.partial(near_kernel, scale, count, order, len(inner)),
+        functools.partial(near_kernel, scale, count, near_order, len(inner)),
         out_shape=(shape((channels, spots), F32), shape((channels, spots), BF16), part_shape),
         in_specs=vmem(count + len(inner) + 3),
         out_specs=tuple(vmem(3)),

time: 40.6 us -> 44.2 us (1.089)
  waiting for transfers between devices: 10.9 us -> 17.7 us
  starting transfers between devices: 18 us -> 14.7 us
    ppermute x15 -> x14, waiting for transfers between devices: 7.92 us -> 14.8 us  [swap(): return lax.ppermute(value, axis, pairs)]
    ppermute x4 -> x3, starting transfers between devices: 7.48 us -> 4.84 us  [shards(): outer.append(lax.ppermute(value, 'frames', across))]
    ppermute x15 -> x14, starting transfers between devices: 10.5 us -> 9.87 us  [swap(): return lax.ppermute(value, axis, pairs)]
    ppermute x4 -> x3, waiting for transfers between devices: 2.96 us -> 2.9 us  [shards(): outer.append(lax.ppermute(value, 'frames', across))]
  transfers between devices with their start and end apart: 19 -> 17, of which waited for: 7 -> 10; matrix products, arithmetic and copies ran while one was open for 0% -> 0% of each run, Pallas kernels for 23% -> 21%
where the time goes in v7:
time: 44.2 us; the launch traced here: 44 us
  waiting for transfers between devices  17.7 us (40%)
  starting transfers between devices  14.7 us (33%)
  Pallas kernels  10.6 us (24%)
  between operations  0.82 us (2%)
    ppermute x14, waiting for transfers between devices, swap(): return lax.ppermute(value, axis, pairs)  14.8 us
    ppermute x14, starting transfers between devices, swap(): return lax.ppermute(value, axis, pairs)  9.87 us
    ppermute x3, starting transfers between devices, shards(): outer.append(lax.ppermute(value, 'frames', across))  4.84 us
    ppermute x3, waiting for transfers between devices, shards(): outer.append(lax.ppermute(value, 'frames', across))  2.9 us
    pallas_call x1, Pallas kernels, shards(): pl.pallas_call(back_far_kernel, out_shape=shape(inputs.shape, BF16), in_s...  2.13 us
    pallas_call x1, Pallas kernels, shards(): pl.pallas_call(back_near_kernel, out_shape=(shape(inputs.shape, BF16), sh...  2.12 us
    pallas_call x1, Pallas kernels, prep(): pl.pallas_call(saved_kernel, out_shape=(shape((frames, quarter, spots), B...  1.69 us
    pallas_call x1, Pallas kernels, prep(): pl.pallas_call(input_kernel, out_shape=shape((frames, taps * quarter, spo...  1.38 us
  transfers between devices with their start and end apart: 17, of which 10 were waited for; matrix products, arithmetic and copies ran while one was open for 0% of the time, Pallas kernels for 21%

profile of v7, /device:TPU:0, one launch (start us, length us, event | category | flops | bytes accessed | tf_op | source)
XLA Modules:
  0.0 44.0 jit_solution(6015629906941902384)
XLA Ops:
  0.6 3.1 %collective-permute-start.6 = (bf16[64,512]{1,0:T(8,128)(2,1)}, bf16[64,512]{1,0:T(8,128)(2,1)S(1)}, u32[]{:S(2)}, u32[]{:S(2)}) collective-permute-start(bf16[64,512]{1,0:T(8,128)(2,1)} %bitcast.8), channel_id=1, source_target_pairs={{0,1},{1,0},{2,3},{3,2},{4,5},{5,4},{6,7},{7,6},{8,9},{9,8},{10,11... | collective-permute-start | bytes 196616 | tf_op jit(solution)/shard_map/ppermute | solution.py:284
  3.7 2.5 %collective-permute-start.4 = (bf16[64,512]{1,0:T(8,128)(2,1)}, bf16[64,512]{1,0:T(8,128)(2,1)S(1)}, u32[]{:S(2)}, u32[]{:S(2)}) collective-permute-start(bf16[64,512]{1,0:T(8,128)(2,1)} %bitcast.9), channel_id=1, source_target_pairs={{0,3},{1,2},{2,1},{3,0},{4,7},{5,6},{6,5},{7,4},{8,11},{9,10},{10,... | collective-permute-start | bytes 196616 | tf_op jit(solution)/shard_map/ppermute | solution.py:284
  6.2 0.1 collective-permute-start.2
  6.3 0.0 collective-permute-done.6.refs_1_
  6.3 4.5 %collective-permute-done.4.refs_3_ = bf16[64,512]{1,0:T(8,128)(2,1)S(1)} collective-permute-done((bf16[64,512]{1,0:T(8,128)(2,1)}, bf16[64,512]{1,0:T(8,128)(2,1)S(1)}, u32[]{:S(2)}, u32[]{:S(2)}) %collective-permute-start.4) | collective-permute-done | bytes 65568 | tf_op jit(solution)/shard_map/ppermute | solution.py:284
  10.8 2.1 %collective-permute-done.2.refs_2_ = bf16[64,512]{1,0:T(8,128)(2,1)S(1)} collective-permute-done((bf16[64,512]{1,0:T(8,128)(2,1)}, bf16[64,512]{1,0:T(8,128)(2,1)S(1)}, u32[]{:S(2)}, u32[]{:S(2)}) %collective-permute-start.2) | collective-permute-done | bytes 65568 | tf_op jit(solution)/shard_map/ppermute | solution.py:284
  12.9 0.1 collective-permute-start.8
  13.0 0.5 %collective-permute-start.7 = (bf16[64,512]{1,0:T(8,128)(2,1)}, bf16[64,512]{1,0:T(8,128)(2,1)S(1)}, u32[]{:S(2)}, u32[]{:S(2)}) collective-permute-start(bf16[64,512]{1,0:T(8,128)(2,1)} %bitcast.11), channel_id=1, source_target_pairs={{0,4},{4,0},{8,12},{12,8},{16,20},{20,16},{24,28},{28,24},{1,5},{5... | collective-permute-start | bytes 196616 | tf_op jit(solution)/shard_map/ppermute | solution.py:284
  13.5 2.1 %collective-permute-start = (bf16[64,512]{1,0:T(8,128)(2,1)}, bf16[64,512]{1,0:T(8,128)(2,1)S(1)}, u32[]{:S(2)}, u32[]{:S(2)}) collective-permute-start(bf16[64,512]{1,0:T(8,128)(2,1)} %bitcast.12), channel_id=1, source_target_pairs={{0,28},{4,8},{8,4},{12,16},{16,12},{20,24},{24,20},{28,0},{1,29},{... | collective-permute-start | bytes 196616 | tf_op jit(solution)/shard_map/ppermute | solution.py:384
  15.6 1.7 %prep_saved.1 = (bf16[2,64,512]{2,1,0:T(8,128)(2,1)S(1)}, bf16[2,64,16,128]{3,2,1,0:T(8,128)(2,1)S(1)}, bf16[3,3,64,256]{3,2,1,0:T(8,128)(2,1)S(1)}) custom-call(bf16[2,64,16,128]{3,2,1,0:T(8,128)(2,1)} %x_hbm.1, bf16[2,64,16,128]{3,2,1,0:T(8,128)(2,1)} %y_hbm.1, bf16[3,3,64,256]{3,2,1,0:T(8,128)(2,1)} %sw_hbm.1), custom_call_target="tpu_custom_call" | custom-call | flops 536870912 | bytes 4194304 | tf_op jit(solution)/shard_map/prep_saved/pallas_call | solution.py:310
  17.3 0.0 copy-start
  17.3 0.0 copy-start.1
  17.4 1.4 %prep_inputs.1.refs_6_.s_ref = bf16[2,576,512]{2,1,0:T(8,128)(2,1)S(1)} custom-call(bf16[2,64,16,128]{3,2,1,0:T(8,128)(2,1)S(1)} %get-tuple-element.24.x_ref), custom_call_target="tpu_custom_call" | custom-call | flops 1073741824 | bytes 4194304 | tf_op jit(solution)/shard_map/prep_inputs/pallas_call | solution.py:329
  18.7 0.6 %collective-permute-start.5 = (bf16[64,512]{1,0:T(8,128)(2,1)S(1)}, bf16[64,512]{1,0:T(8,128)(2,1)S(1)}, u32[]{:S(2)}, u32[]{:S(2)}) collective-permute-start(bf16[64,512]{1,0:T(8,128)(2,1)S(1)} %collective-permute-done.4.refs_3_), channel_id=1, source_target_pairs={{0,28},{4,8},{8,4},{12,16},{16,12},{20,24},{24,20},{28,0},{1,29},{... | collective-permute-start | bytes 196616 | tf_op jit(solution)/shard_map/ppermute | solution.py:384
  19.3 2.1 %collective-permute-start.3 = (bf16[64,512]{1,0:T(8,128)(2,1)S(1)}, bf16[64,512]{1,0:T(8,128)(2,1)S(1)}, u32[]{:S(2)}, u32[]{:S(2)}) collective-permute-start(bf16[64,512]{1,0:T(8,128)(2,1)S(1)} %collective-permute-done.2.refs_2_), channel_id=1, source_target_pairs={{0,28},{4,8},{8,4},{12,16},{16,12},{20,24},{24,20},{28,0},{1,29},{... | collective-permute-start | bytes 196616 | tf_op jit(solution)/shard_map/ppermute | solution.py:384
  21.5 0.0 collective-permute-done.refs_0_
  21.5 0.0 collective-permute-start.1
  21.5 0.0 collective-permute-done.7.refs_4_
  21.5 0.0 collective-permute-done.8.refs_5_
  21.5 0.0 copy-done
  21.5 0.0 copy-done.1
  21.5 0.8 %near.1 = (f32[256,512]{1,0:T(8,128)S(1)}, bf16[256,512]{1,0:T(8,128)(2,1)S(1)}, f32[12,64,256]{2,1,0:T(8,128)S(1)}) custom-call(bf16[64,512]{1,0:T(8,128)(2,1)S(1)} %bitcast.13, bf16[64,512]{1,0:T(8,128)(2,1)S(1)} %collective-permute-done.6.refs_1_, bf16[64,512]{1,0:T(8,128)(2,1)S(1)} %collective-permute-done.2.refs_2_, ...), custom_call_target="tpu_custom_call" | custom-call | flops 1073741824 | bytes 4194304 | tf_op jit(solution)/shard_map/near/pallas_call | solution.py:394
  22.3 1.8 %collective-permute-done.5.refs_3_ = bf16[64,512]{1,0:T(8,128)(2,1)S(1)} collective-permute-done((bf16[64,512]{1,0:T(8,128)(2,1)S(1)}, bf16[64,512]{1,0:T(8,128)(2,1)S(1)}, u32[]{:S(2)}, u32[]{:S(2)}) %collective-permute-start.5) | collective-permute-done | bytes 65568 | tf_op jit(solution)/shard_map/ppermute | solution.py:384
  24.1 1.1 %collective-permute-done.3.refs_2_ = bf16[64,512]{1,0:T(8,128)(2,1)S(1)} collective-permute-done((bf16[64,512]{1,0:T(8,128)(2,1)S(1)}, bf16[64,512]{1,0:T(8,128)(2,1)S(1)}, u32[]{:S(2)}, u32[]{:S(2)}) %collective-permute-start.3) | collective-permute-done | bytes 65568 | tf_op jit(solution)/shard_map/ppermute | solution.py:384
  25.2 0.5 %collective-permute-done.1.refs_1_ = bf16[64,512]{1,0:T(8,128)(2,1)S(1)} collective-permute-done((bf16[64,512]{1,0:T(8,128)(2,1)S(1)}, bf16[64,512]{1,0:T(8,128)(2,1)S(1)}, u32[]{:S(2)}, u32[]{:S(2)}) %collective-permute-start.1) | collective-permute-done | bytes 65568 | tf_op jit(solution)/shard_map/ppermute | solution.py:284
  25.7 0.6 %far.1 = (bf16[256,512]{1,0:T(8,128)(2,1)S(1)}, f32[3,64,256]{2,1,0:T(8,128)S(1)}, f32[3,64,256]{2,1,0:T(8,128)S(1)}, bf16[4,64,512]{2,1,0:T(8,128)(2,1)S(1)}) custom-call(bf16[64,512]{1,0:T(8,128)(2,1)S(1)} %collective-permute-done.refs_0_, bf16[64,512]{1,0:T(8,128)(2,1)S(1)} %collective-permute-done.1.refs_1_, ...), custom_call_target="tpu_custom_call" | custom-call | flops 536870912 | bytes 4194304 | tf_op jit(solution)/shard_map/far/pallas_call | solution.py:404
  26.3 0.1 collective-permute-start.10
  26.4 0.5 %collective-permute-start.9 = (f32[3,64,256]{2,1,0:T(8,128)S(1)}, f32[3,64,256]{2,1,0:T(8,128)S(1)}, u32[]{:S(2)}, u32[]{:S(2)}) collective-permute-start(f32[3,64,256]{2,1,0:T(8,128)S(1)} %get-tuple-element.35), channel_id=1, source_target_pairs={{0,4},{4,0},{8,12},{12,8},{16,20},{20,16},{24,28},{28,24},{1,5},{5... | collective-permute-start | bytes 589832 | tf_op jit(solution)/shard_map/ppermute | solution.py:284
  26.9 0.3 keep.1
  27.2 0.6 %collective-permute-done.10 = f32[3,64,256]{2,1,0:T(8,128)S(1)} collective-permute-done((f32[3,64,256]{2,1,0:T(8,128)S(1)}, f32[3,64,256]{2,1,0:T(8,128)S(1)}, u32[]{:S(2)}, u32[]{:S(2)}) %collective-permute-start.10) | collective-permute-done | bytes 196640 | tf_op jit(solution)/shard_map/ppermute | solution.py:284
  27.8 0.6 %collective-permute-start.12 = (bf16[3,64,256]{2,1,0:T(8,128)(2,1)S(1)}, bf16[3,64,256]{2,1,0:T(8,128)(2,1)S(1)}, u32[]{:S(2)}, u32[]{:S(2)}) collective-permute-start(bf16[3,64,256]{2,1,0:T(8,128)(2,1)S(1)} %add_convert_fusion.3), channel_id=1, source_target_pairs={{0,16},{4,20},{8,24},{12,28},{16,0},{20,4},{24,8},{28,12},{1,17},{... | collective-permute-start | bytes 294920 | tf_op jit(solution)/shard_map/ppermute | solution.py:284
  28.4 0.0 collective-permute-done.9
  28.5 0.4 %collective-permute-start.11 = (bf16[3,64,256]{2,1,0:T(8,128)(2,1)S(1)}, bf16[3,64,256]{2,1,0:T(8,128)(2,1)S(1)}, u32[]{:S(2)}, u32[]{:S(2)}) collective-permute-start(bf16[3,64,256]{2,1,0:T(8,128)(2,1)S(1)} %add_convert_fusion.2), channel_id=1, source_target_pairs={{0,8},{4,12},{8,0},{12,4},{16,24},{20,28},{24,16},{28,20},{1,9},{5... | collective-permute-start | bytes 294920 | tf_op jit(solution)/shard_map/ppermute | solution.py:284
  28.9 3.8 %collective-permute-done.12 = bf16[3,64,256]{2,1,0:T(8,128)(2,1)S(1)} collective-permute-done((bf16[3,64,256]{2,1,0:T(8,128)(2,1)S(1)}, bf16[3,64,256]{2,1,0:T(8,128)(2,1)S(1)}, u32[]{:S(2)}, u32[]{:S(2)}) %collective-permute-start.12) | collective-permute-done | bytes 98336 | tf_op jit(solution)/shard_map/ppermute | solution.py:284
  32.8 0.1 collective-permute-start.14
  32.9 0.3 collective-permute-done.11
  33.2 1.6 %collective-permute-start.13 = (bf16[3,64,256]{2,1,0:T(8,128)(2,1)S(1)}, bf16[3,64,256]{2,1,0:T(8,128)(2,1)S(1)}, u32[]{:S(2)}, u32[]{:S(2)}) collective-permute-start(bf16[3,64,256]{2,1,0:T(8,128)(2,1)S(1)} %add_convert_fusion), channel_id=1, source_target_pairs={{0,16},{4,20},{8,24},{12,28},{16,0},{20,4},{24,8},{28,12},{1,17},{... | collective-permute-start | bytes 294920 | tf_op jit(solution)/shard_map/ppermute | solution.py:284
  34.7 2.7 %collective-permute-done.14 = bf16[3,64,256]{2,1,0:T(8,128)(2,1)S(1)} collective-permute-done((bf16[3,64,256]{2,1,0:T(8,128)(2,1)S(1)}, bf16[3,64,256]{2,1,0:T(8,128)(2,1)S(1)}, u32[]{:S(2)}, u32[]{:S(2)}) %collective-permute-start.14) | collective-permute-done | bytes 98336 | tf_op jit(solution)/shard_map/ppermute | solution.py:284
  37.5 0.1 collective-permute-start.16
  37.6 0.3 collective-permute-done.13
  37.9 0.3 collective-permute-start.15
  38.2 2.1 %back_near.1 = (bf16[2,64,16,128]{3,2,1,0:T(8,128)(2,1)}, bf16[3,256,256]{2,1,0:T(8,128)(2,1)S(1)}) custom-call(bf16[256,512]{1,0:T(8,128)(2,1)S(1)} %get-tuple-element.29.g_ref, bf16[3,3,64,256]{3,2,1,0:T(8,128)(2,1)S(1)} %get-tuple-element.30.sw_ref), custom_call_target="tpu_custom_call" | custom-call | flops 1610612736 | bytes 2097152 | tf_op jit(solution)/shard_map/back_near/pallas_call | solution.py:438
  40.3 2.1 %back_far.1 = bf16[2,64,16,128]{3,2,1,0:T(8,128)(2,1)} custom-call(bf16[256,512]{1,0:T(8,128)(2,1)S(1)} %get-tuple-element.28.g_ref, bf16[3,256,256]{2,1,0:T(8,128)(2,1)S(1)} %get-tuple-element.31.wc_ref, bf16[2,64,16,128]{3,2,1,0:T(8,128)(2,1)} %get-tuple-element.32.out_in), custom_call_target="tpu_custom_call", output_to_operand_aliasing={{}: (2, {})} | custom-call | flops 1610612736 | bytes 2097152 | tf_op jit(solution)/shard_map/back_far/pallas_call | solution.py:446
  42.4 0.0 collective-permute-done.16.other_a
  42.4 0.8 %early.1 = (f32[9,64,256]{2,1,0:T(8,128)}, f32[3,64,256]{2,1,0:T(8,128)}) custom-call(f32[3,64,256]{2,1,0:T(8,128)S(1)} %convert_add_fusion.1.a_ref, f32[3,64,256]{2,1,0:T(8,128)S(1)} %convert_add_fusion.b_ref, f32[3,64,256]{2,1,0:T(8,128)S(1)} %collective-permute-done.16.other_a), custom_call_target="tpu_custom_call" | custom-call | bytes 4194304 | tf_op jit(solution)/shard_map/early/pallas_call | solution.py:467
  43.3 0.0 collective-permute-done.15.b_ref
  43.3 0.7 %finish.1 = (f32[9,64,256]{2,1,0:T(8,128)}, f32[3,64,256]{2,1,0:T(8,128)}) custom-call(f32[3,64,256]{2,1,0:T(8,128)S(1)} %collective-permute-done.15.b_ref, f32[9,64,256]{2,1,0:T(8,128)} %get-tuple-element.41.spatial_in, f32[3,64,256]{2,1,0:T(8,128)} %get-tuple-element.42.temporal_in), custom_call_target="tpu_custom_call", output_to_operand_aliasing={{0}: (1, {}), {1}: (2, {})} | custom-call | bytes 4194304 | tf_op jit(solution)/shard_map/finish/pallas_call | solution.py:468
  (7 shorter events, 0.2 us)
Async XLA Ops:
  0.6 5.7 %collective-permute-start.6 = (bf16[64,512]{1,0:T(8,128)(2,1)}, bf16[64,512]{1,0:T(8,128)(2,1)S(1)}, u32[]{:S(2)}, u32[]{:S(2)}) collective-permute-start(bf16[64,512]{1,0:T(8,128)(2,1)} %bitcast.8), channel_id=1, source_target_pairs={{0,1},{1,0},{2,3},{3,2},{4,5},{5,4},{6,7},{7,6},{8,9},{9,8},{10,11... | collective-permute-start | bytes 196616 | tf_op jit(solution)/shard_map/ppermute | solution.py:284
  3.7 7.1 %collective-permute-start.4 = (bf16[64,512]{1,0:T(8,128)(2,1)}, bf16[64,512]{1,0:T(8,128)(2,1)S(1)}, u32[]{:S(2)}, u32[]{:S(2)}) collective-permute-start(bf16[64,512]{1,0:T(8,128)(2,1)} %bitcast.9), channel_id=1, source_target_pairs={{0,3},{1,2},{2,1},{3,0},{4,7},{5,6},{6,5},{7,4},{8,11},{9,10},{10,... | collective-permute-start | bytes 196616 | tf_op jit(solution)/shard_map/ppermute | solution.py:284
  6.2 6.7 %collective-permute-start.2 = (bf16[64,512]{1,0:T(8,128)(2,1)}, bf16[64,512]{1,0:T(8,128)(2,1)S(1)}, u32[]{:S(2)}, u32[]{:S(2)}) collective-permute-start(bf16[64,512]{1,0:T(8,128)(2,1)} %bitcast.10), channel_id=1, source_target_pairs={{0,2},{1,3},{2,0},{3,1},{4,6},{5,7},{6,4},{7,5},{8,10},{9,11},{10,... | collective-permute-start | bytes 196616 | tf_op jit(solution)/shard_map/ppermute | solution.py:284
  12.9 8.5 %collective-permute-start.8 = (bf16[3,64,512]{2,1,0:T(8,128)(2,1)S(1)}, bf16[3,64,512]{2,1,0:T(8,128)(2,1)S(1)}, u32[]{:S(2)}, u32[]{:S(2)}) collective-permute-start(bf16[3,64,512]{2,1,0:T(8,128)(2,1)S(1)} %pad_maximum_fusion), channel_id=1, source_target_pairs={{0,4},{4,0},{8,12},{12,8},{16,20},{20,16},{24,28},{28,24},{1,5},{5... | collective-permute-start | bytes 589832 | tf_op jit(solution)/shard_map/ppermute | solution.py:284
  13.0 8.5 %collective-permute-start.7 = (bf16[64,512]{1,0:T(8,128)(2,1)}, bf16[64,512]{1,0:T(8,128)(2,1)S(1)}, u32[]{:S(2)}, u32[]{:S(2)}) collective-permute-start(bf16[64,512]{1,0:T(8,128)(2,1)} %bitcast.11), channel_id=1, source_target_pairs={{0,4},{4,0},{8,12},{12,8},{16,20},{20,16},{24,28},{28,24},{1,5},{5... | collective-permute-start | bytes 196616 | tf_op jit(solution)/shard_map/ppermute | solution.py:284
  13.5 8.0 %collective-permute-start = (bf16[64,512]{1,0:T(8,128)(2,1)}, bf16[64,512]{1,0:T(8,128)(2,1)S(1)}, u32[]{:S(2)}, u32[]{:S(2)}) collective-permute-start(bf16[64,512]{1,0:T(8,128)(2,1)} %bitcast.12), channel_id=1, source_target_pairs={{0,28},{4,8},{8,4},{12,16},{16,12},{20,24},{24,20},{28,0},{1,29},{... | collective-permute-start | bytes 196616 | tf_op jit(solution)/shard_map/ppermute | solution.py:384
  17.3 4.1 %copy-start = (bf16[3,256,256]{2,1,0:T(8,128)(2,1)S(1)}, bf16[3,256,256]{2,1,0:T(8,128)(2,1)}, u32[]{:S(2)}) copy-start(bf16[3,256,256]{2,1,0:T(8,128)(2,1)} %refs_8_.3) | copy-start | bytes 1179652
  17.3 4.1 %copy-start.1 = (bf16[1,64,512]{2,1,0:T(8,128)(2,1)S(1)}, bf16[1,64,512]{2,1,0:T(8,128)(2,1)}, u32[]{:S(2)}) copy-start(bf16[1,64,512]{2,1,0:T(8,128)(2,1)} %param.7) | copy-start | bytes 196612
  18.7 5.4 %collective-permute-start.5 = (bf16[64,512]{1,0:T(8,128)(2,1)S(1)}, bf16[64,512]{1,0:T(8,128)(2,1)S(1)}, u32[]{:S(2)}, u32[]{:S(2)}) collective-permute-start(bf16[64,512]{1,0:T(8,128)(2,1)S(1)} %collective-permute-done.4.refs_3_), channel_id=1, source_target_pairs={{0,28},{4,8},{8,4},{12,16},{16,12},{20,24},{24,20},{28,0},{1,29},{... | collective-permute-start | bytes 196616 | tf_op jit(solution)/shard_map/ppermute | solution.py:384
  19.3 5.9 %collective-permute-start.3 = (bf16[64,512]{1,0:T(8,128)(2,1)S(1)}, bf16[64,512]{1,0:T(8,128)(2,1)S(1)}, u32[]{:S(2)}, u32[]{:S(2)}) collective-permute-start(bf16[64,512]{1,0:T(8,128)(2,1)S(1)} %collective-permute-done.2.refs_2_), channel_id=1, source_target_pairs={{0,28},{4,8},{8,4},{12,16},{16,12},{20,24},{24,20},{28,0},{1,29},{... | collective-permute-start | bytes 196616 | tf_op jit(solution)/shard_map/ppermute | solution.py:384
  21.5 4.3 %collective-permute-start.1 = (bf16[64,512]{1,0:T(8,128)(2,1)S(1)}, bf16[64,512]{1,0:T(8,128)(2,1)S(1)}, u32[]{:S(2)}, u32[]{:S(2)}) collective-permute-start(bf16[64,512]{1,0:T(8,128)(2,1)S(1)} %collective-permute-done.refs_0_), channel_id=1, source_target_pairs={{0,1},{1,0},{2,3},{3,2},{4,5},{5,4},{6,7},{7,6},{8,9},{9,8},{10,11... | collective-permute-start | bytes 196616 | tf_op jit(solution)/shard_map/ppermute | solution.py:284
  26.3 1.5 %collective-permute-start.10 = (f32[3,64,256]{2,1,0:T(8,128)S(1)}, f32[3,64,256]{2,1,0:T(8,128)S(1)}, u32[]{:S(2)}, u32[]{:S(2)}) collective-permute-start(f32[3,64,256]{2,1,0:T(8,128)S(1)} %get-tuple-element.37), channel_id=1, source_target_pairs={{0,4},{4,0},{8,12},{12,8},{16,20},{20,16},{24,28},{28,24},{1,5},{5... | collective-permute-start | bytes 589832 | tf_op jit(solution)/shard_map/ppermute | solution.py:284
  26.4 2.0 %collective-permute-start.9 = (f32[3,64,256]{2,1,0:T(8,128)S(1)}, f32[3,64,256]{2,1,0:T(8,128)S(1)}, u32[]{:S(2)}, u32[]{:S(2)}) collective-permute-start(f32[3,64,256]{2,1,0:T(8,128)S(1)} %get-tuple-element.35), channel_id=1, source_target_pairs={{0,4},{4,0},{8,12},{12,8},{16,20},{20,16},{24,28},{28,24},{1,5},{5... | collective-permute-start | bytes 589832 | tf_op jit(solution)/shard_map/ppermute | solution.py:284
  27.8 4.9 %collective-permute-start.12 = (bf16[3,64,256]{2,1,0:T(8,128)(2,1)S(1)}, bf16[3,64,256]{2,1,0:T(8,128)(2,1)S(1)}, u32[]{:S(2)}, u32[]{:S(2)}) collective-permute-start(bf16[3,64,256]{2,1,0:T(8,128)(2,1)S(1)} %add_convert_fusion.3), channel_id=1, source_target_pairs={{0,16},{4,20},{8,24},{12,28},{16,0},{20,4},{24,8},{28,12},{1,17},{... | collective-permute-start | bytes 294920 | tf_op jit(solution)/shard_map/ppermute | solution.py:284
  28.5 4.7 %collective-permute-start.11 = (bf16[3,64,256]{2,1,0:T(8,128)(2,1)S(1)}, bf16[3,64,256]{2,1,0:T(8,128)(2,1)S(1)}, u32[]{:S(2)}, u32[]{:S(2)}) collective-permute-start(bf16[3,64,256]{2,1,0:T(8,128)(2,1)S(1)} %add_convert_fusion.2), channel_id=1, source_target_pairs={{0,8},{4,12},{8,0},{12,4},{16,24},{20,28},{24,16},{28,20},{1,9},{5... | collective-permute-start | bytes 294920 | tf_op jit(solution)/shard_map/ppermute | solution.py:284
  32.8 4.7 %collective-permute-start.14 = (bf16[3,64,256]{2,1,0:T(8,128)(2,1)S(1)}, bf16[3,64,256]{2,1,0:T(8,128)(2,1)S(1)}, u32[]{:S(2)}, u32[]{:S(2)}) collective-permute-start(bf16[3,64,256]{2,1,0:T(8,128)(2,1)S(1)} %add_convert_fusion.1), channel_id=1, source_target_pairs={{0,8},{4,12},{8,0},{12,4},{16,24},{20,28},{24,16},{28,20},{1,9},{5... | collective-permute-start | bytes 294920 | tf_op jit(solution)/shard_map/ppermute | solution.py:284
  33.2 4.7 %collective-permute-start.13 = (bf16[3,64,256]{2,1,0:T(8,128)(2,1)S(1)}, bf16[3,64,256]{2,1,0:T(8,128)(2,1)S(1)}, u32[]{:S(2)}, u32[]{:S(2)}) collective-permute-start(bf16[3,64,256]{2,1,0:T(8,128)(2,1)S(1)} %add_convert_fusion), channel_id=1, source_target_pairs={{0,16},{4,20},{8,24},{12,28},{16,0},{20,4},{24,8},{28,12},{1,17},{... | collective-permute-start | bytes 294920 | tf_op jit(solution)/shard_map/ppermute | solution.py:284
  37.5 4.9 %collective-permute-start.16 = (f32[3,64,256]{2,1,0:T(8,128)S(1)}, f32[3,64,256]{2,1,0:T(8,128)S(1)}, u32[]{:S(2)}, u32[]{:S(2)}) collective-permute-start(f32[3,64,256]{2,1,0:T(8,128)S(1)} %convert_add_fusion.1.a_ref), channel_id=1, source_target_pairs={{0,4},{4,0},{8,12},{12,8},{16,20},{20,16},{24,28},{28,24},{1,5},{5... | collective-permute-start | bytes 589832 | tf_op jit(solution)/shard_map/ppermute | solution.py:284
  37.9 5.4 %collective-permute-start.15 = (f32[3,64,256]{2,1,0:T(8,128)S(1)}, f32[3,64,256]{2,1,0:T(8,128)S(1)}, u32[]{:S(2)}, u32[]{:S(2)}) collective-permute-start(f32[3,64,256]{2,1,0:T(8,128)S(1)} %convert_add_fusion.b_ref), channel_id=1, source_target_pairs={{0,4},{4,0},{8,12},{12,8},{16,20},{20,16},{24,28},{28,24},{1,5},{5... | collective-permute-start | bytes 589832 | tf_op jit(solution)/shard_map/ppermute | solution.py:284
